TPU v7x, 32 devices: a whole 2x2x4 slice. The times are simulated.
32 devices in a mesh: dp: 8 (over z, core), expert: 4 (over y, x).
Axes of the slice: x: 2, y: 2, z: 4, core: 2. Of those that a mesh axis runs over, the one named last changes fastest.
Arguments:
- embedded: bfloat16 [64, 197, 512], P(('dp', 'expert')), may hold values from -6 to 6
- cotangent: bfloat16 [64, 197, 512], P(('dp', 'expert')), may hold values from -6 to 6
- w_qkv: bfloat16 [2, 512, 1536], P(None, 'dp'), may hold values from -0.25 to 0.25
- w_proj: bfloat16 [2, 512, 512], P(None, 'dp'), may hold values from -2.5 to 2.5
- w_router: bfloat16 [2, 512, 8], P(None, 'dp'), may hold values from -0.1875 to 0.1875
- norm_gains: bfloat16 [2, 2, 512], P(None, None, 'dp'), may hold values from 0.25 to 1.75
- norm_shifts: bfloat16 [2, 2, 512], P(None, None, 'dp'), may hold values from -1 to 1
- w_first: bfloat16 [2, 8, 512, 2048], P(None, 'expert', None, 'dp'), may hold values from -0.25 to 0.25
- w_second: bfloat16 [2, 8, 2048, 512], P(None, 'expert', 'dp'), may hold values from -1 to 1
- routes: int32 [2, 64, 197, 2], P(None, ('dp', 'expert')), may hold values from 0 to 7, all different within a row; in each aligned block of 394 rows (0 to 393, 394 to 787, ..., all dimensions but the last counted through in order) at most 147 rows name the same one
Outputs:
- out_images: bfloat16 [64, 197, 512], P(('dp', 'expert'))
- grad_images: float32 [64, 197, 512], P(('dp', 'expert'))
- grad_qkv: float32 [2, 512, 1536], P(None, 'dp')
- grad_proj: float32 [2, 512, 512], P(None, 'dp')
- grad_router: float32 [2, 512, 8], P(None, 'dp')
- grad_gains: float32 [2, 2, 512], P(None, None, 'dp')
- grad_shifts: float32 [2, 2, 512], P(None, None, 'dp')
- grad_first: float32 [2, 8, 512, 2048], P(None, 'expert', None, 'dp')
- grad_second: float32 [2, 8, 2048, 512], P(None, 'expert', 'dp')
Inputs may be any that keep to these rules, and one draw needn't show every extreme that they name: `routes`: the two experts of a token differ. Among the 394 tokens of one device in one block, no expert is named by more than 147 tokens, a bound that some block reaches.
All inputs are finite; a program needn't handle non-finite values.
Results may differ from a plain program's by a relative error of at most 0.019.
Values may be sent and summed in bfloat16 or wider, within the bound.
No kernel may reach another device: no remote copies, remote signals or barrier semaphores. Data moves between devices by JAX's collectives and lax.ppermute only.
A program may use at most 192 MiB of HBM per device.

v0:
```python
import jax
import jax.numpy as jnp
from jax import lax
from jax.sharding import PartitionSpec as P

HEADS = 8
HEAD_DIM = 64
SEQ = 197
LAYERS = 2


EPSILON = 1e-06
ROOT_HALF = 0.7071067811865476
INV_ROOT_TAU = 0.3989422804014327


def layer_norm(values, scale_in, shift_in):
    center = values - jnp.mean(values, axis=-1, keepdims=True)
    variance = jnp.mean(center * center, axis=-1, keepdims=True)
    inverse = lax.rsqrt(variance + EPSILON)
    normed = center * inverse
    return (normed * scale_in + shift_in, normed, inverse)


def norm_back(grad_out, normed, inverse, scale_in):
    grad_normed = grad_out * scale_in
    first_mean = jnp.mean(grad_normed, axis=-1, keepdims=True)
    second_mean = jnp.mean(grad_normed * normed, axis=-1, keepdims=True)
    grad_in = inverse * (grad_normed - first_mean - normed * second_mean)
    return (grad_in, jnp.sum(grad_out * normed, axis=0), jnp.sum(grad_out, axis=0))


def softmax_rows(scores):
    highest = jnp.max(scores, axis=-1, keepdims=True)
    powers = jnp.exp(scores - highest)
    row_total = jnp.sum(powers, axis=-1, keepdims=True)
    return (powers / row_total, highest + jnp.log(row_total))


def gelu_value(preact):
    return 0.5 * preact * (1.0 + lax.erf(preact * ROOT_HALF))


def gelu_slope(preact):
    return (
        0.5 * (1.0 + lax.erf(preact * ROOT_HALF))
        + preact * jnp.exp(-0.5 * preact * preact) * INV_ROOT_TAU
    )


def layer_forward(
    resid, which, w_qkv, w_proj, w_router, norm_gains, norm_shifts, w_first, w_second, routes
):
    qkv_full, proj_full, router_full, gains_full, shifts_full = (
        lax.all_gather(w_qkv[which], "dp", axis=0, tiled=True),
        lax.all_gather(w_proj[which], "dp", axis=0, tiled=True),
        lax.all_gather(w_router[which], "dp", axis=0, tiled=True),
        lax.all_gather(norm_gains[which], "dp", axis=1, tiled=True),
        lax.all_gather(norm_shifts[which], "dp", axis=1, tiled=True),
    )
    first_full, second_full = (
        lax.all_gather(w_first[which], "dp", axis=2, tiled=True),
        lax.all_gather(w_second[which], "dp", axis=1, tiled=True),
    )
    tok_count, width = resid.shape
    images = tok_count // SEQ
    gains_wide = gains_full.astype(jnp.float32)
    shifts_wide = shifts_full.astype(jnp.float32)
    attn_norm, unit_a, inv_a = layer_norm(resid, gains_wide[0], shifts_wide[0])
    attn_in = attn_norm.astype(jnp.bfloat16)
    packed = jnp.dot(attn_in, qkv_full, preferred_element_type=jnp.float32)
    head_shape = (images, SEQ, HEADS, HEAD_DIM)
    query = (packed[:, :width] * HEAD_DIM ** (-0.5)).astype(jnp.bfloat16).reshape(head_shape)
    keyed = packed[:, width : 2 * width].astype(jnp.bfloat16).reshape(head_shape)
    valued = packed[:, 2 * width :].astype(jnp.bfloat16).reshape(head_shape)
    scores = jnp.einsum("iqhd,ikhd->ihqk", query, keyed, preferred_element_type=jnp.float32)
    probs, log_total = softmax_rows(scores)
    mixed = jnp.einsum(
        "ihqk,ikhd->iqhd", probs.astype(jnp.bfloat16), valued, preferred_element_type=jnp.float32
    )
    mixed = mixed.reshape(tok_count, width).astype(jnp.bfloat16)
    resid_mid = resid + jnp.dot(mixed, proj_full, preferred_element_type=jnp.float32)
    moe_norm, unit_b, inv_b = layer_norm(resid_mid, gains_wide[1], shifts_wide[1])
    moe_in = moe_norm.astype(jnp.bfloat16)
    logits = jnp.dot(moe_in, router_full, preferred_element_type=jnp.float32)
    router_probs, ignored_total = softmax_rows(logits)
    experts_total = router_full.shape[1]
    local_count = first_full.shape[0]
    peers = lax.axis_size("expert")
    capacity = max(2, 3 * tok_count // experts_total)
    route = routes[which].reshape(tok_count, 2)
    labels = jnp.arange(experts_total, dtype=jnp.int32)
    pick_first = (route[:, 0:1] == labels[None, :]).astype(jnp.int32)
    pick_second = (route[:, 1:2] == labels[None, :]).astype(jnp.int32)
    both_picks = pick_first + pick_second
    before = jnp.cumsum(both_picks, axis=0) - both_picks
    slot_first = route[:, 0] * capacity + jnp.sum(before * pick_first, axis=1)
    slot_second = route[:, 1] * capacity + jnp.sum(before * pick_second, axis=1)
    slot_ids = jnp.arange(experts_total * capacity, dtype=jnp.int32)
    place_first = (slot_ids[:, None] == slot_first[None, :]).astype(jnp.bfloat16)
    place_second = (slot_ids[:, None] == slot_second[None, :]).astype(jnp.bfloat16)
    outgoing = jnp.dot(place_first + place_second, moe_in, preferred_element_type=jnp.float32)
    outgoing = outgoing.astype(jnp.bfloat16).reshape(peers, local_count, capacity, width)
    incoming = lax.all_to_all(outgoing, "expert", split_axis=0, concat_axis=0, tiled=True)
    hidden_pre = jnp.einsum(
        "sjcd,jdf->sjcf", incoming, first_full, preferred_element_type=jnp.float32
    )
    hidden_act = gelu_value(hidden_pre).astype(jnp.bfloat16)
    result = jnp.einsum(
        "sjcf,jfd->sjcd", hidden_act, second_full, preferred_element_type=jnp.float32
    ).astype(jnp.bfloat16)
    returned = lax.all_to_all(result, "expert", split_axis=0, concat_axis=0, tiled=True).reshape(
        experts_total * capacity, width
    )
    pick_first_f = pick_first.astype(jnp.float32)
    pick_second_f = pick_second.astype(jnp.float32)
    gate_first = jnp.sum(router_probs * pick_first_f, axis=1)
    gate_second = jnp.sum(router_probs * pick_second_f, axis=1)
    back_first = jnp.take(returned, slot_first, axis=0).astype(jnp.float32)
    back_second = jnp.take(returned, slot_second, axis=0).astype(jnp.float32)
    resid_out = resid_mid + (gate_first[:, None] * back_first + gate_second[:, None] * back_second)
    saved = (
        qkv_full,
        proj_full,
        router_full,
        gains_wide,
        first_full,
        second_full,
        unit_a,
        inv_a,
        attn_in,
        query,
        keyed,
        valued,
        log_total,
        mixed,
        unit_b,
        inv_b,
        moe_in,
        router_probs,
        pick_first_f,
        pick_second_f,
        slot_first,
        slot_second,
        place_first,
        place_second,
        incoming,
        hidden_pre,
        hidden_act,
        returned,
        gate_first,
        gate_second,
    )
    return (resid_out, saved)


def layer_backward(grad_out, saved):
    (
        qkv_full,
        proj_full,
        router_full,
        gains_wide,
        first_full,
        second_full,
        unit_a,
        inv_a,
        attn_in,
        query,
        keyed,
        valued,
        log_total,
        mixed,
        unit_b,
        inv_b,
        moe_in,
        router_probs,
        pick_first_f,
        pick_second_f,
        slot_first,
        slot_second,
        place_first,
        place_second,
        incoming,
        hidden_pre,
        hidden_act,
        returned,
        gate_first,
        gate_second,
    ) = saved
    tok_count, width = grad_out.shape
    images = tok_count // SEQ
    back_first = jnp.take(returned, slot_first, axis=0).astype(jnp.float32)
    back_second = jnp.take(returned, slot_second, axis=0).astype(jnp.float32)
    grad_gate_first = jnp.sum(grad_out * back_first, axis=1)
    grad_gate_second = jnp.sum(grad_out * back_second, axis=1)
    send_first = (gate_first[:, None] * grad_out).astype(jnp.bfloat16)
    send_second = (gate_second[:, None] * grad_out).astype(jnp.bfloat16)
    slot_grads = jnp.dot(place_first, send_first, preferred_element_type=jnp.float32) + jnp.dot(
        place_second, send_second, preferred_element_type=jnp.float32
    )
    slot_grads = slot_grads.astype(jnp.bfloat16).reshape(incoming.shape)
    grad_result = lax.all_to_all(slot_grads, "expert", split_axis=0, concat_axis=0, tiled=True)
    grad_act = jnp.einsum(
        "sjcd,jfd->sjcf", grad_result, second_full, preferred_element_type=jnp.float32
    )
    grad_second = jnp.einsum(
        "sjcf,sjcd->jfd", hidden_act, grad_result, preferred_element_type=jnp.float32
    )
    grad_pre = (grad_act * gelu_slope(hidden_pre)).astype(jnp.bfloat16)
    grad_first = jnp.einsum(
        "sjcd,sjcf->jdf", incoming, grad_pre, preferred_element_type=jnp.float32
    )
    grad_rows = jnp.einsum(
        "sjcf,jdf->sjcd", grad_pre, first_full, preferred_element_type=jnp.float32
    ).astype(jnp.bfloat16)
    grad_back = lax.all_to_all(
        grad_rows, "expert", split_axis=0, concat_axis=0, tiled=True
    ).reshape(-1, width)
    grad_moe = jnp.einsum(
        "st,sd->td", place_first + place_second, grad_back, preferred_element_type=jnp.float32
    )
    grad_probs = pick_first_f * grad_gate_first[:, None] + pick_second_f * grad_gate_second[:, None]
    weighted = jnp.sum(router_probs * grad_probs, axis=1, keepdims=True)
    grad_logits = (router_probs * (grad_probs - weighted)).astype(jnp.bfloat16)
    grad_router = jnp.einsum("td,te->de", moe_in, grad_logits, preferred_element_type=jnp.float32)
    grad_moe = grad_moe + jnp.einsum(
        "te,de->td", grad_logits, router_full, preferred_element_type=jnp.float32
    )
    grad_norm_b, gain_b_grad, shift_b_grad = norm_back(grad_moe, unit_b, inv_b, gains_wide[1])
    grad_mid = grad_out + grad_norm_b
    grad_branch = grad_mid.astype(jnp.bfloat16)
    grad_proj = jnp.einsum("td,te->de", mixed, grad_branch, preferred_element_type=jnp.float32)
    grad_mixed = jnp.einsum("te,de->td", grad_branch, proj_full, preferred_element_type=jnp.float32)
    grad_mixed = grad_mixed.astype(jnp.bfloat16).reshape(images, SEQ, HEADS, HEAD_DIM)
    scores = jnp.einsum("iqhd,ikhd->ihqk", query, keyed, preferred_element_type=jnp.float32)
    probs = jnp.exp(scores - log_total)
    grad_weights = jnp.einsum(
        "iqhd,ikhd->ihqk", grad_mixed, valued, preferred_element_type=jnp.float32
    )
    grad_valued = jnp.einsum(
        "ihqk,iqhd->ikhd",
        probs.astype(jnp.bfloat16),
        grad_mixed,
        preferred_element_type=jnp.float32,
    ).astype(jnp.bfloat16)
    row_inner = jnp.sum(probs * grad_weights, axis=-1, keepdims=True)
    grad_scores = (probs * (grad_weights - row_inner)).astype(jnp.bfloat16)
    grad_query = jnp.einsum(
        "ihqk,ikhd->iqhd", grad_scores, keyed, preferred_element_type=jnp.float32
    ).astype(jnp.bfloat16)
    grad_query = grad_query * jnp.asarray(HEAD_DIM ** (-0.5), jnp.bfloat16)
    grad_keyed = jnp.einsum(
        "ihqk,iqhd->ikhd", grad_scores, query, preferred_element_type=jnp.float32
    ).astype(jnp.bfloat16)
    grad_packed = jnp.concatenate(
        [
            grad_query.reshape(tok_count, width),
            grad_keyed.reshape(tok_count, width),
            grad_valued.reshape(tok_count, width),
        ],
        axis=1,
    )
    grad_qkv = jnp.einsum("td,te->de", attn_in, grad_packed, preferred_element_type=jnp.float32)
    grad_attn = jnp.einsum("te,de->td", grad_packed, qkv_full, preferred_element_type=jnp.float32)
    grad_norm_a, gain_a_grad, shift_a_grad = norm_back(grad_attn, unit_a, inv_a, gains_wide[0])
    grad_in = grad_mid + grad_norm_a
    dense = (
        grad_qkv,
        grad_proj,
        grad_router,
        jnp.stack([gain_a_grad, gain_b_grad]),
        jnp.stack([shift_a_grad, shift_b_grad]),
    )
    return (grad_in, dense, (grad_first, grad_second))


def body(
    embedded, cotangent, w_qkv, w_proj, w_router, norm_gains, norm_shifts, w_first, w_second, routes
):
    images, length, width = embedded.shape
    tok_count = images * length
    resid = embedded.reshape(tok_count, width).astype(jnp.float32)
    layer_inputs = []
    for which in range(LAYERS):
        layer_inputs.append(resid)
        resid, saved = layer_forward(
            resid,
            which,
            w_qkv,
            w_proj,
            w_router,
            norm_gains,
            norm_shifts,
            w_first,
            w_second,
            routes,
        )
    out_images = resid.reshape(images, length, width).astype(jnp.bfloat16)
    grad = cotangent.reshape(tok_count, width).astype(jnp.float32)
    dense_layers = []
    expert_layers = []
    for which in reversed(range(LAYERS)):
        ignored, saved = layer_forward(
            layer_inputs[which],
            which,
            w_qkv,
            w_proj,
            w_router,
            norm_gains,
            norm_shifts,
            w_first,
            w_second,
            routes,
        )
        grad, dense, expert_part = layer_backward(grad, saved)
        totals = (
            lax.psum(dense[0].astype(jnp.bfloat16), "expert").astype(jnp.float32),
            lax.psum(dense[1].astype(jnp.bfloat16), "expert").astype(jnp.float32),
            lax.psum(dense[2].astype(jnp.bfloat16), "expert").astype(jnp.float32),
            lax.psum(dense[3].astype(jnp.bfloat16), "expert").astype(jnp.float32),
            lax.psum(dense[4].astype(jnp.bfloat16), "expert").astype(jnp.float32),
        )
        shares = (
            lax.psum_scatter(
                totals[0].astype(jnp.bfloat16), "dp", scatter_dimension=0, tiled=True
            ).astype(jnp.float32),
            lax.psum_scatter(
                totals[1].astype(jnp.bfloat16), "dp", scatter_dimension=0, tiled=True
            ).astype(jnp.float32),
            lax.psum_scatter(
                totals[2].astype(jnp.bfloat16), "dp", scatter_dimension=0, tiled=True
            ).astype(jnp.float32),
            lax.psum_scatter(
                totals[3].astype(jnp.bfloat16), "dp", scatter_dimension=1, tiled=True
            ).astype(jnp.float32),
            lax.psum_scatter(
                totals[4].astype(jnp.bfloat16), "dp", scatter_dimension=1, tiled=True
            ).astype(jnp.float32),
        )
        expert_shares = (
            lax.psum_scatter(
                expert_part[0].astype(jnp.bfloat16), "dp", scatter_dimension=2, tiled=True
            ).astype(jnp.float32),
            lax.psum_scatter(
                expert_part[1].astype(jnp.bfloat16), "dp", scatter_dimension=1, tiled=True
            ).astype(jnp.float32),
        )
        dense_layers.insert(0, shares)
        expert_layers.insert(0, expert_shares)
    grad_images = grad.reshape(images, length, width)
    grad_qkv = jnp.stack([entry[0] for entry in dense_layers])
    grad_proj = jnp.stack([entry[1] for entry in dense_layers])
    grad_router = jnp.stack([entry[2] for entry in dense_layers])
    grad_gains = jnp.stack([entry[3] for entry in dense_layers])
    grad_shifts = jnp.stack([entry[4] for entry in dense_layers])
    grad_first = jnp.stack([entry[0] for entry in expert_layers])
    grad_second = jnp.stack([entry[1] for entry in expert_layers])
    return (
        out_images,
        grad_images,
        grad_qkv,
        grad_proj,
        grad_router,
        grad_gains,
        grad_shifts,
        grad_first,
        grad_second,
    )


def solution(mesh):
    return jax.shard_map(
        body,
        mesh=mesh,
        in_specs=(
            P(("dp", "expert"), None, None),
            P(("dp", "expert"), None, None),
            P(None, "dp", None),
            P(None, "dp", None),
            P(None, "dp", None),
            P(None, None, "dp"),
            P(None, None, "dp"),
            P(None, "expert", None, "dp"),
            P(None, "expert", "dp", None),
            P(None, ("dp", "expert"), None, None),
        ),
        out_specs=(
            P(("dp", "expert"), None, None),
            P(("dp", "expert"), None, None),
            P(None, "dp", None),
            P(None, "dp", None),
            P(None, "dp", None),
            P(None, None, "dp"),
            P(None, None, "dp"),
            P(None, "expert", None, "dp"),
            P(None, "expert", "dp", None),
        ),
        check_vma=False,
    )
```

profile of v0, /device:TPU:0, one launch (start us, length us, event | category | flops | bytes accessed | tf_op | source)
XLA Modules:
  0.0 1093.9 jit_solution(856967177096205174)
XLA Ops:
  16.5 17.0 %all-gather = bf16[1,2,512]{1,0,2:T(2,128)(2,1)S(1)} all-gather(bf16[1,2,64]{1,0,2:T(2,128)(2,1)S(1)} %copy.377), channel_id=2, replica_groups=mesh['dp'=8,'expert'=4] {'dp'}, dimensions={2}, use_global_device_ids=true | all-gather | bytes 2304 | tf_op jit(solution)/shard_map/all_gather | solution.py:58
  37.7 14.6 %all-gather.1 = bf16[1,2,512]{1,0,2:T(2,128)(2,1)S(1)} all-gather(bf16[1,2,64]{1,0,2:T(2,128)(2,1)S(1)} %copy.378), channel_id=3, replica_groups=mesh['dp'=8,'expert'=4] {'dp'}, dimensions={2}, use_global_device_ids=true | all-gather | bytes 2304 | tf_op jit(solution)/shard_map/all_gather | solution.py:59
  55.9 20.8 %all-gather.3 = bf16[1,512,512]{2,1,0:T(8,128)(2,1)} all-gather(bf16[1,64,512]{2,1,0:T(8,128)(2,1)S(1)} %get-tuple-element.126), channel_id=5, replica_groups=mesh['dp'=8,'expert'=4] {'dp'}, dimensions={1}, use_global_device_ids=true | all-gather | bytes 589824 | tf_op jit(solution)/shard_map/all_gather | solution.py:56
  114.1 4.3 all-to-all-start
  118.4 17.5 %all-gather.4 = bf16[1,512,8]{2,0,1:T(2,128)(2,1)S(1)} all-gather(bf16[1,64,8]{2,0,1:T(2,128)(2,1)} %copy.379), channel_id=6, replica_groups=mesh['dp'=8,'expert'=4] {'dp'}, dimensions={1}, use_global_device_ids=true | all-gather | bytes 9216 | tf_op jit(solution)/shard_map/all_gather | solution.py:57
  137.4 14.6 %all-gather.7 = bf16[1,2,512]{1,0,2:T(2,128)(2,1)S(1)} all-gather(bf16[1,2,64]{1,0,2:T(2,128)(2,1)S(1)} %copy.380), channel_id=9, replica_groups=mesh['dp'=8,'expert'=4] {'dp'}, dimensions={2}, use_global_device_ids=true | all-gather | bytes 2304 | tf_op jit(solution)/shard_map/all_gather | solution.py:58
  153.6 15.8 %all-gather.8 = bf16[1,2,512]{1,0,2:T(2,128)(2,1)S(1)} all-gather(bf16[1,2,64]{1,0,2:T(2,128)(2,1)} %copy.381), channel_id=10, replica_groups=mesh['dp'=8,'expert'=4] {'dp'}, dimensions={2}, use_global_device_ids=true | all-gather | bytes 2304 | tf_op jit(solution)/shard_map/all_gather | solution.py:59
  181.5 9.1 fusion.17
  190.6 6.4 fusion.77
  199.4 4.3 all-to-all-start.1
  204.3 19.3 %all-gather.10 = bf16[1,512,512]{2,1,0:T(8,128)(2,1)} all-gather(bf16[1,64,512]{2,1,0:T(8,128)(2,1)S(1)} %copy-done.50), channel_id=12, replica_groups=mesh['dp'=8,'expert'=4] {'dp'}, dimensions={1}, use_global_device_ids=true | all-gather | bytes 589824 | tf_op jit(solution)/shard_map/all_gather | solution.py:56
  230.3 4.5 gather_fusion
  234.8 4.1 gather_fusion.1
  282.2 4.3 all-to-all-start.2
  287.2 15.1 %all-gather.11 = bf16[1,512,8]{2,0,1:T(2,128)(2,1)S(1)} all-gather(bf16[1,64,8]{2,0,1:T(2,128)(2,1)} %copy.382), channel_id=13, replica_groups=mesh['dp'=8,'expert'=4] {'dp'}, dimensions={1}, use_global_device_ids=true | all-gather | bytes 9216 | tf_op jit(solution)/shard_map/all_gather | solution.py:57
  307.2 9.1 fusion.13
  316.3 6.4 fusion.83
  325.0 4.3 all-to-all-start.3
  330.7 14.8 %all-to-all-done.3 = bf16[4,2,147,512]{3,1,2,0:T(2,128)(2,1)} async-done(((bf16[4,2,147,512]{3,1,2,0:T(2,128)(2,1)}), bf16[4,2,147,512]{3,1,2,0:T(2,128)(2,1)}, u32[]{:S(2)}, u32[]{:S(2)}) %all-to-all-start.3) | async-done | bytes 1204256 | tf_op jit(solution)/shard_map/all_to_all | solution.py:112
  350.7 4.0 gather_fusion.3
  354.7 4.0 gather_fusion.2
  369.8 18.6 %all_to_all.44 = bf16[4,2,147,512]{3,1,2,0:T(2,128)(2,1)S(1)} all-to-all(bf16[4,2,147,512]{3,1,2,0:T(2,128)(2,1)S(1)} %copy.295), channel_id=1, replica_groups=mesh['dp'=8,'expert'=4] {'expert'}, dimensions={0} | all-to-all | bytes 2408448 | tf_op jit(solution)/shard_map/all_to_all | solution.py:202
  388.4 8.1 fusion.5
  401.6 4.3 all-to-all-start.5
  405.9 13.9 %all-to-all-done.5 = bf16[4,2,147,512]{3,1,2,0:T(2,128)(2,1)} async-done(((bf16[4,2,147,512]{3,1,2,0:T(2,128)(2,1)}), bf16[4,2,147,512]{3,1,2,0:T(2,128)(2,1)}, u32[]{:S(2)}, u32[]{:S(2)}) %all-to-all-start.5) | async-done | bytes 1204256 | tf_op jit(solution)/shard_map/all_to_all | solution.py:216
  470.5 18.2 %all_to_all.45 = bf16[4,2,147,512]{3,1,2,0:T(2,128)(2,1)S(1)} all-to-all(bf16[4,2,147,512]{3,1,2,0:T(2,128)(2,1)S(1)} %copy.311), channel_id=1, replica_groups=mesh['dp'=8,'expert'=4] {'expert'}, dimensions={0} | all-to-all | bytes 2408448 | tf_op jit(solution)/shard_map/all_to_all | solution.py:202
  488.6 8.1 fusion.11
  501.8 4.4 all-to-all-start.7
  509.0 11.1 %all-to-all-done.7 = bf16[4,2,147,512]{3,1,2,0:T(2,128)(2,1)} async-done(((bf16[4,2,147,512]{3,1,2,0:T(2,128)(2,1)}), bf16[4,2,147,512]{3,1,2,0:T(2,128)(2,1)}, u32[]{:S(2)}, u32[]{:S(2)}) %all-to-all-start.7) | async-done | bytes 1204256 | tf_op jit(solution)/shard_map/all_to_all | solution.py:216
  531.2 4.1 convolution_convert_fusion
  568.4 6.4 reduce-scatter.39.cloned.1.call-done
  574.8 35.1 %reduce-scatter.37.cloned.1.call-done = bf16[64,1536]{1,0:T(8,128)(2,1)} async-done(((bf16[512,1536]{1,0:T(8,128)(2,1)}), bf16[64,1536]{1,0:T(8,128)(2,1)}) %reduce-scatter.37.cloned.1.call-update) | async-done | bytes 196624 | tf_op jit(solution)/shard_map/reduce_scatter | solution.py:324
  610.0 34.8 %reduce-scatter.35.cloned.1.call-done = bf16[64,1536]{1,0:T(8,128)(2,1)} async-done(((bf16[512,1536]{1,0:T(8,128)(2,1)}), bf16[64,1536]{1,0:T(8,128)(2,1)}) %reduce-scatter.35.cloned.1.call-update) | async-done | bytes 196624 | tf_op jit(solution)/shard_map/reduce_scatter | solution.py:324
  645.1 8.4 bitcast_convert_fusion
  654.8 8.5 bitcast_convert_fusion.1
  663.4 8.4 bitcast_convert_fusion.2
  672.1 8.3 bitcast_convert_fusion.3
  682.5 24.9 %reduce-scatter.53.cloned.1.call-done = bf16[64,2]{1,0:T(8,128)(2,1)} async-done(((bf16[512,2]{1,0:T(8,128)(2,1)}), bf16[64,2]{1,0:T(8,128)(2,1)}) %reduce-scatter.53.cloned.1.call-update) | async-done | bytes 272
  708.2 30.8 %reduce-scatter.49.cloned.1.call-done = bf16[64,2]{1,0:T(8,128)(2,1)} async-done(((bf16[512,2]{1,0:T(8,128)(2,1)}), bf16[64,2]{1,0:T(8,128)(2,1)}) %reduce-scatter.49.cloned.1.call-update) | async-done | bytes 272
  739.8 30.6 %reduce-scatter.43.cloned.1.call-done = bf16[64,8]{1,0:T(8,128)(2,1)} async-done(((bf16[512,8]{1,0:T(8,128)(2,1)}), bf16[64,8]{1,0:T(8,128)(2,1)}) %reduce-scatter.43.cloned.1.call-update) | async-done | bytes 1040
  773.1 28.1 %reduce-scatter.51.cloned.1.call-done = bf16[64,2]{1,0:T(8,128)(2,1)} async-done(((bf16[512,2]{1,0:T(8,128)(2,1)}), bf16[64,2]{1,0:T(8,128)(2,1)}) %reduce-scatter.51.cloned.1.call-update) | async-done | bytes 272
  802.0 30.7 %reduce-scatter.47.cloned.1.call-done = bf16[64,2]{1,0:T(8,128)(2,1)} async-done(((bf16[512,2]{1,0:T(8,128)(2,1)}), bf16[64,2]{1,0:T(8,128)(2,1)}) %reduce-scatter.47.cloned.1.call-update) | async-done | bytes 272
  833.5 10.2 all-reduce.2
  845.4 34.3 %all-reduce.6.cloned.1.call-done = (bf16[64,1536]{1,0:T(8,128)(2,1)}, bf16[64,1536]{1,0:T(8,128)(2,1)}, bf16[64,512]{1,0:T(8,128)(2,1)}, bf16[64,512]{1,0:T(8,128)(2,1)}) async-done(((bf16[64,1536]{1,0:T(8,128)(2,1)}, bf16[64,1536]{1,0:T(8,128)(2,1)}, bf16[64,512]{1,0:T(8,128)(2,1)}, bf16[64,512]{1,0:T(8,128)(2,1)}), (bf16[64,1536]{1,0:T(8,128)(2,1)}, bf16[64,1536]{1,0:T(8,128)(2,1)}, ...) | async-done | bytes 524304 | tf_op jit(solution)/shard_map/psum | solution.py:317
  883.3 48.5 %reduce-scatter.33.cloned.1.call-done = bf16[2,256,512]{2,1,0:T(8,128)(2,1)} async-done(((bf16[2,2048,512]{2,1,0:T(8,128)(2,1)}), bf16[2,256,512]{2,1,0:T(8,128)(2,1)}) %reduce-scatter.33.cloned.1.call-update) | async-done | bytes 524304 | tf_op jit(solution)/shard_map/reduce_scatter | solution.py:344
  931.9 50.7 %reduce-scatter.31.cloned.1.call-done = bf16[2,256,512]{2,1,0:T(8,128)(2,1)} async-done(((bf16[2,2048,512]{2,1,0:T(8,128)(2,1)}), bf16[2,256,512]{2,1,0:T(8,128)(2,1)}) %reduce-scatter.31.cloned.1.call-update) | async-done | bytes 524304 | tf_op jit(solution)/shard_map/reduce_scatter | solution.py:344
  985.2 47.9 %reduce-scatter.29.cloned.1.call-done = bf16[2,512,256]{2,1,0:T(8,128)(2,1)} async-done(((bf16[2,512,2048]{2,1,0:T(8,128)(2,1)}), bf16[2,512,256]{2,1,0:T(8,128)(2,1)}) %reduce-scatter.29.cloned.1.call-update) | async-done | bytes 524304 | tf_op jit(solution)/shard_map/reduce_scatter | solution.py:341
  1033.2 50.7 %reduce-scatter.27.cloned.1.call-done = bf16[2,512,256]{2,1,0:T(8,128)(2,1)} async-done(((bf16[2,512,2048]{2,1,0:T(8,128)(2,1)}), bf16[2,512,256]{2,1,0:T(8,128)(2,1)}) %reduce-scatter.27.cloned.1.call-update) | async-done | bytes 524304 | tf_op jit(solution)/shard_map/reduce_scatter | solution.py:341
  (571 shorter events, 274.5 us)
Async XLA Ops:
  7.2 76.4 %all-gather.21.cloned.1.call-start = ((), (), s32[]{:S(2)}) async-start(), calls=%async_computation.26 | async-start | bytes 1769472 | tf_op jit(solution)/shard_map/all_gather | solution.py:55
  9.1 172.3 %all-gather.23.cloned.1.call-start = ((), (), s32[]{:S(2)}) async-start(), calls=%async_computation.27 | async-start | bytes 4718592 | tf_op jit(solution)/shard_map/all_gather | solution.py:62
  11.5 179.2 %all-gather.25.cloned.1.call-start = ((), (), s32[]{:S(2)}) async-start(), calls=%async_computation.28 | async-start | bytes 4718592 | tf_op jit(solution)/shard_map/all_gather | solution.py:63
  12.6 229.4 %all-gather.27.cloned.1.call-start = ((), (), s32[]{:S(2)}) async-start(), calls=%async_computation.29 | async-start | bytes 1769472 | tf_op jit(solution)/shard_map/all_gather | solution.py:55
  13.2 294.0 %all-gather.29.cloned.1.call-start = ((), (), s32[]{:S(2)}) async-start(), calls=%async_computation.30 | async-start | bytes 4718592 | tf_op jit(solution)/shard_map/all_gather | solution.py:62
  13.8 302.5 %all-gather.31.cloned.1.call-start = ((), (), s32[]{:S(2)}) async-start(), calls=%async_computation.31 | async-start | bytes 4718592 | tf_op jit(solution)/shard_map/all_gather | solution.py:63
  14.5 22.5 %copy-start.132 = (bf16[2,2,64]{2,1,0:T(2,128)(2,1)S(1)}, bf16[2,2,64]{2,1,0:T(2,128)(2,1)}, u32[]{:S(2)}) copy-start(bf16[2,2,64]{2,1,0:T(2,128)(2,1)} %param.18) | copy-start | bytes 1540
  15.7 39.6 %copy-start.57 = (bf16[2,64,512]{2,1,0:T(8,128)(2,1)S(1)}, bf16[2,64,512]{2,1,0:T(8,128)(2,1)}, u32[]{:S(2)}) copy-start(bf16[2,64,512]{2,1,0:T(8,128)(2,1)} %param.15) | copy-start | bytes 393220
  33.8 42.9 %copy-start.110 = (s32[2,2,197,2]{2,3,1,0:T(2,128)S(1)}, s32[2,2,197,2]{2,3,1,0:T(2,128)}, u32[]{:S(2)}) copy-start(s32[2,2,197,2]{2,3,1,0:T(2,128)} %param.21) | copy-start | bytes 18916
  33.9 45.8 %copy-start.130 = (bf16[2,64,8]{1,2,0:T(8,128)(2,1)S(1)}, bf16[2,64,8]{1,2,0:T(8,128)(2,1)}, u32[]{:S(2)}) copy-start(bf16[2,64,8]{1,2,0:T(8,128)(2,1)} %param.16) | copy-start | bytes 6148
  36.6 49.3 %copy-start.94 = (f32[512]{0:T(512)}, f32[512]{0:T(512)S(1)}, u32[]{:S(2)}) copy-start(f32[512]{0:T(512)S(1)} %get-tuple-element.80) | copy-start | bytes 6148
  36.6 68.1 %copy-start.100 = (f32[512]{0:T(512)}, f32[512]{0:T(512)S(1)}, u32[]{:S(2)}) copy-start(f32[512]{0:T(512)S(1)} %get-tuple-element.79) | copy-start | bytes 6148
  36.7 49.2 %copy-start.8 = (f32[394,512]{1,0:T(8,128)}, f32[394,512]{1,0:T(8,128)S(1)}, u32[]{:S(2)}) copy-start(f32[394,512]{1,0:T(8,128)S(1)} %reshape.331) | copy-start | bytes 2420740
  36.9 49.0 %copy-start.78 = (f32[394]{0:T(512)}, f32[394]{0:T(512)S(1)}, u32[]{:S(2)}) copy-start(f32[394]{0:T(512)S(1)} %rsqrt.40) | copy-start | bytes 4732
  37.0 48.9 %copy-start.80 = (f32[394]{0:T(512)}, f32[394]{0:T(512)S(1)}, u32[]{:S(2)}) copy-start(f32[394]{0:T(512)S(1)} %div.51) | copy-start | bytes 4732
  55.3 30.6 %copy-start.104 = (f32[512]{0:T(512)}, f32[512]{0:T(512)S(1)}, u32[]{:S(2)}) copy-start(f32[512]{0:T(512)S(1)} %get-tuple-element.82) | copy-start | bytes 6148
  79.0 26.5 %copy-start.116 = (s32[394]{0:T(512)}, s32[394]{0:T(512)S(1)}, u32[]{:S(2)}) copy-start(s32[394]{0:T(512)S(1)} %get-tuple-element.110) | copy-start | bytes 4732
  79.0 26.5 %copy-start.118 = (s32[394]{0:T(512)}, s32[394]{0:T(512)S(1)}, u32[]{:S(2)}) copy-start(s32[394]{0:T(512)S(1)} %get-tuple-element.168) | copy-start | bytes 4732
  114.1 67.3 %all-to-all-start = ((bf16[4,2,147,512]{3,1,2,0:T(2,128)(2,1)}), bf16[4,2,147,512]{3,1,2,0:T(2,128)(2,1)}, u32[]{:S(2)}, u32[]{:S(2)}) async-start(bf16[4,2,147,512]{3,1,2,0:T(2,128)(2,1)} %copy.273), calls=%async_computation | async-start | bytes 2408448 | tf_op jit(solution)/shard_map/all_to_all | solution.py:104
  180.2 61.7 %copy-start.106 = (f32[512]{0:T(512)}, f32[512]{0:T(512)S(1)}, u32[]{:S(2)}) copy-start(f32[512]{0:T(512)S(1)} %get-tuple-element.78) | copy-start | bytes 6148
  181.5 92.2 %copy-start.112 = (s32[394]{0:T(512)}, s32[394]{0:T(512)S(1)}, u32[]{:S(2)}) copy-start(s32[394]{0:T(512)S(1)} %get-tuple-element.104) | copy-start | bytes 4732
  197.1 26.6 %copy-start.71 = (bf16[1,512,8]{1,2,0:T(8,128)(2,1)S(1)}, bf16[1,512,8]{1,2,0:T(8,128)(2,1)}, u32[]{:S(2)}) copy-start(bf16[1,512,8]{1,2,0:T(8,128)(2,1)} %copy.271) | copy-start | bytes 24580
  197.1 27.8 %copy-start.59 = (s32[394,1]{0,1:T(1,128)S(1)}, s32[394,1]{0,1:T(1,128)}, u32[]{:S(2)}) copy-start(s32[394,1]{0,1:T(1,128)} %copy-done.58) | copy-start | bytes 4732
  197.1 27.8 %copy-start.62 = (s32[394,1]{0,1:T(1,128)S(1)}, s32[394,1]{0,1:T(1,128)}, u32[]{:S(2)}) copy-start(s32[394,1]{0,1:T(1,128)} %copy-done.61) | copy-start | bytes 4732
  199.4 25.7 %all-to-all-start.1 = ((bf16[4,2,147,512]{3,1,2,0:T(2,128)(2,1)}), bf16[4,2,147,512]{3,1,2,0:T(2,128)(2,1)}, u32[]{:S(2)}, u32[]{:S(2)}) async-start(bf16[4,2,147,512]{3,1,2,0:T(2,128)(2,1)} %copy.275), calls=%async_computation.1 | async-start | bytes 2408448 | tf_op jit(solution)/shard_map/all_to_all | solution.py:112
  204.3 69.4 %copy-start.114 = (s32[394]{0:T(512)}, s32[394]{0:T(512)S(1)}, u32[]{:S(2)}) copy-start(s32[394]{0:T(512)S(1)} %get-tuple-element.106) | copy-start | bytes 4732
  282.2 25.0 %all-to-all-start.2 = ((bf16[4,2,147,512]{3,1,2,0:T(2,128)(2,1)}), bf16[4,2,147,512]{3,1,2,0:T(2,128)(2,1)}, u32[]{:S(2)}, u32[]{:S(2)}) async-start(bf16[4,2,147,512]{3,1,2,0:T(2,128)(2,1)} %copy.290), calls=%async_computation.2 | async-start | bytes 2408448 | tf_op jit(solution)/shard_map/all_to_all | solution.py:104
  325.0 20.4 %all-to-all-start.3 = ((bf16[4,2,147,512]{3,1,2,0:T(2,128)(2,1)}), bf16[4,2,147,512]{3,1,2,0:T(2,128)(2,1)}, u32[]{:S(2)}, u32[]{:S(2)}) async-start(bf16[4,2,147,512]{3,1,2,0:T(2,128)(2,1)} %copy.292), calls=%async_computation.3 | async-start | bytes 2408448 | tf_op jit(solution)/shard_map/all_to_all | solution.py:112
  367.4 21.0 %copy-start.136 = (bf16[1,2,2048,512]{3,2,1,0:T(8,128)(2,1)S(1)}, bf16[1,2,2048,512]{3,2,1,0:T(8,128)(2,1)}, u32[]{:S(2)}) copy-start(bf16[1,2,2048,512]{3,2,1,0:T(8,128)(2,1)} %all-gather.31.cloned.1.call-done) | copy-start | bytes 12582916
  401.6 18.2 %all-to-all-start.5 = ((bf16[4,2,147,512]{3,1,2,0:T(2,128)(2,1)}), bf16[4,2,147,512]{3,1,2,0:T(2,128)(2,1)}, u32[]{:S(2)}, u32[]{:S(2)}) async-start(bf16[4,2,147,512]{3,1,2,0:T(2,128)(2,1)} %copy.297), calls=%async_computation.5 | async-start | bytes 2408448 | tf_op jit(solution)/shard_map/all_to_all | solution.py:216
  501.8 18.2 %all-to-all-start.7 = ((bf16[4,2,147,512]{3,1,2,0:T(2,128)(2,1)}), bf16[4,2,147,512]{3,1,2,0:T(2,128)(2,1)}, u32[]{:S(2)}, u32[]{:S(2)}) async-start(bf16[4,2,147,512]{3,1,2,0:T(2,128)(2,1)} %copy.313), calls=%async_computation.7 | async-start | bytes 2408448 | tf_op jit(solution)/shard_map/all_to_all | solution.py:216
  506.2 62.2 %reduce-scatter.41.cloned.1.call-start = ((), (), s32[]{:S(2)}) async-start(), calls=%async_computation.35 | async-start | bytes 589824 | tf_op jit(solution)/shard_map/reduce_scatter | solution.py:327
  508.8 66.0 %reduce-scatter.39.cloned.1.call-start = ((), (), s32[]{:S(2)}) async-start(), calls=%async_computation.34 | async-start | bytes 589824 | tf_op jit(solution)/shard_map/reduce_scatter | solution.py:327
  531.1 78.8 %reduce-scatter.37.cloned.1.call-start = ((), (), s32[]{:S(2)}) async-start(), calls=%async_computation.33 | async-start | bytes 1769472 | tf_op jit(solution)/shard_map/reduce_scatter | solution.py:324
  535.3 109.5 %reduce-scatter.35.cloned.1.call-start = ((), (), s32[]{:S(2)}) async-start(), calls=%async_computation.32 | async-start | bytes 1769472 | tf_op jit(solution)/shard_map/reduce_scatter | solution.py:324
  559.2 121.3 %reduce-scatter.45.cloned.1.call-start = ((), (), s32[]{:S(2)}) async-start(), calls=%async_computation.37 | async-start | bytes 147456
  560.2 147.2 %reduce-scatter.53.cloned.1.call-start = ((), (), s32[]{:S(2)}) async-start(), calls=%async_computation.41 | async-start | bytes 147456
  561.2 177.9 %reduce-scatter.49.cloned.1.call-start = ((), (), s32[]{:S(2)}) async-start(), calls=%async_computation.39 | async-start | bytes 147456
  562.1 208.3 %reduce-scatter.43.cloned.1.call-start = ((), (), s32[]{:S(2)}) async-start(), calls=%async_computation.36 | async-start | bytes 147456
  563.1 238.1 %reduce-scatter.51.cloned.1.call-start = ((), (), s32[]{:S(2)}) async-start(), calls=%async_computation.40 | async-start | bytes 147456
  567.5 265.2 %reduce-scatter.47.cloned.1.call-start = ((), (), s32[]{:S(2)}) async-start(), calls=%async_computation.38 | async-start | bytes 147456
  568.4 311.4 %all-reduce.6.cloned.1.call-start = ((), (), s32[]{:S(2)}) async-start(), calls=%async_computation.42 | async-start | bytes 1048576 | tf_op jit(solution)/shard_map/psum | solution.py:317
  644.8 287.1 %reduce-scatter.33.cloned.1.call-start = ((), (), s32[]{:S(2)}) async-start(), calls=%async_computation.25 | async-start | bytes 4718592 | tf_op jit(solution)/shard_map/reduce_scatter | solution.py:344
  653.5 329.1 %reduce-scatter.31.cloned.1.call-start = ((), (), s32[]{:S(2)}) async-start(), calls=%async_computation.24 | async-start | bytes 4718592 | tf_op jit(solution)/shard_map/reduce_scatter | solution.py:344
  663.3 369.8 %reduce-scatter.29.cloned.1.call-start = ((), (), s32[]{:S(2)}) async-start(), calls=%async_computation.23 | async-start | bytes 4718592 | tf_op jit(solution)/shard_map/reduce_scatter | solution.py:341
  671.8 412.1 %reduce-scatter.27.cloned.1.call-start = ((), (), s32[]{:S(2)}) async-start(), calls=%async_computation.22 | async-start | bytes 4718592 | tf_op jit(solution)/shard_map/reduce_scatter | solution.py:341
  680.4 90.8 %copy-start.13 = (f32[394,512]{1,0:T(8,128)S(1)}, f32[394,512]{1,0:T(8,128)}, u32[]{:S(2)}) copy-start(f32[394,512]{1,0:T(8,128)} %copy-done.12) | copy-start | bytes 2420740
  680.4 90.8 %copy-start.49 = (f32[394,512]{1,0:T(8,128)S(1)}, f32[394,512]{1,0:T(8,128)}, u32[]{:S(2)}) copy-start(f32[394,512]{1,0:T(8,128)} %get-tuple-element.166) | copy-start | bytes 2420740
  (118 other events, 429.0 us)
Sparse Core Ops, SparseCore 0:
  10.2 29.4 all-gather.20
  41.3 51.4 all-gather.22
  94.4 47.3 all-gather.24
  143.9 25.6 all-gather.26
  171.0 50.4 all-gather.28
  222.9 45.9 all-gather.30
  509.3 33.6 reduce-scatter.40
  545.3 29.4 reduce-scatter.38
  577.7 32.2 reduce-scatter.36
  612.1 32.6 reduce-scatter.34
  647.6 28.8 reduce-scatter.44
  678.6 28.7 reduce-scatter.52
  710.2 28.7 reduce-scatter.48
  741.7 28.6 reduce-scatter.42
  772.5 28.7 reduce-scatter.50
  803.9 28.7 reduce-scatter.46
  835.8 43.9 all-reduce.5
  881.9 49.8 reduce-scatter.32
  934.2 48.3 reduce-scatter.30
  984.7 48.3 reduce-scatter.28
  1035.5 48.3 reduce-scatter.26
where the time goes:
time: 1100 us; the launch traced here: 1090 us
  waiting for transfers between devices  495 us (45%)
  local copies, waits for them, and re-layouts  187 us (17%)
  blocking collectives  182 us (17%)
  matrix products  151 us (14%)
  other arithmetic  35 us (3%)
  starting transfers between devices  27.2 us (2%)
  between operations  16.9 us (2%)
    unnamed x27, waiting for transfers between devices  147 us
    reduce_scatter x2, waiting for transfers between devices, body(): lax.psum_scatter(expert_part[1].astype(jnp.bfloat16), 'dp', scatter_dimen...  99.3 us
    reduce_scatter x2, waiting for transfers between devices, body(): lax.psum_scatter(expert_part[0].astype(jnp.bfloat16), 'dp', scatter_dimen...  98.6 us
    reduce_scatter x2, waiting for transfers between devices, body(): lax.psum_scatter(totals[0].astype(jnp.bfloat16), 'dp', scatter_dimension=...  70 us
    all_gather x2, blocking collectives, layer_forward(): lax.all_gather(w_proj[which], 'dp', axis=0, tiled=True)  40.1 us
    all_to_all x2, blocking collectives, layer_backward(): lax.all_to_all(slot_grads, 'expert', split_axis=0, concat_axis=0, tiled=T...  36.8 us
    psum x1, waiting for transfers between devices, body(): lax.psum(dense[0].astype(jnp.bfloat16), 'expert').astype(jnp.float32)  34.3 us
    all_gather x2, blocking collectives, layer_forward(): lax.all_gather(w_router[which], 'dp', axis=0, tiled=True)  32.6 us
  transfers between devices with their start and end apart: 27, of which 16 were waited for; matrix products, arithmetic and copies ran while one was open for 23% of the time, Pallas kernels for 0%

commit v1 on v0

v1 whole, which is shorter than its diff:
```python
import jax
import jax.numpy as jnp
from jax import lax
from jax.sharding import PartitionSpec as P

HEADS = 8
HEAD_DIM = 64
SEQ = 197
LAYERS = 2


EPSILON = 1e-06
ROOT_HALF = 0.7071067811865476
INV_ROOT_TAU = 0.3989422804014327


def layer_norm(values, scale_in, shift_in):
    center = values - jnp.mean(values, axis=-1, keepdims=True)
    variance = jnp.mean(center * center, axis=-1, keepdims=True)
    inverse = lax.rsqrt(variance + EPSILON)
    normed = center * inverse
    return (normed * scale_in + shift_in, normed, inverse)


def norm_back(grad_out, normed, inverse, scale_in):
    grad_normed = grad_out * scale_in
    first_mean = jnp.mean(grad_normed, axis=-1, keepdims=True)
    second_mean = jnp.mean(grad_normed * normed, axis=-1, keepdims=True)
    grad_in = inverse * (grad_normed - first_mean - normed * second_mean)
    return (grad_in, jnp.sum(grad_out * normed, axis=0), jnp.sum(grad_out, axis=0))


def softmax_rows(scores):
    highest = jnp.max(scores, axis=-1, keepdims=True)
    powers = jnp.exp(scores - highest)
    row_total = jnp.sum(powers, axis=-1, keepdims=True)
    return (powers / row_total, highest + jnp.log(row_total))


def gelu_value(preact):
    return 0.5 * preact * (1.0 + lax.erf(preact * ROOT_HALF))


def gelu_slope(preact):
    return (
        0.5 * (1.0 + lax.erf(preact * ROOT_HALF))
        + preact * jnp.exp(-0.5 * preact * preact) * INV_ROOT_TAU
    )


def gather_dense(which, w_qkv, w_proj, w_router, norm_gains, norm_shifts):
    packed = jnp.concatenate(
        [
            w_qkv[which],
            w_proj[which],
            w_router[which],
            norm_gains[which].T,
            norm_shifts[which].T,
        ],
        axis=1,
    )
    full = lax.all_gather(packed, "dp", axis=0, tiled=True)
    width = full.shape[0]
    experts = w_router.shape[2]
    wide = full[:, 4 * width :]
    gains = wide[:, experts : experts + 2].T.astype(jnp.float32)
    shifts = wide[:, experts + 2 : experts + 4].T.astype(jnp.float32)
    return (full[:, : 3 * width], full[:, 3 * width : 4 * width], wide[:, :experts], gains, shifts)


def gather_experts(which, w_first, w_second):
    first_full = lax.all_gather(w_first[which], "dp", axis=2, tiled=True)
    second_full = lax.all_gather(w_second[which], "dp", axis=1, tiled=True)
    return (first_full, second_full)


def route_tables(route, experts_total, capacity):
    labels = jnp.arange(experts_total, dtype=jnp.int32)
    pick_first = (route[:, 0:1] == labels[None, :]).astype(jnp.int32)
    pick_second = (route[:, 1:2] == labels[None, :]).astype(jnp.int32)
    both_picks = pick_first + pick_second
    before = jnp.cumsum(both_picks, axis=0) - both_picks
    slot_first = route[:, 0] * capacity + jnp.sum(before * pick_first, axis=1)
    slot_second = route[:, 1] * capacity + jnp.sum(before * pick_second, axis=1)
    slot_ids = jnp.arange(experts_total * capacity, dtype=jnp.int32)
    place_first = (slot_ids[:, None] == slot_first[None, :]).astype(jnp.bfloat16)
    place_second = (slot_ids[:, None] == slot_second[None, :]).astype(jnp.bfloat16)
    return (
        pick_first.astype(jnp.float32),
        pick_second.astype(jnp.float32),
        place_first,
        place_second,
    )


def exchange(block):
    return lax.all_to_all(block, "expert", split_axis=0, concat_axis=0, tiled=True)


def layer_forward(resid, dense, experts, tables):
    qkv_full, proj_full, router_full, gains_wide, shifts_wide = dense
    first_full, second_full = experts
    pick_first_f, pick_second_f, place_first, place_second = tables
    tok_count, width = resid.shape
    images = tok_count // SEQ
    attn_norm, unit_a, inv_a = layer_norm(resid, gains_wide[0], shifts_wide[0])
    attn_in = attn_norm.astype(jnp.bfloat16)
    packed = jnp.dot(attn_in, qkv_full, preferred_element_type=jnp.float32)
    head_shape = (images, SEQ, HEADS, HEAD_DIM)
    query = (packed[:, :width] * HEAD_DIM ** (-0.5)).astype(jnp.bfloat16).reshape(head_shape)
    keyed = packed[:, width : 2 * width].astype(jnp.bfloat16).reshape(head_shape)
    valued = packed[:, 2 * width :].astype(jnp.bfloat16).reshape(head_shape)
    scores = jnp.einsum("iqhd,ikhd->ihqk", query, keyed, preferred_element_type=jnp.float32)
    probs, log_total = softmax_rows(scores)
    mixed = jnp.einsum(
        "ihqk,ikhd->iqhd", probs.astype(jnp.bfloat16), valued, preferred_element_type=jnp.float32
    )
    mixed = mixed.reshape(tok_count, width).astype(jnp.bfloat16)
    resid_mid = resid + jnp.dot(mixed, proj_full, preferred_element_type=jnp.float32)
    moe_norm, unit_b, inv_b = layer_norm(resid_mid, gains_wide[1], shifts_wide[1])
    moe_in = moe_norm.astype(jnp.bfloat16)
    logits = jnp.dot(moe_in, router_full, preferred_element_type=jnp.float32)
    router_probs, _ = softmax_rows(logits)
    experts_total = router_full.shape[1]
    local_count = first_full.shape[0]
    peers = lax.axis_size("expert")
    capacity = place_first.shape[0] // experts_total
    outgoing = jnp.dot(place_first + place_second, moe_in, preferred_element_type=jnp.float32)
    outgoing = outgoing.astype(jnp.bfloat16).reshape(peers, local_count, capacity, width)
    incoming = exchange(outgoing)
    hidden_pre = jnp.einsum(
        "sjcd,jdf->sjcf", incoming, first_full, preferred_element_type=jnp.float32
    )
    hidden_act = gelu_value(hidden_pre).astype(jnp.bfloat16)
    result = jnp.einsum(
        "sjcf,jfd->sjcd", hidden_act, second_full, preferred_element_type=jnp.float32
    ).astype(jnp.bfloat16)
    returned = exchange(result).reshape(experts_total * capacity, width)
    gate_first = jnp.sum(router_probs * pick_first_f, axis=1)
    gate_second = jnp.sum(router_probs * pick_second_f, axis=1)
    back_first = jnp.einsum("st,sd->td", place_first, returned, preferred_element_type=jnp.float32)
    back_second = jnp.einsum(
        "st,sd->td", place_second, returned, preferred_element_type=jnp.float32
    )
    resid_out = resid_mid + (gate_first[:, None] * back_first + gate_second[:, None] * back_second)
    saved = (
        unit_a,
        inv_a,
        attn_in,
        query,
        keyed,
        valued,
        log_total,
        mixed,
        unit_b,
        inv_b,
        moe_in,
        router_probs,
        incoming,
        hidden_pre,
        hidden_act,
        back_first,
        back_second,
        gate_first,
        gate_second,
    )
    return (resid_out, saved)


def layer_backward(grad_out, dense, experts, tables, saved):
    qkv_full, proj_full, router_full, gains_wide, _ = dense
    first_full, second_full = experts
    pick_first_f, pick_second_f, place_first, place_second = tables
    (
        unit_a,
        inv_a,
        attn_in,
        query,
        keyed,
        valued,
        log_total,
        mixed,
        unit_b,
        inv_b,
        moe_in,
        router_probs,
        incoming,
        hidden_pre,
        hidden_act,
        back_first,
        back_second,
        gate_first,
        gate_second,
    ) = saved
    tok_count, width = grad_out.shape
    images = tok_count // SEQ
    send_first = (gate_first[:, None] * grad_out).astype(jnp.bfloat16)
    send_second = (gate_second[:, None] * grad_out).astype(jnp.bfloat16)
    slot_grads = jnp.dot(place_first, send_first, preferred_element_type=jnp.float32) + jnp.dot(
        place_second, send_second, preferred_element_type=jnp.float32
    )
    slot_grads = slot_grads.astype(jnp.bfloat16).reshape(incoming.shape)
    grad_result = exchange(slot_grads)
    grad_gate_first = jnp.sum(grad_out * back_first, axis=1)
    grad_gate_second = jnp.sum(grad_out * back_second, axis=1)
    grad_act = jnp.einsum(
        "sjcd,jfd->sjcf", grad_result, second_full, preferred_element_type=jnp.float32
    )
    grad_pre = (grad_act * gelu_slope(hidden_pre)).astype(jnp.bfloat16)
    grad_rows = jnp.einsum(
        "sjcf,jdf->sjcd", grad_pre, first_full, preferred_element_type=jnp.float32
    ).astype(jnp.bfloat16)
    grad_back = exchange(grad_rows)
    grad_second = jnp.einsum(
        "sjcf,sjcd->jfd", hidden_act, grad_result, preferred_element_type=jnp.float32
    ).astype(jnp.bfloat16)
    grad_first = jnp.einsum(
        "sjcd,sjcf->jdf", incoming, grad_pre, preferred_element_type=jnp.float32
    ).astype(jnp.bfloat16)
    grad_back, grad_second, grad_first = lax.optimization_barrier(
        (grad_back, grad_second, grad_first)
    )
    share_second = lax.psum_scatter(grad_second, "dp", scatter_dimension=1, tiled=True)
    share_first = lax.psum_scatter(grad_first, "dp", scatter_dimension=2, tiled=True)
    grad_back = grad_back.reshape(-1, width)
    grad_moe = jnp.einsum(
        "st,sd->td", place_first + place_second, grad_back, preferred_element_type=jnp.float32
    )
    grad_probs = pick_first_f * grad_gate_first[:, None] + pick_second_f * grad_gate_second[:, None]
    weighted = jnp.sum(router_probs * grad_probs, axis=1, keepdims=True)
    grad_logits = (router_probs * (grad_probs - weighted)).astype(jnp.bfloat16)
    grad_router = jnp.einsum("td,te->de", moe_in, grad_logits, preferred_element_type=jnp.float32)
    grad_moe = grad_moe + jnp.einsum(
        "te,de->td", grad_logits, router_full, preferred_element_type=jnp.float32
    )
    grad_norm_b, gain_b_grad, shift_b_grad = norm_back(grad_moe, unit_b, inv_b, gains_wide[1])
    grad_mid = grad_out + grad_norm_b
    grad_branch = grad_mid.astype(jnp.bfloat16)
    grad_proj = jnp.einsum("td,te->de", mixed, grad_branch, preferred_element_type=jnp.float32)
    grad_mixed = jnp.einsum("te,de->td", grad_branch, proj_full, preferred_element_type=jnp.float32)
    grad_mixed = grad_mixed.astype(jnp.bfloat16).reshape(images, SEQ, HEADS, HEAD_DIM)
    scores = jnp.einsum("iqhd,ikhd->ihqk", query, keyed, preferred_element_type=jnp.float32)
    probs = jnp.exp(scores - log_total)
    grad_weights = jnp.einsum(
        "iqhd,ikhd->ihqk", grad_mixed, valued, preferred_element_type=jnp.float32
    )
    grad_valued = jnp.einsum(
        "ihqk,iqhd->ikhd",
        probs.astype(jnp.bfloat16),
        grad_mixed,
        preferred_element_type=jnp.float32,
    ).astype(jnp.bfloat16)
    row_inner = jnp.sum(probs * grad_weights, axis=-1, keepdims=True)
    grad_scores = (probs * (grad_weights - row_inner)).astype(jnp.bfloat16)
    grad_query = jnp.einsum(
        "ihqk,ikhd->iqhd", grad_scores, keyed, preferred_element_type=jnp.float32
    ).astype(jnp.bfloat16)
    grad_query = grad_query * jnp.asarray(HEAD_DIM ** (-0.5), jnp.bfloat16)
    grad_keyed = jnp.einsum(
        "ihqk,iqhd->ikhd", grad_scores, query, preferred_element_type=jnp.float32
    ).astype(jnp.bfloat16)
    grad_packed = jnp.concatenate(
        [
            grad_query.reshape(tok_count, width),
            grad_keyed.reshape(tok_count, width),
            grad_valued.reshape(tok_count, width),
        ],
        axis=1,
    )
    grad_qkv = jnp.einsum("td,te->de", attn_in, grad_packed, preferred_element_type=jnp.float32)
    grad_attn = jnp.einsum("te,de->td", grad_packed, qkv_full, preferred_element_type=jnp.float32)
    grad_norm_a, gain_a_grad, shift_a_grad = norm_back(grad_attn, unit_a, inv_a, gains_wide[0])
    grad_in = grad_mid + grad_norm_a
    low = jnp.bfloat16
    small = jnp.concatenate(
        [
            grad_qkv.astype(low),
            grad_proj.astype(low),
            grad_router.astype(low),
            jnp.stack([gain_a_grad, gain_b_grad, shift_a_grad, shift_b_grad], axis=1).astype(low),
        ],
        axis=1,
    )
    share_small = lax.psum_scatter(small, "dp", scatter_dimension=0, tiled=True)
    return (grad_in, share_small, share_first, share_second)


def body(
    embedded, cotangent, w_qkv, w_proj, w_router, norm_gains, norm_shifts, w_first, w_second, routes
):
    images, length, width = embedded.shape
    tok_count = images * length
    experts_total = w_router.shape[2]
    capacity = -(-max(2, 3 * tok_count // experts_total) // 8) * 8
    resid = embedded.reshape(tok_count, width).astype(jnp.float32)
    dense, experts, tables, saved = [], [], [], []
    for which in range(LAYERS):
        dense.append(gather_dense(which, w_qkv, w_proj, w_router, norm_gains, norm_shifts))
        experts.append(gather_experts(which, w_first, w_second))
    for which in range(LAYERS):
        tables.append(route_tables(routes[which].reshape(tok_count, 2), experts_total, capacity))
        resid, kept = layer_forward(resid, dense[which], experts[which], tables[which])
        saved.append(kept)
    out_images = resid.reshape(images, length, width).astype(jnp.bfloat16)
    grad = cotangent.reshape(tok_count, width).astype(jnp.float32)
    smalls, firsts, seconds = [None] * LAYERS, [None] * LAYERS, [None] * LAYERS
    for which in reversed(range(LAYERS)):
        grad, smalls[which], firsts[which], seconds[which] = layer_backward(
            grad, dense[which], experts[which], tables[which], saved[which]
        )
    total = lax.psum(jnp.stack(smalls), "expert").astype(jnp.float32)
    grad_images = grad.reshape(images, length, width)
    wide = total[:, :, 4 * width :]
    return (
        out_images,
        grad_images,
        total[:, :, : 3 * width],
        total[:, :, 3 * width : 4 * width],
        wide[:, :, :experts_total],
        jnp.swapaxes(wide[:, :, experts_total : experts_total + 2], 1, 2),
        jnp.swapaxes(wide[:, :, experts_total + 2 :], 1, 2),
        jnp.stack(firsts).astype(jnp.float32),
        jnp.stack(seconds).astype(jnp.float32),
    )


def solution(mesh):
    return jax.shard_map(
        body,
        mesh=mesh,
        in_specs=(
            P(("dp", "expert"), None, None),
            P(("dp", "expert"), None, None),
            P(None, "dp", None),
            P(None, "dp", None),
            P(None, "dp", None),
            P(None, None, "dp"),
            P(None, None, "dp"),
            P(None, "expert", None, "dp"),
            P(None, "expert", "dp", None),
            P(None, ("dp", "expert"), None, None),
        ),
        out_specs=(
            P(("dp", "expert"), None, None),
            P(("dp", "expert"), None, None),
            P(None, "dp", None),
            P(None, "dp", None),
            P(None, "dp", None),
            P(None, None, "dp"),
            P(None, None, "dp"),
            P(None, "expert", None, "dp"),
            P(None, "expert", "dp", None),
        ),
        check_vma=False,
    )
```

time: 1100 us -> 789 us (0.72)
  blocking collectives: 182 us -> 0 us
  local copies, waits for them, and re-layouts: 187 us -> 84.7 us
  waiting for transfers between devices: 495 us -> 464 us
  other arithmetic: 35 us -> 24 us
    all_gather x6, waiting for transfers between devices: 0.03 us -> 149 us  [the longest x2 76.1 us: gather_experts(): second_full = lax.all_gather(w_second[which], 'dp', axis=1, tiled=True)]
    unnamed x27 -> x13, waiting for transfers between devices: 147 us -> 3.6 us
    all_gather x8 -> x0, blocking collectives: 135 us -> none  [the longest x2 40.1 us: layer_forward(): lax.all_gather(w_proj[which], 'dp', axis=0, tiled=True)]
    reduce_scatter x8 -> x6, waiting for transfers between devices: 274 us -> 231 us  [the longest x2 98.6 us: layer_backward(): lax.psum_scatter(grad_first, 'dp', scatter_dimension=2, tiled=True)]
    all_to_all x2 -> x0, blocking collectives: 36.8 us -> none  [layer_backward(): lax.all_to_all(slot_grads, 'expert', split_axis=0, concat_axis=0, tiled=T...]
    reshape x13 -> x1, local copies, waits for them, and re-layouts: 32.8 us -> 0.01 us  [the longest x4 11.9 us: layer_forward(): outgoing.astype(jnp.bfloat16).reshape(peers, local_count, capacity, width)]
    unnamed x304 -> x225, local copies, waits for them, and re-layouts: 32.4 us -> 13.3 us
    gather x4 -> x0, local copies, waits for them, and re-layouts: 16.6 us -> none  [the longest x2 8.56 us: layer_forward(): back_first = jnp.take(returned, slot_first, axis=0).astype(jnp.float32)]
  transfers between devices with their start and end apart: 27 -> 21, of which waited for: 16 -> 15; matrix products, arithmetic and copies ran while one was open for 23% -> 24% of each run, Pallas kernels for 0% -> 0%
where the time goes in v1:
time: 789 us; the launch traced here: 779 us
  waiting for transfers between devices  464 us (59%)
  matrix products  156 us (20%)
  local copies, waits for them, and re-layouts  84.7 us (11%)
  starting transfers between devices  34.3 us (4%)
  other arithmetic  24 us (3%)
  between operations  16 us (2%)
    reduce_scatter x2, waiting for transfers between devices, layer_backward(): lax.psum_scatter(grad_first, 'dp', scatter_dimension=2, tiled=True)  98.6 us
    reduce_scatter x2, waiting for transfers between devices, layer_backward(): lax.psum_scatter(grad_second, 'dp', scatter_dimension=1, tiled=True)  96.2 us
    all_gather x2, waiting for transfers between devices, gather_experts(): second_full = lax.all_gather(w_second[which], 'dp', axis=1, tiled=True)  76.1 us
    all_gather x2, waiting for transfers between devices, gather_dense(): full = lax.all_gather(packed, 'dp', axis=0, tiled=True)  42.9 us
    psum x1, waiting for transfers between devices, body(): total = lax.psum(jnp.stack(smalls), 'expert').astype(jnp.float32)  40.3 us
    all_to_all x8, waiting for transfers between devices, exchange(): lax.all_to_all(block, 'expert', split_axis=0, concat_axis=0, tiled=True)  40 us
    reduce_scatter x2, waiting for transfers between devices, layer_backward(): share_small = lax.psum_scatter(small, 'dp', scatter_dimension=0, tiled=True)  36.1 us
    all_to_all x8, starting transfers between devices, exchange(): lax.all_to_all(block, 'expert', split_axis=0, concat_axis=0, tiled=True)  33.8 us
  transfers between devices with their start and end apart: 21, of which 15 were waited for; matrix products, arithmetic and copies ran while one was open for 24% of the time, Pallas kernels for 0%

profile of v1, /device:TPU:0, one launch (start us, length us, event | category | flops | bytes accessed | tf_op | source)
XLA Modules:
  0.0 778.8 jit_solution(11909952631616538560)
XLA Ops:
  20.8 24.8 %all-gather.11.cloned.1.call-done = bf16[512,2060]{1,0:T(8,128)(2,1)} async-done(((bf16[64,2060]{1,0:T(8,128)(2,1)}), bf16[512,2060]{1,0:T(8,128)(2,1)}) %all-gather.11.cloned.1.call-update) | async-done | bytes 2109456 | tf_op jit(solution)/shard_map/all_gather | solution.py:62
  47.3 3.7 fusion.208
  62.7 3.8 all-to-all-start
  68.1 14.7 %all-to-all-done = bf16[4,2,152,512]{3,2,1,0:T(8,128)(2,1)S(1)} async-done(((bf16[4,2,152,512]{3,2,1,0:T(8,128)(2,1)}), bf16[4,2,152,512]{3,2,1,0:T(8,128)(2,1)S(1)}, u32[]{:S(2)}, u32[]{:S(2)}) %all-to-all-start) | async-done | bytes 1245216 | tf_op jit(solution)/shard_map/all_to_all | solution.py:97
  82.8 12.2 %all-gather.15.cloned.1.call-done = bf16[1,2,512,2048]{3,2,1,0:T(8,128)(2,1)} async-done(((bf16[1,2,512,256]{3,2,1,0:T(8,128)(2,1)}), bf16[1,2,512,2048]{3,2,1,0:T(8,128)(2,1)}) %all-gather.15.cloned.1.call-update) | async-done | bytes 4194320 | tf_op jit(solution)/shard_map/all_gather | solution.py:72
  95.0 8.7 %fusion.17 = (bf16[4,2,152,2048]{3,2,0,1:T(8,128)(2,1)}, f32[2,4,152,2048]{3,2,1,0:T(8,128)}) fusion(bf16[1,2,512,2048]{3,2,1,0:T(8,128)(2,1)} %all-gather.15.cloned.1.call-done, bf16[4,2,152,512]{3,2,1,0:T(8,128)(2,1)S(1)} %all-to-all-done), kind=kOutput, calls=%fused_computation.23 | convolution fusion | flops 2562588672 | bytes 20381696 | tf_op jit(solution)/shard_map/sjcd,jdf->sjcf/dot_general | solution.py:131
  103.7 38.0 %all-gather.17.cloned.1.call-done = bf16[1,2,2048,512]{3,2,1,0:T(8,128)(2,1)} async-done(((bf16[1,2,256,512]{3,2,1,0:T(8,128)(2,1)}), bf16[1,2,2048,512]{3,2,1,0:T(8,128)(2,1)}) %all-gather.17.cloned.1.call-update) | async-done | bytes 4194320 | tf_op jit(solution)/shard_map/all_gather | solution.py:73
  141.7 6.4 fusion.81
  149.3 3.6 all-to-all-start.1
  154.3 18.0 %all-gather.13.cloned.1.call-done = bf16[512,2060]{1,0:T(8,128)(2,1)} async-done(((bf16[64,2060]{1,0:T(8,128)(2,1)}), bf16[512,2060]{1,0:T(8,128)(2,1)}) %all-gather.13.cloned.1.call-update) | async-done | bytes 2109456 | tf_op jit(solution)/shard_map/all_gather | solution.py:62
  198.6 4.7 all-to-all-start.2
  203.3 18.2 %all-gather.19.cloned.1.call-done = bf16[1,2,512,2048]{3,2,1,0:T(8,128)(2,1)} async-done(((bf16[1,2,512,256]{3,2,1,0:T(8,128)(2,1)}), bf16[1,2,512,2048]{3,2,1,0:T(8,128)(2,1)}) %all-gather.19.cloned.1.call-update) | async-done | bytes 4194320 | tf_op jit(solution)/shard_map/all_gather | solution.py:72
  221.6 9.0 %fusion.13 = (bf16[4,2,152,2048]{3,2,0,1:T(8,128)(2,1)}, f32[2,4,152,2048]{3,2,1,0:T(8,128)}) fusion(bf16[1,2,512,2048]{3,2,1,0:T(8,128)(2,1)} %all-gather.19.cloned.1.call-done, bf16[4,2,152,512]{3,2,1,0:T(8,128)(2,1)} %all-to-all-done.2), kind=kOutput, calls=%fused_computation.17 | convolution fusion | flops 2562588672 | bytes 20381696 | tf_op jit(solution)/shard_map/sjcd,jdf->sjcf/dot_general | solution.py:131
  230.6 38.1 %all-gather.21.cloned.1.call-done = bf16[1,2,2048,512]{3,2,1,0:T(8,128)(2,1)} async-done(((bf16[1,2,256,512]{3,2,1,0:T(8,128)(2,1)}), bf16[1,2,2048,512]{3,2,1,0:T(8,128)(2,1)}) %all-gather.21.cloned.1.call-update) | async-done | bytes 4194320 | tf_op jit(solution)/shard_map/all_gather | solution.py:73
  268.7 6.4 fusion.87
  276.3 4.3 all-to-all-start.3
  286.0 11.0 %all-to-all-done.3 = bf16[4,2,152,512]{3,2,1,0:T(8,128)(2,1)} async-done(((bf16[4,2,152,512]{3,2,1,0:T(8,128)(2,1)}), bf16[4,2,152,512]{3,2,1,0:T(8,128)(2,1)}, u32[]{:S(2)}, u32[]{:S(2)}) %all-to-all-start.3) | async-done | bytes 1245216 | tf_op jit(solution)/shard_map/all_to_all | solution.py:97
  299.4 3.5 multiply_reduce_fusion.13
  305.9 4.3 all-to-all-start.4
  311.6 14.2 %all-to-all-done.4 = bf16[4,2,152,512]{3,2,1,0:T(8,128)(2,1)} async-done(((bf16[4,2,152,512]{3,2,1,0:T(8,128)(2,1)}), bf16[4,2,152,512]{3,2,1,0:T(8,128)(2,1)}, u32[]{:S(2)}, u32[]{:S(2)}) %all-to-all-start.4) | async-done | bytes 1245216 | tf_op jit(solution)/shard_map/all_to_all | solution.py:97
  325.9 8.7 %fusion.5 = bf16[4,2,152,2048]{3,2,0,1:T(8,128)(2,1)S(1)} fusion(f32[2,4,152,2048]{3,2,1,0:T(8,128)} %get-tuple-element.147, bf16[1,2,2048,512]{3,2,1,0:T(8,128)(2,1)} %all-gather.21.cloned.1.call-done, bf16[4,2,152,512]{3,2,1,0:T(8,128)(2,1)} %all-to-all-done.4), kind=kOutput, calls=%fused_computation.7 | convolution fusion | flops 2575040512 | bytes 20381696 | tf_op jit(solution)/shard_map/sjcd,jfd->sjcf/dot_general | solution.py:206
  334.6 2.8 fusion.84
  338.5 4.4 all-to-all-start.5
  342.9 8.2 %bitcast_convert_fusion.2 = bf16[2,512,2048]{2,1,0:T(8,128)(2,1)} fusion(bf16[4,2,152,512]{3,2,1,0:T(8,128)(2,1)} %all-to-all-done.2, bf16[4,2,152,2048]{3,2,0,1:T(8,128)(2,1)} %copy-done.106), kind=kOutput, calls=%fused_computation.28 | convolution fusion | flops 2552233984 | bytes 10420224 | tf_op jit(solution)/shard_map/sjcd,sjcf->jdf/dot_general | solution.py:217
  351.2 8.3 %bitcast_convert_fusion.3 = bf16[2,2048,512]{2,1,0:T(8,128)(2,1)} fusion(bf16[4,2,152,2048]{3,2,0,1:T(8,128)(2,1)} %get-tuple-element.146, bf16[4,2,152,512]{3,2,1,0:T(8,128)(2,1)} %all-to-all-done.4), kind=kOutput, calls=%fused_computation.29 | convolution fusion | flops 2552233984 | bytes 10420224 | tf_op jit(solution)/shard_map/sjcf,sjcd->jfd/dot_general | solution.py:214
  367.8 2.5 reshape.334
  370.2 2.4 copy.259
  382.3 3.9 multiply_reduce_fusion.3
  391.0 4.4 all-to-all-start.6
  402.7 3.9 convolution_convert_fusion
  406.6 4.8 concatenate.25
  411.4 8.7 %fusion.11 = bf16[4,2,152,2048]{3,2,0,1:T(8,128)(2,1)S(1)} fusion(f32[2,4,152,2048]{3,2,1,0:T(8,128)} %get-tuple-element.136, bf16[1,2,2048,512]{3,2,1,0:T(8,128)(2,1)} %all-gather.17.cloned.1.call-done, bf16[4,2,152,512]{3,2,1,0:T(8,128)(2,1)} %all-to-all-done.6), kind=kOutput, calls=%fused_computation.13 | convolution fusion | flops 2575040512 | bytes 20381696 | tf_op jit(solution)/shard_map/sjcd,jfd->sjcf/dot_general | solution.py:206
  420.2 2.8 fusion.78
  424.1 4.1 all-to-all-start.7
  428.3 7.5 bitcast_convert_fusion
  435.8 8.2 %bitcast_convert_fusion.1 = bf16[2,2048,512]{2,1,0:T(8,128)(2,1)} fusion(bf16[4,2,152,2048]{3,2,0,1:T(8,128)(2,1)} %get-tuple-element.135, bf16[4,2,152,512]{3,2,1,0:T(8,128)(2,1)} %all-to-all-done.6), kind=kOutput, calls=%fused_computation.27 | convolution fusion | flops 2552233984 | bytes 10420224 | tf_op jit(solution)/shard_map/sjcf,sjcd->jfd/dot_general | solution.py:214
  451.4 2.4 reshape.335
  469.2 2.8 multiply_reduce_fusion.5
  474.1 2.4 convolution_convert_fusion.1
  476.5 4.4 concatenate.24
  481.0 36.1 %reduce-scatter.7.cloned.1.call-done = bf16[64,2060]{1,0:T(8,128)(2,1)} async-done(((bf16[512,2060]{1,0:T(8,128)(2,1)}), bf16[64,2060]{1,0:T(8,128)(2,1)}) %reduce-scatter.7.cloned.1.call-update) | async-done | bytes 263696 | tf_op jit(solution)/shard_map/reduce_scatter | solution.py:284
  525.0 40.3 %all-reduce.4.cloned.1.call-done = bf16[2,64,2060]{2,1,0:T(8,128)(2,1)} async-done(((bf16[2,64,2060]{2,1,0:T(8,128)(2,1)}), bf16[2,64,2060]{2,1,0:T(8,128)(2,1)}) %all-reduce.4.cloned.1.call-update) | async-done | bytes 527376 | tf_op jit(solution)/shard_map/psum | solution.py:311
  572.0 45.4 %reduce-scatter.17.cloned.1.call-done = bf16[2,256,512]{2,1,0:T(8,128)(2,1)} async-done(((bf16[2,2048,512]{2,1,0:T(8,128)(2,1)}), bf16[2,256,512]{2,1,0:T(8,128)(2,1)}) %reduce-scatter.17.cloned.1.call-update) | async-done | bytes 524304 | tf_op jit(solution)/shard_map/reduce_scatter | solution.py:223
  617.4 50.7 %reduce-scatter.15.cloned.1.call-done = bf16[2,256,512]{2,1,0:T(8,128)(2,1)} async-done(((bf16[2,2048,512]{2,1,0:T(8,128)(2,1)}), bf16[2,256,512]{2,1,0:T(8,128)(2,1)}) %reduce-scatter.15.cloned.1.call-update) | async-done | bytes 524304 | tf_op jit(solution)/shard_map/reduce_scatter | solution.py:223
  668.1 2.7 maximum_convert_fusion.1
  670.8 47.9 %reduce-scatter.13.cloned.1.call-done = bf16[2,512,256]{2,1,0:T(8,128)(2,1)} async-done(((bf16[2,512,2048]{2,1,0:T(8,128)(2,1)}), bf16[2,512,256]{2,1,0:T(8,128)(2,1)}) %reduce-scatter.13.cloned.1.call-update) | async-done | bytes 524304 | tf_op jit(solution)/shard_map/reduce_scatter | solution.py:224
  718.7 50.7 %reduce-scatter.11.cloned.1.call-done = bf16[2,512,256]{2,1,0:T(8,128)(2,1)} async-done(((bf16[2,512,2048]{2,1,0:T(8,128)(2,1)}), bf16[2,512,256]{2,1,0:T(8,128)(2,1)}) %reduce-scatter.11.cloned.1.call-update) | async-done | bytes 524304 | tf_op jit(solution)/shard_map/reduce_scatter | solution.py:224
  769.4 2.7 maximum_convert_fusion
  (439 shorter events, 140.6 us)
Async XLA Ops:
  7.2 38.5 %all-gather.11.cloned.1.call-start = ((), (), s32[]{:S(2)}) async-start(), calls=%async_computation.14 | async-start | bytes 2506752 | tf_op jit(solution)/shard_map/all_gather | solution.py:62
  12.5 82.5 %all-gather.15.cloned.1.call-start = ((), (), s32[]{:S(2)}) async-start(), calls=%async_computation.23 | async-start | bytes 4718592 | tf_op jit(solution)/shard_map/all_gather | solution.py:72
  13.7 128.1 %all-gather.17.cloned.1.call-start = ((), (), s32[]{:S(2)}) async-start(), calls=%async_computation.24 | async-start | bytes 4718592 | tf_op jit(solution)/shard_map/all_gather | solution.py:73
  14.8 157.6 %all-gather.13.cloned.1.call-start = ((), (), s32[]{:S(2)}) async-start(), calls=%async_computation.15 | async-start | bytes 2506752 | tf_op jit(solution)/shard_map/all_gather | solution.py:62
  16.0 205.6 %all-gather.19.cloned.1.call-start = ((), (), s32[]{:S(2)}) async-start(), calls=%async_computation.25 | async-start | bytes 4718592 | tf_op jit(solution)/shard_map/all_gather | solution.py:72
  16.6 252.1 %all-gather.21.cloned.1.call-start = ((), (), s32[]{:S(2)}) async-start(), calls=%async_computation.26 | async-start | bytes 4718592 | tf_op jit(solution)/shard_map/all_gather | solution.py:73
  18.7 291.5 %copy-start.60 = (s32[394,1]{0,1:T(1,128)}, s32[394,1]{0,1:T(1,128)S(1)}, u32[]{:S(2)}) copy-start(s32[394,1]{0,1:T(1,128)S(1)} %get-tuple-element.119) | copy-start | bytes 4732
  18.7 291.5 %copy-start.62 = (s32[394,1]{0,1:T(1,128)}, s32[394,1]{0,1:T(1,128)S(1)}, u32[]{:S(2)}) copy-start(s32[394,1]{0,1:T(1,128)S(1)} %get-tuple-element.120) | copy-start | bytes 4732
  18.8 135.4 %copy-start.56 = (s32[394,1]{0,1:T(1,128)}, s32[394,1]{0,1:T(1,128)S(1)}, u32[]{:S(2)}) copy-start(s32[394,1]{0,1:T(1,128)S(1)} %get-tuple-element.123) | copy-start | bytes 4732
  18.8 135.4 %copy-start.58 = (s32[394,1]{0,1:T(1,128)}, s32[394,1]{0,1:T(1,128)S(1)}, u32[]{:S(2)}) copy-start(s32[394,1]{0,1:T(1,128)S(1)} %get-tuple-element.124) | copy-start | bytes 4732
  20.5 30.6 %copy-start.83 = (f32[394]{0:T(512)}, f32[394]{0:T(512)S(1)}, u32[]{:S(2)}) copy-start(f32[394]{0:T(512)S(1)} %div.83) | copy-start | bytes 4732
  20.7 30.4 %copy-start.85 = (f32[394]{0:T(512)}, f32[394]{0:T(512)S(1)}, u32[]{:S(2)}) copy-start(f32[394]{0:T(512)S(1)} %rsqrt.36) | copy-start | bytes 4732
  20.8 37.8 %copy-start.12 = (f32[394,512]{1,0:T(8,128)}, f32[394,512]{1,0:T(8,128)S(1)}, u32[]{:S(2)}) copy-start(f32[394,512]{1,0:T(8,128)S(1)} %reshape.314) | copy-start | bytes 2420740
  20.8 153.3 %copy-start.100 = (s32[394]{0:T(512)}, s32[394]{0:T(512)S(1)}, u32[]{:S(2)}) copy-start(s32[394]{0:T(512)S(1)} %get-tuple-element.162) | copy-start | bytes 4732
  20.8 154.3 %copy-start.96 = (s32[394]{0:T(512)}, s32[394]{0:T(512)S(1)}, u32[]{:S(2)}) copy-start(s32[394]{0:T(512)S(1)} %get-tuple-element.161) | copy-start | bytes 4732
  47.3 13.3 %copy-start.75 = (f32[512]{0:T(512)}, f32[512]{0:T(512)S(1)}, u32[]{:S(2)}) copy-start(f32[512]{0:T(512)S(1)} %get-tuple-element.160) | copy-start | bytes 6148
  60.3 114.8 %copy-start.2 = (f32[394,512]{1,0:T(8,128)}, f32[394,512]{1,0:T(8,128)S(1)}, u32[]{:S(2)}) copy-start(f32[394,512]{1,0:T(8,128)S(1)} %get-tuple-element.134) | copy-start | bytes 2420740
  60.8 92.2 %copy-start.30 = (bf16[394,512]{1,0:T(8,128)(2,1)}, bf16[394,512]{1,0:T(8,128)(2,1)S(1)}, u32[]{:S(2)}) copy-start(bf16[394,512]{1,0:T(8,128)(2,1)S(1)} %add_convert_fusion.3) | copy-start | bytes 1210372
  62.7 20.1 %all-to-all-start = ((bf16[4,2,152,512]{3,2,1,0:T(8,128)(2,1)}), bf16[4,2,152,512]{3,2,1,0:T(8,128)(2,1)S(1)}, u32[]{:S(2)}, u32[]{:S(2)}) async-start(bf16[4,2,152,512]{3,2,1,0:T(8,128)(2,1)} %bitcast.263), calls=%async_computation | async-start | bytes 2490368 | tf_op jit(solution)/shard_map/all_to_all | solution.py:97
  82.8 20.9 %copy-start.47 = (bf16[4,2,152,512]{3,2,1,0:T(8,128)(2,1)}, bf16[4,2,152,512]{3,2,1,0:T(8,128)(2,1)S(1)}, u32[]{:S(2)}) copy-start(bf16[4,2,152,512]{3,2,1,0:T(8,128)(2,1)S(1)} %all-to-all-done) | copy-start | bytes 3735556
  149.3 24.7 %all-to-all-start.1 = ((bf16[4,2,152,512]{3,2,1,0:T(8,128)(2,1)}), bf16[4,2,152,512]{3,2,1,0:T(8,128)(2,1)S(1)}, u32[]{:S(2)}, u32[]{:S(2)}) async-start(bf16[4,2,152,512]{3,2,1,0:T(8,128)(2,1)} %copy.238), calls=%async_computation.1 | async-start | bytes 2490368 | tf_op jit(solution)/shard_map/all_to_all | solution.py:97
  154.2 20.9 %copy-start.64 = (f32[394]{0:T(512)}, f32[394]{0:T(512)S(1)}, u32[]{:S(2)}) copy-start(f32[394]{0:T(512)S(1)} %get-tuple-element.137) | copy-start | bytes 4732
  154.2 20.9 %copy-start.68 = (f32[394]{0:T(512)}, f32[394]{0:T(512)S(1)}, u32[]{:S(2)}) copy-start(f32[394]{0:T(512)S(1)} %fusion.197) | copy-start | bytes 4732
  154.3 20.9 %copy-start.92 = (f32[394]{0:T(512)}, f32[394]{0:T(512)S(1)}, u32[]{:S(2)}) copy-start(f32[394]{0:T(512)S(1)} %get-tuple-element.91) | copy-start | bytes 4732
  154.3 20.9 %copy-start.94 = (f32[394]{0:T(512)}, f32[394]{0:T(512)S(1)}, u32[]{:S(2)}) copy-start(f32[394]{0:T(512)S(1)} %get-tuple-element.90) | copy-start | bytes 4732
  173.7 208.4 %copy-start.79 = (f32[512]{0:T(512)}, f32[512]{0:T(512)S(1)}, u32[]{:S(2)}) copy-start(f32[512]{0:T(512)S(1)} %get-tuple-element.78) | copy-start | bytes 6148
  177.2 205.0 %copy-start.72 = (f32[394]{0:T(512)}, f32[394]{0:T(512)S(1)}, u32[]{:S(2)}) copy-start(f32[394]{0:T(512)S(1)} %broadcast_multiply_fusion.10) | copy-start | bytes 4732
  177.4 204.8 %copy-start.80 = (f32[394]{0:T(512)}, f32[394]{0:T(512)S(1)}, u32[]{:S(2)}) copy-start(f32[394]{0:T(512)S(1)} %add_rsqrt_fusion.2) | copy-start | bytes 4732
  198.6 22.9 %all-to-all-start.2 = ((bf16[4,2,152,512]{3,2,1,0:T(8,128)(2,1)}), bf16[4,2,152,512]{3,2,1,0:T(8,128)(2,1)}, u32[]{:S(2)}, u32[]{:S(2)}) async-start(bf16[4,2,152,512]{3,2,1,0:T(8,128)(2,1)} %bitcast.266), calls=%async_computation.2 | async-start | bytes 2490368 | tf_op jit(solution)/shard_map/all_to_all | solution.py:97
  276.3 20.8 %all-to-all-start.3 = ((bf16[4,2,152,512]{3,2,1,0:T(8,128)(2,1)}), bf16[4,2,152,512]{3,2,1,0:T(8,128)(2,1)}, u32[]{:S(2)}, u32[]{:S(2)}) async-start(bf16[4,2,152,512]{3,2,1,0:T(8,128)(2,1)} %copy.252), calls=%async_computation.3 | async-start | bytes 2490368 | tf_op jit(solution)/shard_map/all_to_all | solution.py:97
  305.9 20.0 %all-to-all-start.4 = ((bf16[4,2,152,512]{3,2,1,0:T(8,128)(2,1)}), bf16[4,2,152,512]{3,2,1,0:T(8,128)(2,1)}, u32[]{:S(2)}, u32[]{:S(2)}) async-start(bf16[4,2,152,512]{3,2,1,0:T(8,128)(2,1)} %bitcast.265), calls=%async_computation.4 | async-start | bytes 2490368 | tf_op jit(solution)/shard_map/all_to_all | solution.py:97
  325.9 8.7 %copy-start.104 = (bf16[1,2,512,2048]{3,2,1,0:T(8,128)(2,1)S(1)}, bf16[1,2,512,2048]{3,2,1,0:T(8,128)(2,1)}, u32[]{:S(2)}) copy-start(bf16[1,2,512,2048]{3,2,1,0:T(8,128)(2,1)} %all-gather.19.cloned.1.call-done) | copy-start | bytes 12582916
  338.5 21.0 %all-to-all-start.5 = ((bf16[4,2,152,512]{3,2,1,0:T(8,128)(2,1)}), bf16[4,2,152,512]{3,2,1,0:T(8,128)(2,1)}, u32[]{:S(2)}, u32[]{:S(2)}) async-start(bf16[4,2,152,512]{3,2,1,0:T(8,128)(2,1)} %copy.255), calls=%async_computation.5 | async-start | bytes 2490368 | tf_op jit(solution)/shard_map/all_to_all | solution.py:97
  389.1 7.8 copy-start.31
  391.0 10.4 %copy-start.21 = (bf16[394,512]{0,1:T(8,128)(2,1)S(1)}, bf16[394,512]{0,1:T(8,128)(2,1)}, u32[]{:S(2)}) copy-start(bf16[394,512]{0,1:T(8,128)(2,1)} %convert_element_type.338) | copy-start | bytes 1210372
  391.0 20.4 %all-to-all-start.6 = ((bf16[4,2,152,512]{3,2,1,0:T(8,128)(2,1)}), bf16[4,2,152,512]{3,2,1,0:T(8,128)(2,1)}, u32[]{:S(2)}, u32[]{:S(2)}) async-start(bf16[4,2,152,512]{3,2,1,0:T(8,128)(2,1)} %bitcast.262), calls=%async_computation.6 | async-start | bytes 2490368 | tf_op jit(solution)/shard_map/all_to_all | solution.py:97
  395.5 85.6 %reduce-scatter.9.cloned.1.call-start = ((), (), s32[]{:S(2)}) async-start(), calls=%async_computation.17 | async-start | bytes 2506752 | tf_op jit(solution)/shard_map/reduce_scatter | solution.py:284
  411.4 8.7 %copy-start.103 = (bf16[1,2,512,2048]{3,2,1,0:T(8,128)(2,1)S(1)}, bf16[1,2,512,2048]{3,2,1,0:T(8,128)(2,1)}, u32[]{:S(2)}) copy-start(bf16[1,2,512,2048]{3,2,1,0:T(8,128)(2,1)} %all-gather.15.cloned.1.call-done) | copy-start | bytes 12582916
  424.1 19.9 %all-to-all-start.7 = ((bf16[4,2,152,512]{3,2,1,0:T(8,128)(2,1)}), bf16[4,2,152,512]{3,2,1,0:T(8,128)(2,1)S(1)}, u32[]{:S(2)}, u32[]{:S(2)}) async-start(bf16[4,2,152,512]{3,2,1,0:T(8,128)(2,1)} %copy.271), calls=%async_computation.7 | async-start | bytes 2490368 | tf_op jit(solution)/shard_map/all_to_all | solution.py:97
  428.3 88.8 %reduce-scatter.7.cloned.1.call-start = ((), (), s32[]{:S(2)}) async-start(), calls=%async_computation.16 | async-start | bytes 2506752 | tf_op jit(solution)/shard_map/reduce_scatter | solution.py:284
  435.8 8.2 %copy-start.98 = (s32[394]{0:T(512)S(1)}, s32[394]{0:T(512)}, u32[]{:S(2)}) copy-start(s32[394]{0:T(512)} %copy-done.96) | copy-start | bytes 4732
  435.8 8.2 %copy-start.102 = (s32[394]{0:T(512)S(1)}, s32[394]{0:T(512)}, u32[]{:S(2)}) copy-start(s32[394]{0:T(512)} %copy-done.100) | copy-start | bytes 4732
  449.0 7.2 copy-start.1
  481.0 84.4 %all-reduce.4.cloned.1.call-start = ((), (), s32[]{:S(2)}) async-start(), calls=%async_computation.18 | async-start | bytes 1114112 | tf_op jit(solution)/shard_map/psum | solution.py:311
  519.1 98.4 %reduce-scatter.17.cloned.1.call-start = ((), (), s32[]{:S(2)}) async-start(), calls=%async_computation.22 | async-start | bytes 4718592 | tf_op jit(solution)/shard_map/reduce_scatter | solution.py:223
  519.6 148.5 %reduce-scatter.15.cloned.1.call-start = ((), (), s32[]{:S(2)}) async-start(), calls=%async_computation.21 | async-start | bytes 4718592 | tf_op jit(solution)/shard_map/reduce_scatter | solution.py:223
  520.4 198.3 %reduce-scatter.13.cloned.1.call-start = ((), (), s32[]{:S(2)}) async-start(), calls=%async_computation.20 | async-start | bytes 4718592 | tf_op jit(solution)/shard_map/reduce_scatter | solution.py:224
  521.0 248.5 %reduce-scatter.11.cloned.1.call-start = ((), (), s32[]{:S(2)}) async-start(), calls=%async_computation.19 | async-start | bytes 4718592 | tf_op jit(solution)/shard_map/reduce_scatter | solution.py:224
  (80 other events, 185.9 us)
Sparse Core Ops, SparseCore 0:
  12.7 32.9 all-gather.10
  47.8 47.1 all-gather.14
  96.7 45.0 all-gather.16
  143.2 29.0 all-gather.12
  174.3 47.1 all-gather.18
  223.6 45.0 all-gather.20
  411.5 35.9 reduce-scatter.8
  481.1 35.9 reduce-scatter.6
  520.7 44.5 all-reduce.3
  567.5 49.8 reduce-scatter.16
  619.7 48.3 reduce-scatter.14
  670.3 48.3 reduce-scatter.12
  721.0 48.3 reduce-scatter.10

commit v2 on v1

--- a/solution.py
+++ b/solution.py
@@ -97,10 +97,9 @@
     return lax.all_to_all(block, "expert", split_axis=0, concat_axis=0, tiled=True)
 
 
-def layer_forward(resid, dense, experts, tables):
+def attend_forward(resid, dense, tables):
     qkv_full, proj_full, router_full, gains_wide, shifts_wide = dense
-    first_full, second_full = experts
-    pick_first_f, pick_second_f, place_first, place_second = tables
+    pick_first_f, pick_second_f, _, _ = tables
     tok_count, width = resid.shape
     images = tok_count // SEQ
     attn_norm, unit_a, inv_a = layer_norm(resid, gains_wide[0], shifts_wide[0])
@@ -121,88 +120,55 @@
     moe_in = moe_norm.astype(jnp.bfloat16)
     logits = jnp.dot(moe_in, router_full, preferred_element_type=jnp.float32)
     router_probs, _ = softmax_rows(logits)
-    experts_total = router_full.shape[1]
-    local_count = first_full.shape[0]
-    peers = lax.axis_size("expert")
-    capacity = place_first.shape[0] // experts_total
-    outgoing = jnp.dot(place_first + place_second, moe_in, preferred_element_type=jnp.float32)
-    outgoing = outgoing.astype(jnp.bfloat16).reshape(peers, local_count, capacity, width)
-    incoming = exchange(outgoing)
+    gate_first = jnp.sum(router_probs * pick_first_f, axis=1)
+    gate_second = jnp.sum(router_probs * pick_second_f, axis=1)
+    router_probs, gate_first, gate_second = lax.optimization_barrier(
+        (router_probs, gate_first, gate_second)
+    )
+    attn_saved = (unit_a, inv_a, attn_in, query, keyed, valued, log_total, mixed)
+    moe_saved = (unit_b, inv_b, moe_in, router_probs, gate_first, gate_second)
+    return (resid_mid, attn_saved, moe_saved)
+
+
+def slots_of(rows, place, block_shape):
+    slots = jnp.dot(place, rows, preferred_element_type=jnp.float32)
+    return slots.astype(jnp.bfloat16).reshape(block_shape)
+
+
+def gated_slots(grad_out, moe_saved, tables, block_shape):
+    gate_first, gate_second = moe_saved[4:]
+    place_first, place_second = tables[2:]
+    send_first = (gate_first[:, None] * grad_out).astype(jnp.bfloat16)
+    send_second = (gate_second[:, None] * grad_out).astype(jnp.bfloat16)
+    slots = jnp.dot(place_first, send_first, preferred_element_type=jnp.float32) + jnp.dot(
+        place_second, send_second, preferred_element_type=jnp.float32
+    )
+    return slots.astype(jnp.bfloat16).reshape(block_shape)
+
+
+def experts_hidden(incoming, first_full):
     hidden_pre = jnp.einsum(
         "sjcd,jdf->sjcf", incoming, first_full, preferred_element_type=jnp.float32
     )
-    hidden_act = gelu_value(hidden_pre).astype(jnp.bfloat16)
-    result = jnp.einsum(
+    return (hidden_pre, gelu_value(hidden_pre).astype(jnp.bfloat16))
+
+
+def experts_result(hidden_act, second_full):
+    return jnp.einsum(
         "sjcf,jfd->sjcd", hidden_act, second_full, preferred_element_type=jnp.float32
     ).astype(jnp.bfloat16)
-    returned = exchange(result).reshape(experts_total * capacity, width)
-    gate_first = jnp.sum(router_probs * pick_first_f, axis=1)
-    gate_second = jnp.sum(router_probs * pick_second_f, axis=1)
-    back_first = jnp.einsum("st,sd->td", place_first, returned, preferred_element_type=jnp.float32)
-    back_second = jnp.einsum(
-        "st,sd->td", place_second, returned, preferred_element_type=jnp.float32
-    )
-    resid_out = resid_mid + (gate_first[:, None] * back_first + gate_second[:, None] * back_second)
-    saved = (
-        unit_a,
-        inv_a,
-        attn_in,
-        query,
-        keyed,
-        valued,
-        log_total,
-        mixed,
-        unit_b,
-        inv_b,
-        moe_in,
-        router_probs,
-        incoming,
-        hidden_pre,
-        hidden_act,
-        back_first,
-        back_second,
-        gate_first,
-        gate_second,
-    )
-    return (resid_out, saved)
-
-
-def layer_backward(grad_out, dense, experts, tables, saved):
-    qkv_full, proj_full, router_full, gains_wide, _ = dense
+
+
+def rows_back(returned, place):
+    return jnp.einsum("st,sd->td", place, returned, preferred_element_type=jnp.float32)
+
+
+def experts_backward(grad_result, incoming, hidden_pre, hidden_act, experts):
     first_full, second_full = experts
-    pick_first_f, pick_second_f, place_first, place_second = tables
-    (
-        unit_a,
-        inv_a,
-        attn_in,
-        query,
-        keyed,
-        valued,
-        log_total,
-        mixed,
-        unit_b,
-        inv_b,
-        moe_in,
-        router_probs,
-        incoming,
-        hidden_pre,
-        hidden_act,
-        back_first,
-        back_second,
-        gate_first,
-        gate_second,
-    ) = saved
-    tok_count, width = grad_out.shape
-    images = tok_count // SEQ
-    send_first = (gate_first[:, None] * grad_out).astype(jnp.bfloat16)
-    send_second = (gate_second[:, None] * grad_out).astype(jnp.bfloat16)
-    slot_grads = jnp.dot(place_first, send_first, preferred_element_type=jnp.float32) + jnp.dot(
-        place_second, send_second, preferred_element_type=jnp.float32
-    )
-    slot_grads = slot_grads.astype(jnp.bfloat16).reshape(incoming.shape)
-    grad_result = exchange(slot_grads)
-    grad_gate_first = jnp.sum(grad_out * back_first, axis=1)
-    grad_gate_second = jnp.sum(grad_out * back_second, axis=1)
+    grad_second = jnp.einsum(
+        "sjcf,sjcd->jfd", hidden_act, grad_result, preferred_element_type=jnp.float32
+    ).astype(jnp.bfloat16)
+    share_second = lax.psum_scatter(grad_second, "dp", scatter_dimension=1, tiled=True)
     grad_act = jnp.einsum(
         "sjcd,jfd->sjcf", grad_result, second_full, preferred_element_type=jnp.float32
     )
@@ -211,21 +177,25 @@
         "sjcf,jdf->sjcd", grad_pre, first_full, preferred_element_type=jnp.float32
     ).astype(jnp.bfloat16)
     grad_back = exchange(grad_rows)
-    grad_second = jnp.einsum(
-        "sjcf,sjcd->jfd", hidden_act, grad_result, preferred_element_type=jnp.float32
-    ).astype(jnp.bfloat16)
     grad_first = jnp.einsum(
         "sjcd,sjcf->jdf", incoming, grad_pre, preferred_element_type=jnp.float32
     ).astype(jnp.bfloat16)
-    grad_back, grad_second, grad_first = lax.optimization_barrier(
-        (grad_back, grad_second, grad_first)
-    )
-    share_second = lax.psum_scatter(grad_second, "dp", scatter_dimension=1, tiled=True)
+    grad_back, grad_first = lax.optimization_barrier((grad_back, grad_first))
     share_first = lax.psum_scatter(grad_first, "dp", scatter_dimension=2, tiled=True)
+    return (grad_back, share_first, share_second)
+
+
+def tokens_backward(grad_out, grad_back, backs, dense, tables, attn_saved, moe_saved):
+    qkv_full, proj_full, router_full, gains_wide, _ = dense
+    pick_first_f, pick_second_f, place_first, place_second = tables
+    unit_a, inv_a, attn_in, query, keyed, valued, log_total, mixed = attn_saved
+    unit_b, inv_b, moe_in, router_probs, _, _ = moe_saved
+    tok_count, width = grad_out.shape
+    images = tok_count // SEQ
+    grad_gate_first = jnp.sum(grad_out * backs[0], axis=1)
+    grad_gate_second = jnp.sum(grad_out * backs[1], axis=1)
     grad_back = grad_back.reshape(-1, width)
-    grad_moe = jnp.einsum(
-        "st,sd->td", place_first + place_second, grad_back, preferred_element_type=jnp.float32
-    )
+    grad_moe = rows_back(grad_back, place_first + place_second)
     grad_probs = pick_first_f * grad_gate_first[:, None] + pick_second_f * grad_gate_second[:, None]
     weighted = jnp.sum(router_probs * grad_probs, axis=1, keepdims=True)
     grad_logits = (router_probs * (grad_probs - weighted)).astype(jnp.bfloat16)
@@ -281,34 +251,74 @@
         ],
         axis=1,
     )
-    share_small = lax.psum_scatter(small, "dp", scatter_dimension=0, tiled=True)
-    return (grad_in, share_small, share_first, share_second)
-
-
-def body(
+    peers, shares = lax.axis_size("expert"), lax.axis_size("dp")
+    piece = width // (peers * shares)
+    columns = small.shape[1]
+    small = small.reshape(shares, peers, piece, columns).swapaxes(0, 1)
+    small = exchange(small)
+    small = jnp.sum(small.astype(jnp.float32), axis=0).astype(low)
+    return (grad_in, small)
+
+
+def whole_step(
     embedded, cotangent, w_qkv, w_proj, w_router, norm_gains, norm_shifts, w_first, w_second, routes
 ):
     images, length, width = embedded.shape
     tok_count = images * length
     experts_total = w_router.shape[2]
+    peers = lax.axis_size("expert")
     capacity = -(-max(2, 3 * tok_count // experts_total) // 8) * 8
+    block_shape = (peers, experts_total // peers, capacity, width)
     resid = embedded.reshape(tok_count, width).astype(jnp.float32)
-    dense, experts, tables, saved = [], [], [], []
+    grad = cotangent.reshape(tok_count, width).astype(jnp.float32)
+    dense, experts, tables = [], [], []
     for which in range(LAYERS):
         dense.append(gather_dense(which, w_qkv, w_proj, w_router, norm_gains, norm_shifts))
         experts.append(gather_experts(which, w_first, w_second))
+    attn_saved, moe_saved, kept = [], [], []
+    grad_result = None
     for which in range(LAYERS):
-        tables.append(route_tables(routes[which].reshape(tok_count, 2), experts_total, capacity))
-        resid, kept = layer_forward(resid, dense[which], experts[which], tables[which])
-        saved.append(kept)
+        table = route_tables(routes[which].reshape(tok_count, 2), experts_total, capacity)
+        tables.append(table)
+        resid_mid, attn_part, moe_part = attend_forward(resid, dense[which], table)
+        outgoing = slots_of(moe_part[2], table[2] + table[3], block_shape)
+        incoming = exchange(outgoing)
+        if which == LAYERS - 1:
+            slots = gated_slots(grad, moe_part, table, block_shape)
+            grad_result = exchange(slots)
+        hidden_pre, hidden_act = experts_hidden(incoming, experts[which][0])
+        result = experts_result(hidden_act, experts[which][1])
+        returned = exchange(result).reshape(experts_total * capacity, width)
+        backs = (rows_back(returned, table[2]), rows_back(returned, table[3]))
+        resid = resid_mid + (
+            moe_part[4][:, None] * backs[0] + moe_part[5][:, None] * backs[1]
+        )
+        attn_saved.append(attn_part)
+        moe_saved.append(moe_part)
+        kept.append((incoming, hidden_pre, hidden_act, backs))
     out_images = resid.reshape(images, length, width).astype(jnp.bfloat16)
-    grad = cotangent.reshape(tok_count, width).astype(jnp.float32)
     smalls, firsts, seconds = [None] * LAYERS, [None] * LAYERS, [None] * LAYERS
     for which in reversed(range(LAYERS)):
-        grad, smalls[which], firsts[which], seconds[which] = layer_backward(
-            grad, dense[which], experts[which], tables[which], saved[which]
+        incoming, hidden_pre, hidden_act, backs = kept[which]
+        if which < LAYERS - 1:
+            slots = gated_slots(grad, moe_saved[which], tables[which], block_shape)
+            grad_result = exchange(slots)
+        grad_back, firsts[which], seconds[which] = experts_backward(
+            grad_result, incoming, hidden_pre, hidden_act, experts[which]
         )
-    total = lax.psum(jnp.stack(smalls), "expert").astype(jnp.float32)
+        grad, smalls[which] = tokens_backward(
+            grad,
+            grad_back,
+            backs,
+            dense[which],
+            tables[which],
+            attn_saved[which],
+            moe_saved[which],
+        )
+    both = jnp.stack(smalls, axis=2)
+    both = lax.psum_scatter(both, "dp", scatter_dimension=0, tiled=True)[0]
+    total = lax.all_gather(both, "expert", axis=0, tiled=True)
+    total = total.swapaxes(0, 1).astype(jnp.float32)
     grad_images = grad.reshape(images, length, width)
     wide = total[:, :, 4 * width :]
     return (
@@ -325,8 +335,9 @@
 
 
 def solution(mesh):
+
     return jax.shard_map(
-        body,
+        whole_step,
         mesh=mesh,
         in_specs=(
             P(("dp", "expert"), None, None),

time: 789 us -> 759 us (0.962)
  waiting for transfers between devices: 464 us -> 354 us
  local copies, waits for them, and re-layouts: 84.7 us -> 121 us
  starting transfers between devices: 34.3 us -> 53.8 us
  blocking collectives: 0 us -> 10.3 us
  matrix products: 156 us -> 166 us
    psum x1 -> x0, waiting for transfers between devices: 40.3 us -> none  [body(): total = lax.psum(jnp.stack(smalls), 'expert').astype(jnp.float32)]
    reduce_scatter x6 -> x5, waiting for transfers between devices: 231 us -> 194 us  [the longest x2 98.6 us: experts_backward(): lax.psum_scatter(grad_first, 'dp', scatter_dimension=2, tiled=True)]
    all_gather x2, waiting for transfers between devices: 30.5 us -> 2.19 us  [gather_experts(): first_full = lax.all_gather(w_first[which], 'dp', axis=2, tiled=True)]
    all_gather x2, waiting for transfers between devices: 76.1 us -> 50.1 us  [gather_experts(): second_full = lax.all_gather(w_second[which], 'dp', axis=1, tiled=True)]
    reshape x24 -> x26, local copies, waits for them, and re-layouts: 22.4 us -> 46.3 us  [the longest x4 9.27 us: tokens_backward(): grad_mixed.astype(jnp.bfloat16).reshape(images, SEQ, HEADS, HEAD_DIM)]
    all_to_all x8 -> x10, waiting for transfers between devices: 40 us -> 63 us  [exchange(): lax.all_to_all(block, 'expert', split_axis=0, concat_axis=0, tiled=True)]
    all_to_all x8 -> x10, starting transfers between devices: 33.8 us -> 53.1 us  [exchange(): lax.all_to_all(block, 'expert', split_axis=0, concat_axis=0, tiled=True)]
    all_gather x0 -> x1, blocking collectives: none -> 10.3 us  [whole_step(): total = lax.all_gather(both, 'expert', axis=0, tiled=True)]
  transfers between devices with their start and end apart: 21 -> 21, of which waited for: 15 -> 15; matrix products, arithmetic and copies ran while one was open for 24% -> 32% of each run, Pallas kernels for 0% -> 0%
where the time goes in v2:
time: 759 us; the launch traced here: 747 us
  waiting for transfers between devices  354 us (47%)
  matrix products  166 us (22%)
  local copies, waits for them, and re-layouts  121 us (16%)
  starting transfers between devices  53.8 us (7%)
  other arithmetic  26.9 us (4%)
  between operations  15.8 us (2%)
  blocking collectives  10.3 us (1%)
    reduce_scatter x2, waiting for transfers between devices, experts_backward(): lax.psum_scatter(grad_first, 'dp', scatter_dimension=2, tiled=True)  98.6 us
    reduce_scatter x2, waiting for transfers between devices, experts_backward(): lax.psum_scatter(grad_second, 'dp', scatter_dimension=1, tiled=True)  85.3 us
    all_to_all x10, waiting for transfers between devices, exchange(): lax.all_to_all(block, 'expert', split_axis=0, concat_axis=0, tiled=True)  63 us
    all_to_all x10, starting transfers between devices, exchange(): lax.all_to_all(block, 'expert', split_axis=0, concat_axis=0, tiled=True)  53.1 us
    all_gather x2, waiting for transfers between devices, gather_experts(): second_full = lax.all_gather(w_second[which], 'dp', axis=1, tiled=True)  50.1 us
    all_gather x2, waiting for transfers between devices, gather_dense(): full = lax.all_gather(packed, 'dp', axis=0, tiled=True)  42.3 us
    unnamed x167, local copies, waits for them, and re-layouts  19.1 us
    dot_general x2, matrix products, experts_hidden(): jnp.einsum('sjcd,jdf->sjcf', incoming, first_full, preferred_element_type...  18.1 us
  transfers between devices with their start and end apart: 21, of which 15 were waited for; matrix products, arithmetic and copies ran while one was open for 32% of the time, Pallas kernels for 0%

profile of v2, /device:TPU:0, one launch (start us, length us, event | category | flops | bytes accessed | tf_op | source)
XLA Modules:
  0.0 747.1 jit_solution(16665770765900609418)
XLA Ops:
  22.0 23.6 %all-gather.12.cloned.1.call-done = bf16[512,2060]{1,0:T(8,128)(2,1)} async-done(((bf16[64,2060]{1,0:T(8,128)(2,1)}), bf16[512,2060]{1,0:T(8,128)(2,1)}) %all-gather.12.cloned.1.call-update) | async-done | bytes 2109456 | tf_op jit(solution)/shard_map/all_gather | solution.py:62
  71.9 4.5 all-to-all-start
  82.3 10.7 %all-to-all-done = bf16[4,2,152,512]{3,2,1,0:T(8,128)(2,1)} async-done(((bf16[4,2,152,512]{3,2,1,0:T(8,128)(2,1)}), bf16[4,2,152,512]{3,2,1,0:T(8,128)(2,1)}, u32[]{:S(2)}, u32[]{:S(2)}) %all-to-all-start) | async-done | bytes 1245216 | tf_op jit(solution)/shard_map/all_to_all | solution.py:97
  95.1 9.1 %fusion.17 = (bf16[4,2,152,2048]{3,2,0,1:T(8,128)(2,1)}, f32[2,4,152,2048]{3,2,1,0:T(8,128)}) fusion(bf16[1,2,512,2048]{3,2,1,0:T(8,128)(2,1)} %all-gather.16.cloned.1.call-done, bf16[4,2,152,512]{3,2,1,0:T(8,128)(2,1)} %all-to-all-done), kind=kOutput, calls=%fused_computation.23 | convolution fusion | flops 2562588672 | bytes 20381696 | tf_op jit(solution)/shard_map/sjcd,jdf->sjcf/dot_general | solution.py:150
  104.2 37.6 %all-gather.18.cloned.1.call-done = bf16[1,2,2048,512]{3,2,1,0:T(8,128)(2,1)} async-done(((bf16[1,2,256,512]{3,2,1,0:T(8,128)(2,1)}), bf16[1,2,2048,512]{3,2,1,0:T(8,128)(2,1)}) %all-gather.18.cloned.1.call-update) | async-done | bytes 4194320 | tf_op jit(solution)/shard_map/all_gather | solution.py:73
  141.8 6.4 fusion.81
  149.4 4.3 all-to-all-start.1
  153.7 18.7 %all-gather.14.cloned.1.call-done = bf16[512,2060]{1,0:T(8,128)(2,1)} async-done(((bf16[64,2060]{1,0:T(8,128)(2,1)}), bf16[512,2060]{1,0:T(8,128)(2,1)}) %all-gather.14.cloned.1.call-update) | async-done | bytes 2109456 | tf_op jit(solution)/shard_map/all_gather | solution.py:62
  176.6 3.6 fusion.201
  213.1 13.1 %all-to-all-start.2 = ((bf16[4,2,152,512]{3,2,1,0:T(8,128)(2,1)}), bf16[4,2,152,512]{3,2,1,0:T(8,128)(2,1)}, u32[]{:S(2)}, u32[]{:S(2)}) async-start(bf16[4,2,152,512]{3,2,1,0:T(8,128)(2,1)} %bitcast.290), calls=%async_computation.2 | async-start | bytes 2490368 | tf_op jit(solution)/shard_map/all_to_all | solution.py:97
  231.7 10.7 %all-to-all-done.2 = bf16[4,2,152,512]{3,2,1,0:T(8,128)(2,1)} async-done(((bf16[4,2,152,512]{3,2,1,0:T(8,128)(2,1)}), bf16[4,2,152,512]{3,2,1,0:T(8,128)(2,1)}, u32[]{:S(2)}, u32[]{:S(2)}) %all-to-all-start.2) | async-done | bytes 1245216 | tf_op jit(solution)/shard_map/all_to_all | solution.py:97
  242.4 4.3 all-to-all-start.4
  246.7 9.1 %fusion.13 = (bf16[4,2,152,2048]{3,2,0,1:T(8,128)(2,1)}, f32[2,4,152,2048]{3,2,1,0:T(8,128)}) fusion(bf16[1,2,512,2048]{3,2,1,0:T(8,128)(2,1)} %all-gather.20.cloned.1.call-done, bf16[4,2,152,512]{3,2,1,0:T(8,128)(2,1)} %all-to-all-done.2), kind=kOutput, calls=%fused_computation.17 | convolution fusion | flops 2562588672 | bytes 20381696 | tf_op jit(solution)/shard_map/sjcd,jdf->sjcf/dot_general | solution.py:150
  255.8 12.4 %all-gather.22.cloned.1.call-done = bf16[1,2,2048,512]{3,2,1,0:T(8,128)(2,1)} async-done(((bf16[1,2,256,512]{3,2,1,0:T(8,128)(2,1)}), bf16[1,2,2048,512]{3,2,1,0:T(8,128)(2,1)}) %all-gather.22.cloned.1.call-update) | async-done | bytes 4194320 | tf_op jit(solution)/shard_map/all_gather | solution.py:73
  268.2 6.4 fusion.87
  275.8 4.3 all-to-all-start.3
  280.1 8.7 %fusion.5 = bf16[4,2,152,2048]{3,2,0,1:T(8,128)(2,1)S(1)} fusion(f32[2,4,152,2048]{3,2,1,0:T(8,128)} %get-tuple-element.164, bf16[1,2,2048,512]{3,2,1,0:T(8,128)(2,1)} %all-gather.22.cloned.1.call-done, bf16[4,2,152,512]{3,2,1,0:T(8,128)(2,1)} %all-to-all-done.4), kind=kOutput, calls=%fused_computation.7 | convolution fusion | flops 2575040512 | bytes 20381696 | tf_op jit(solution)/shard_map/sjcd,jfd->sjcf/dot_general | solution.py:172
  288.8 2.8 fusion.84
  292.7 6.4 bitcast_convert_fusion.3
  299.1 4.7 all-to-all-start.5
  306.3 3.2 multiply_reduce_fusion.13
  309.6 10.7 %all-to-all-done.5 = bf16[4,2,152,512]{3,2,1,0:T(8,128)(2,1)} async-done(((bf16[4,2,152,512]{3,2,1,0:T(8,128)(2,1)}), bf16[4,2,152,512]{3,2,1,0:T(8,128)(2,1)}, u32[]{:S(2)}, u32[]{:S(2)}) %all-to-all-start.5) | async-done | bytes 1245216 | tf_op jit(solution)/shard_map/all_to_all | solution.py:97
  332.7 2.9 fusion.137
  362.2 4.5 all-to-all-start.6
  379.5 4.1 convolution_convert_fusion
  383.6 4.6 concatenate.25
  388.2 3.1 copy.471
  391.4 8.7 %fusion.11 = bf16[4,2,152,2048]{3,2,0,1:T(8,128)(2,1)S(1)} fusion(f32[2,4,152,2048]{3,2,1,0:T(8,128)} %get-tuple-element.153, bf16[1,2,2048,512]{3,2,1,0:T(8,128)(2,1)} %all-gather.18.cloned.1.call-done, bf16[4,2,152,512]{3,2,1,0:T(8,128)(2,1)} %all-to-all-done.6), kind=kOutput, calls=%fused_computation.13 | convolution fusion | flops 2575040512 | bytes 20381696 | tf_op jit(solution)/shard_map/sjcd,jfd->sjcf/dot_general | solution.py:172
  400.1 2.8 fusion.78
  404.0 4.3 all-to-all-start.7
  408.3 8.3 %bitcast_convert_fusion.2 = bf16[2,512,2048]{2,1,0:T(8,128)(2,1)} fusion(bf16[4,2,152,512]{3,2,1,0:T(8,128)(2,1)} %all-to-all-done, bf16[4,2,152,2048]{3,2,0,1:T(8,128)(2,1)} %copy-done.76), kind=kOutput, calls=%fused_computation.28 | convolution fusion | flops 2552233984 | bytes 10420224 | tf_op jit(solution)/shard_map/sjcd,sjcf->jdf/dot_general | solution.py:180
  416.6 7.3 all-to-all-done.7
  423.9 4.7 all-to-all-start.9
  456.0 3.5 multiply_reduce_fusion.5
  463.0 4.4 concatenate.24
  467.4 3.2 copy.472
  470.6 4.5 all-to-all-start.8
  477.3 23.6 %all-to-all-done.8 = bf16[4,8,16,2060]{3,2,1,0:T(8,128)(2,1)} async-done(((bf16[4,8,16,2060]{3,2,1,0:T(8,128)(2,1)}), bf16[4,8,16,2060]{3,2,1,0:T(8,128)(2,1)}, u32[]{:S(2)}, u32[]{:S(2)}) %all-to-all-start.8) | async-done | bytes 2109472 | tf_op jit(solution)/shard_map/all_to_all | solution.py:97
  504.1 8.2 %bitcast_convert_fusion = bf16[2,2048,512]{2,1,0:T(8,128)(2,1)} fusion(bf16[4,2,152,2048]{3,2,0,1:T(8,128)(2,1)} %get-tuple-element.163, bf16[4,2,152,512]{3,2,1,0:T(8,128)(2,1)} %all-to-all-done.4), kind=kOutput, calls=%fused_computation.26 | convolution fusion | flops 2552233984 | bytes 10420224 | tf_op jit(solution)/shard_map/sjcf,sjcd->jfd/dot_general | solution.py:168
  512.4 8.2 %bitcast_convert_fusion.1 = bf16[2,2048,512]{2,1,0:T(8,128)(2,1)} fusion(bf16[4,2,152,2048]{3,2,0,1:T(8,128)(2,1)} %get-tuple-element.152, bf16[4,2,152,512]{3,2,1,0:T(8,128)(2,1)} %all-to-all-done.6), kind=kOutput, calls=%fused_computation.27 | convolution fusion | flops 2552233984 | bytes 10420224 | tf_op jit(solution)/shard_map/sjcf,sjcd->jfd/dot_general | solution.py:168
  525.3 9.7 %reduce-scatter.6.cloned.1.call-done = bf16[1,16,2,2060]{3,1,2,0:T(8,128)(2,1)} async-done(((bf16[8,16,2,2060]{3,1,2,0:T(8,128)(2,1)}), bf16[1,16,2,2060]{3,1,2,0:T(8,128)(2,1)}) %reduce-scatter.6.cloned.1.call-update) | async-done | bytes 131856 | tf_op jit(solution)/shard_map/reduce_scatter | solution.py:319
  536.0 10.3 %all-gather.4 = bf16[1,64,2,2060]{3,2,0,1:T(2,128)(2,1)S(1)} all-gather(bf16[1,16,2,2060]{3,2,0,1:T(2,128)(2,1)S(1)} %copy.399), channel_id=6, replica_groups=mesh['dp'=8,'expert'=4] {'expert'}, dimensions={1}, use_global_device_ids=true | all-gather | bytes 659200 | tf_op jit(solution)/shard_map/all_gather | solution.py:320
  550.8 34.6 %reduce-scatter.14.cloned.1.call-done = bf16[2,256,512]{2,1,0:T(8,128)(2,1)} async-done(((bf16[2,2048,512]{2,1,0:T(8,128)(2,1)}), bf16[2,256,512]{2,1,0:T(8,128)(2,1)}) %reduce-scatter.14.cloned.1.call-update) | async-done | bytes 524304 | tf_op jit(solution)/shard_map/reduce_scatter | solution.py:171
  585.4 50.7 %reduce-scatter.12.cloned.1.call-done = bf16[2,256,512]{2,1,0:T(8,128)(2,1)} async-done(((bf16[2,2048,512]{2,1,0:T(8,128)(2,1)}), bf16[2,256,512]{2,1,0:T(8,128)(2,1)}) %reduce-scatter.12.cloned.1.call-update) | async-done | bytes 524304 | tf_op jit(solution)/shard_map/reduce_scatter | solution.py:171
  636.1 2.7 maximum_convert_fusion.1
  638.8 47.9 %reduce-scatter.10.cloned.1.call-done = bf16[2,512,256]{2,1,0:T(8,128)(2,1)} async-done(((bf16[2,512,2048]{2,1,0:T(8,128)(2,1)}), bf16[2,512,256]{2,1,0:T(8,128)(2,1)}) %reduce-scatter.10.cloned.1.call-update) | async-done | bytes 524304 | tf_op jit(solution)/shard_map/reduce_scatter | solution.py:184
  686.7 50.7 %reduce-scatter.8.cloned.1.call-done = bf16[2,512,256]{2,1,0:T(8,128)(2,1)} async-done(((bf16[2,512,2048]{2,1,0:T(8,128)(2,1)}), bf16[2,512,256]{2,1,0:T(8,128)(2,1)}) %reduce-scatter.8.cloned.1.call-update) | async-done | bytes 524304 | tf_op jit(solution)/shard_map/reduce_scatter | solution.py:184
  737.4 2.7 maximum_convert_fusion
  (388 shorter events, 195.9 us)
Async XLA Ops:
  7.2 5.4 copy-start.44
  7.2 6.5 copy-start.45
  7.2 38.5 %all-gather.12.cloned.1.call-start = ((), (), s32[]{:S(2)}) async-start(), calls=%async_computation.15 | async-start | bytes 2506752 | tf_op jit(solution)/shard_map/all_gather | solution.py:62
  12.5 82.6 %all-gather.16.cloned.1.call-start = ((), (), s32[]{:S(2)}) async-start(), calls=%async_computation.22 | async-start | bytes 4718592 | tf_op jit(solution)/shard_map/all_gather | solution.py:72
  13.6 3.6 copy-start.29
  13.7 128.2 %all-gather.18.cloned.1.call-start = ((), (), s32[]{:S(2)}) async-start(), calls=%async_computation.23 | async-start | bytes 4718592 | tf_op jit(solution)/shard_map/all_gather | solution.py:73
  14.9 157.6 %all-gather.14.cloned.1.call-start = ((), (), s32[]{:S(2)}) async-start(), calls=%async_computation.16 | async-start | bytes 2506752 | tf_op jit(solution)/shard_map/all_gather | solution.py:62
  16.1 230.6 %all-gather.20.cloned.1.call-start = ((), (), s32[]{:S(2)}) async-start(), calls=%async_computation.24 | async-start | bytes 4718592 | tf_op jit(solution)/shard_map/all_gather | solution.py:72
  16.7 251.5 %all-gather.22.cloned.1.call-start = ((), (), s32[]{:S(2)}) async-start(), calls=%async_computation.25 | async-start | bytes 4718592 | tf_op jit(solution)/shard_map/all_gather | solution.py:73
  18.8 30.8 %copy-start.14 = (f32[394,512]{1,0:T(8,128)}, f32[394,512]{1,0:T(8,128)S(1)}, u32[]{:S(2)}) copy-start(f32[394,512]{1,0:T(8,128)S(1)} %reshape.322) | copy-start | bytes 2420740
  19.0 30.6 %copy-start.62 = (f32[394]{0:T(512)}, f32[394]{0:T(512)S(1)}, u32[]{:S(2)}) copy-start(f32[394]{0:T(512)S(1)} %rsqrt.36) | copy-start | bytes 4732
  19.1 30.5 %copy-start.64 = (f32[394]{0:T(512)}, f32[394]{0:T(512)S(1)}, u32[]{:S(2)}) copy-start(f32[394]{0:T(512)S(1)} %div.83) | copy-start | bytes 4732
  22.0 337.3 %copy-start.72 = (s32[394]{0:T(512)}, s32[394]{0:T(512)S(1)}, u32[]{:S(2)}) copy-start(s32[394]{0:T(512)S(1)} %get-tuple-element.178) | copy-start | bytes 4732
  22.0 338.2 %copy-start.69 = (s32[394]{0:T(512)}, s32[394]{0:T(512)S(1)}, u32[]{:S(2)}) copy-start(s32[394]{0:T(512)S(1)} %get-tuple-element.177) | copy-start | bytes 4732
  47.3 21.1 %copy-start.54 = (f32[512]{0:T(512)}, f32[512]{0:T(512)S(1)}, u32[]{:S(2)}) copy-start(f32[512]{0:T(512)S(1)} %get-tuple-element.176) | copy-start | bytes 6148
  68.2 3.8 copy-start.51
  68.4 3.5 copy-start.56
  71.9 21.1 %all-to-all-start = ((bf16[4,2,152,512]{3,2,1,0:T(8,128)(2,1)}), bf16[4,2,152,512]{3,2,1,0:T(8,128)(2,1)}, u32[]{:S(2)}, u32[]{:S(2)}) async-start(bf16[4,2,152,512]{3,2,1,0:T(8,128)(2,1)} %bitcast.288), calls=%async_computation | async-start | bytes 2490368 | tf_op jit(solution)/shard_map/all_to_all | solution.py:97
  149.4 24.8 %all-to-all-start.1 = ((bf16[4,2,152,512]{3,2,1,0:T(8,128)(2,1)}), bf16[4,2,152,512]{3,2,1,0:T(8,128)(2,1)}, u32[]{:S(2)}, u32[]{:S(2)}) async-start(bf16[4,2,152,512]{3,2,1,0:T(8,128)(2,1)} %copy.335), calls=%async_computation.1 | async-start | bytes 2490368 | tf_op jit(solution)/shard_map/all_to_all | solution.py:97
  173.8 184.5 %copy-start.58 = (f32[512]{0:T(512)}, f32[512]{0:T(512)S(1)}, u32[]{:S(2)}) copy-start(f32[512]{0:T(512)S(1)} %get-tuple-element.95) | copy-start | bytes 6148
  174.2 6.3 copy-start.68
  176.6 3.9 copy-start.35
  176.6 3.9 copy-start.25
  180.2 178.1 %copy-start.53 = (f32[394]{0:T(512)}, f32[394]{0:T(512)S(1)}, u32[]{:S(2)}) copy-start(f32[394]{0:T(512)S(1)} %broadcast_multiply_fusion.10) | copy-start | bytes 4732
  180.5 177.9 %copy-start.59 = (f32[394]{0:T(512)}, f32[394]{0:T(512)S(1)}, u32[]{:S(2)}) copy-start(f32[394]{0:T(512)S(1)} %add_rsqrt_fusion.2) | copy-start | bytes 4732
  213.1 29.3 %all-to-all-start.2 = ((bf16[4,2,152,512]{3,2,1,0:T(8,128)(2,1)}), bf16[4,2,152,512]{3,2,1,0:T(8,128)(2,1)}, u32[]{:S(2)}, u32[]{:S(2)}) async-start(bf16[4,2,152,512]{3,2,1,0:T(8,128)(2,1)} %bitcast.290), calls=%async_computation.2 | async-start | bytes 2490368 | tf_op jit(solution)/shard_map/all_to_all | solution.py:97
  226.2 3.5 copy-start.30
  242.4 33.4 %all-to-all-start.4 = ((bf16[4,2,152,512]{3,2,1,0:T(8,128)(2,1)}), bf16[4,2,152,512]{3,2,1,0:T(8,128)(2,1)}, u32[]{:S(2)}, u32[]{:S(2)}) async-start(bf16[4,2,152,512]{3,2,1,0:T(8,128)(2,1)} %bitcast.289), calls=%async_computation.4 | async-start | bytes 2490368 | tf_op jit(solution)/shard_map/all_to_all | solution.py:97
  275.8 23.3 %all-to-all-start.3 = ((bf16[4,2,152,512]{3,2,1,0:T(8,128)(2,1)}), bf16[4,2,152,512]{3,2,1,0:T(8,128)(2,1)}, u32[]{:S(2)}, u32[]{:S(2)}) async-start(bf16[4,2,152,512]{3,2,1,0:T(8,128)(2,1)} %copy.349), calls=%async_computation.3 | async-start | bytes 2490368 | tf_op jit(solution)/shard_map/all_to_all | solution.py:97
  280.1 8.7 %copy-start.75 = (bf16[1,2,512,2048]{3,2,1,0:T(8,128)(2,1)S(1)}, bf16[1,2,512,2048]{3,2,1,0:T(8,128)(2,1)}, u32[]{:S(2)}) copy-start(bf16[1,2,512,2048]{3,2,1,0:T(8,128)(2,1)} %all-gather.20.cloned.1.call-done) | copy-start | bytes 12582916
  299.1 21.2 %all-to-all-start.5 = ((bf16[4,2,152,512]{3,2,1,0:T(8,128)(2,1)}), bf16[4,2,152,512]{3,2,1,0:T(8,128)(2,1)}, u32[]{:S(2)}, u32[]{:S(2)}) async-start(bf16[4,2,152,512]{3,2,1,0:T(8,128)(2,1)} %copy.352), calls=%async_computation.5 | async-start | bytes 2490368 | tf_op jit(solution)/shard_map/all_to_all | solution.py:97
  353.1 3.4 copy-start.26
  362.2 29.2 %all-to-all-start.6 = ((bf16[4,2,152,512]{3,2,1,0:T(8,128)(2,1)}), bf16[4,2,152,512]{3,2,1,0:T(8,128)(2,1)}, u32[]{:S(2)}, u32[]{:S(2)}) async-start(bf16[4,2,152,512]{3,2,1,0:T(8,128)(2,1)} %bitcast.287), calls=%async_computation.6 | async-start | bytes 2490368 | tf_op jit(solution)/shard_map/all_to_all | solution.py:97
  391.4 8.7 %copy-start.74 = (bf16[1,2,512,2048]{3,2,1,0:T(8,128)(2,1)S(1)}, bf16[1,2,512,2048]{3,2,1,0:T(8,128)(2,1)}, u32[]{:S(2)}) copy-start(bf16[1,2,512,2048]{3,2,1,0:T(8,128)(2,1)} %all-gather.16.cloned.1.call-done) | copy-start | bytes 12582916
  404.0 19.9 %all-to-all-start.7 = ((bf16[4,2,152,512]{3,2,1,0:T(8,128)(2,1)}), bf16[4,2,152,512]{3,2,1,0:T(8,128)(2,1)}, u32[]{:S(2)}, u32[]{:S(2)}) async-start(bf16[4,2,152,512]{3,2,1,0:T(8,128)(2,1)} %copy.367), calls=%async_computation.7 | async-start | bytes 2490368 | tf_op jit(solution)/shard_map/all_to_all | solution.py:97
  416.6 12.0 %copy-start.70 = (s32[394]{0:T(512)S(1)}, s32[394]{0:T(512)}, u32[]{:S(2)}) copy-start(s32[394]{0:T(512)} %copy-done.69) | copy-start | bytes 4732
  416.6 12.0 %copy-start.73 = (s32[394]{0:T(512)S(1)}, s32[394]{0:T(512)}, u32[]{:S(2)}) copy-start(s32[394]{0:T(512)} %copy-done.72) | copy-start | bytes 4732
  423.9 46.6 %all-to-all-start.9 = ((bf16[4,8,16,2060]{3,2,1,0:T(8,128)(2,1)}), bf16[4,8,16,2060]{3,2,1,0:T(8,128)(2,1)}, u32[]{:S(2)}, u32[]{:S(2)}) async-start(bf16[4,8,16,2060]{3,2,1,0:T(8,128)(2,1)} %bitcast.281), calls=%async_computation.9 | async-start | bytes 4456448 | tf_op jit(solution)/shard_map/all_to_all | solution.py:97
  448.4 3.8 copy-start.20
  456.0 4.1 copy-start.13
  456.0 4.1 copy-start.18
  456.0 4.6 copy-start.67
  470.6 30.3 %all-to-all-start.8 = ((bf16[4,8,16,2060]{3,2,1,0:T(8,128)(2,1)}), bf16[4,8,16,2060]{3,2,1,0:T(8,128)(2,1)}, u32[]{:S(2)}, u32[]{:S(2)}) async-start(bf16[4,8,16,2060]{3,2,1,0:T(8,128)(2,1)} %bitcast.282), calls=%async_computation.8 | async-start | bytes 4456448 | tf_op jit(solution)/shard_map/all_to_all | solution.py:97
  475.0 60.0 %reduce-scatter.6.cloned.1.call-start = ((), (), s32[]{:S(2)}) async-start(), calls=%async_computation.17 | async-start | bytes 1253376 | tf_op jit(solution)/shard_map/reduce_scatter | solution.py:319
  504.1 81.4 %reduce-scatter.14.cloned.1.call-start = ((), (), s32[]{:S(2)}) async-start(), calls=%async_computation.21 | async-start | bytes 4718592 | tf_op jit(solution)/shard_map/reduce_scatter | solution.py:171
  512.3 123.8 %reduce-scatter.12.cloned.1.call-start = ((), (), s32[]{:S(2)}) async-start(), calls=%async_computation.20 | async-start | bytes 4718592 | tf_op jit(solution)/shard_map/reduce_scatter | solution.py:171
  520.6 166.1 %reduce-scatter.10.cloned.1.call-start = ((), (), s32[]{:S(2)}) async-start(), calls=%async_computation.19 | async-start | bytes 4718592 | tf_op jit(solution)/shard_map/reduce_scatter | solution.py:184
  521.2 216.2 %reduce-scatter.8.cloned.1.call-start = ((), (), s32[]{:S(2)}) async-start(), calls=%async_computation.18 | async-start | bytes 4718592 | tf_op jit(solution)/shard_map/reduce_scatter | solution.py:184
  (50 other events, 93.2 us)
Sparse Core Ops, SparseCore 0:
  12.7 32.9 all-gather.11
  47.8 47.2 all-gather.15
  96.8 45.0 all-gather.17
  143.3 29.0 all-gather.13
  174.4 47.1 all-gather.19
  223.1 45.0 all-gather.21
  504.2 30.7 reduce-scatter.5
  537.3 48.1 reduce-scatter.13
  587.7 48.3 reduce-scatter.11
  638.3 48.3 reduce-scatter.9
  689.0 48.3 reduce-scatter.7

commit v3 on v2

--- a/solution.py
+++ b/solution.py
@@ -48,24 +48,42 @@
     )
 
 
-def gather_dense(which, w_qkv, w_proj, w_router, norm_gains, norm_shifts):
+def gather_quarters(w_qkv, w_proj, w_router, norm_gains, norm_shifts):
+    peers, rank = lax.axis_size("expert"), lax.axis_index("expert")
+    piece = w_qkv.shape[1] // peers
     packed = jnp.concatenate(
-        [
-            w_qkv[which],
-            w_proj[which],
-            w_router[which],
-            norm_gains[which].T,
-            norm_shifts[which].T,
-        ],
-        axis=1,
-    )
-    full = lax.all_gather(packed, "dp", axis=0, tiled=True)
-    width = full.shape[0]
-    experts = w_router.shape[2]
-    wide = full[:, 4 * width :]
+        [w_qkv, w_proj, w_router, jnp.swapaxes(norm_gains, 1, 2), jnp.swapaxes(norm_shifts, 1, 2)],
+        axis=2,
+    )
+    packed = lax.dynamic_slice_in_dim(packed, rank * piece, piece, axis=1)
+    return lax.all_gather(packed, "dp", axis=1, tiled=True)
+
+
+def spread_dense(quarter, experts):
+    peers, shares = lax.axis_size("expert"), lax.axis_size("dp")
+    rows, columns = quarter.shape
+    parts = exchange(jnp.broadcast_to(quarter[None], (peers, rows, columns)))
+    width = peers * rows
+    parts = parts.reshape(peers, shares, rows // shares, columns)
+
+    def whole(start, stop):
+        return parts[..., start:stop].swapaxes(0, 1).reshape(width, stop - start)
+
+    base = 4 * width
+    wide = whole(base, columns)
     gains = wide[:, experts : experts + 2].T.astype(jnp.float32)
     shifts = wide[:, experts + 2 : experts + 4].T.astype(jnp.float32)
-    return (full[:, : 3 * width], full[:, 3 * width : 4 * width], wide[:, :experts], gains, shifts)
+    return (whole(0, 3 * width), whole(3 * width, base), wide[:, :experts], gains, shifts)
+
+
+def owner_gates(incoming, router_full):
+    logits = jnp.einsum("sjcd,de->sjce", incoming, router_full, preferred_element_type=jnp.float32)
+    router_probs, _ = softmax_rows(logits)
+    local = incoming.shape[1]
+    own = lax.axis_index("expert") * local + jnp.arange(local, dtype=jnp.int32)
+    labels = jnp.arange(router_full.shape[1], dtype=jnp.int32)
+    pick = (own[:, None] == labels[None, :]).astype(jnp.float32)
+    return jnp.sum(router_probs * pick[None, :, None, :], axis=-1, keepdims=True)
 
 
 def gather_experts(which, w_first, w_second):
@@ -272,21 +290,28 @@
     resid = embedded.reshape(tok_count, width).astype(jnp.float32)
     grad = cotangent.reshape(tok_count, width).astype(jnp.float32)
     dense, experts, tables = [], [], []
+    quarters = gather_quarters(w_qkv, w_proj, w_router, norm_gains, norm_shifts)
     for which in range(LAYERS):
-        dense.append(gather_dense(which, w_qkv, w_proj, w_router, norm_gains, norm_shifts))
         experts.append(gather_experts(which, w_first, w_second))
+        tables.append(
+            route_tables(routes[which].reshape(tok_count, 2), experts_total, capacity)
+        )
+    last = tables[LAYERS - 1]
+    slots = slots_of(cotangent.reshape(tok_count, width), last[2] + last[3], block_shape)
+    cot_rows = exchange(slots)
+    for which in range(LAYERS):
+        dense.append(spread_dense(quarters[which], experts_total))
     attn_saved, moe_saved, kept = [], [], []
     grad_result = None
     for which in range(LAYERS):
-        table = route_tables(routes[which].reshape(tok_count, 2), experts_total, capacity)
-        tables.append(table)
+        table = tables[which]
         resid_mid, attn_part, moe_part = attend_forward(resid, dense[which], table)
         outgoing = slots_of(moe_part[2], table[2] + table[3], block_shape)
         incoming = exchange(outgoing)
+        hidden_pre, hidden_act = experts_hidden(incoming, experts[which][0])
         if which == LAYERS - 1:
-            slots = gated_slots(grad, moe_part, table, block_shape)
-            grad_result = exchange(slots)
-        hidden_pre, hidden_act = experts_hidden(incoming, experts[which][0])
+            gates = owner_gates(incoming, dense[which][2])
+            grad_result = (gates * cot_rows.astype(jnp.float32)).astype(jnp.bfloat16)
         result = experts_result(hidden_act, experts[which][1])
         returned = exchange(result).reshape(experts_total * capacity, width)
         backs = (rows_back(returned, table[2]), rows_back(returned, table[3]))

time: 759 us -> 721 us (0.950)
  waiting for transfers between devices: 354 us -> 294 us
  local copies, waits for them, and re-layouts: 121 us -> 149 us
    all_gather x2, waiting for transfers between devices: 50.1 us -> 0.01 us  [gather_experts(): second_full = lax.all_gather(w_second[which], 'dp', axis=1, tiled=True)]
    all_gather x2 -> x1, waiting for transfers between devices: 42.3 us -> 12.9 us  [gather_quarters(): return lax.all_gather(packed, 'dp', axis=1, tiled=True)]
    all_to_all x10 -> x12, waiting for transfers between devices: 63 us -> 84.5 us  [exchange(): lax.all_to_all(block, 'expert', split_axis=0, concat_axis=0, tiled=True)]
    transpose x6 -> x14, local copies, waits for them, and re-layouts: 1.81 us -> 14.7 us  [the longest x12 13.1 us: whole(): return parts[..., start:stop].swapaxes(0, 1).reshape(width, stop - start)]
    unnamed x167 -> x243, local copies, waits for them, and re-layouts: 19.1 us -> 21.9 us
    all_to_all x10 -> x12, starting transfers between devices: 53.1 us -> 52.8 us  [exchange(): lax.all_to_all(block, 'expert', split_axis=0, concat_axis=0, tiled=True)]
  transfers between devices with their start and end apart: 21 -> 22, of which waited for: 15 -> 14; matrix products, arithmetic and copies ran while one was open for 32% -> 38% of each run, Pallas kernels for 0% -> 0%
where the time goes in v3:
time: 721 us; the launch traced here: 713 us
  waiting for transfers between devices  294 us (41%)
  matrix products  162 us (22%)
  local copies, waits for them, and re-layouts  149 us (21%)
  starting transfers between devices  53.4 us (7%)
  other arithmetic  27.3 us (4%)
  between operations  16.6 us (2%)
  blocking collectives  10.3 us (1%)
    reduce_scatter x2, waiting for transfers between devices, experts_backward(): lax.psum_scatter(grad_first, 'dp', scatter_dimension=2, tiled=True)  98.6 us
    reduce_scatter x2, waiting for transfers between devices, experts_backward(): lax.psum_scatter(grad_second, 'dp', scatter_dimension=1, tiled=True)  85.7 us
    all_to_all x12, waiting for transfers between devices, exchange(): lax.all_to_all(block, 'expert', split_axis=0, concat_axis=0, tiled=True)  84.5 us
    all_to_all x12, starting transfers between devices, exchange(): lax.all_to_all(block, 'expert', split_axis=0, concat_axis=0, tiled=True)  52.8 us
    unnamed x243, local copies, waits for them, and re-layouts  21.9 us
    dot_general x2, matrix products, experts_hidden(): jnp.einsum('sjcd,jdf->sjcf', incoming, first_full, preferred_element_type...  18.1 us
    dot_general x2, matrix products, experts_backward(): jnp.einsum('sjcd,jfd->sjcf', grad_result, second_full, preferred_element_...  17 us
    dot_general x2, matrix products, experts_backward(): jnp.einsum('sjcf,sjcd->jfd', hidden_act, grad_result, preferred_element_t...  16.6 us
  transfers between devices with their start and end apart: 22, of which 14 were waited for; matrix products, arithmetic and copies ran while one was open for 38% of the time, Pallas kernels for 0%

profile of v3, /device:TPU:0, one launch (start us, length us, event | category | flops | bytes accessed | tf_op | source)
XLA Modules:
  0.0 713.2 jit_solution(12251457799776861412)
XLA Ops:
  24.2 12.9 %all-gather.11.cloned.1.call-done = bf16[2,128,2060]{2,1,0:T(8,128)(2,1)} async-done(((bf16[2,16,2060]{2,1,0:T(8,128)(2,1)}), bf16[2,128,2060]{2,1,0:T(8,128)(2,1)}) %all-gather.11.cloned.1.call-update) | async-done | bytes 1054736 | tf_op jit(solution)/shard_map/all_gather | solution.py:59
  40.3 3.7 all-to-all-start
  44.9 2.9 convolution_convert_fusion.2
  48.8 20.8 %all-to-all-done = bf16[4,128,2060]{1,2,0:T(8,128)(2,1)S(1)} async-done(((bf16[4,128,2060]{1,2,0:T(8,128)(2,1)}), bf16[4,128,2060]{1,2,0:T(8,128)(2,1)S(1)}, u32[]{:S(2)}, u32[]{:S(2)}) %all-to-all-start) | async-done | bytes 2109472 | tf_op jit(solution)/shard_map/all_to_all | solution.py:115
  69.7 3.0 broadcast_in_dim.11
  72.7 4.7 all-to-all-start.3
  77.4 2.9 copy.426
  107.3 4.7 all-to-all-start.1
  112.0 4.1 copy.443
  121.0 6.9 all-to-all-done.1
  127.9 9.1 %fusion.19 = (bf16[4,2,152,2048]{3,2,0,1:T(8,128)(2,1)}, f32[2,4,152,2048]{3,2,1,0:T(8,128)}) fusion(bf16[1,2,512,2048]{3,2,1,0:T(8,128)(2,1)} %all-gather.13.cloned.1.call-done, bf16[4,2,152,512]{3,2,1,0:T(8,128)(2,1)} %all-to-all-done.1), kind=kOutput, calls=%fused_computation.25 | convolution fusion | flops 2562588672 | bytes 20381696 | tf_op jit(solution)/shard_map/sjcd,jdf->sjcf/dot_general | solution.py:168
  137.0 6.5 fusion.81
  144.7 4.3 all-to-all-start.2
  154.8 9.4 %all-to-all-done.2 = bf16[4,2,152,512]{3,2,1,0:T(8,128)(2,1)} async-done(((bf16[4,2,152,512]{3,2,1,0:T(8,128)(2,1)}), bf16[4,2,152,512]{3,2,1,0:T(8,128)(2,1)}, u32[]{:S(2)}, u32[]{:S(2)}) %all-to-all-start.2) | async-done | bytes 1245216 | tf_op jit(solution)/shard_map/all_to_all | solution.py:115
  166.6 3.6 fusion.202
  203.2 4.4 all-to-all-start.4
  209.0 13.9 %all-to-all-done.4 = bf16[4,2,152,512]{3,2,1,0:T(8,128)(2,1)} async-done(((bf16[4,2,152,512]{3,2,1,0:T(8,128)(2,1)}), bf16[4,2,152,512]{3,2,1,0:T(8,128)(2,1)}, u32[]{:S(2)}, u32[]{:S(2)}) %all-to-all-start.4) | async-done | bytes 1245216 | tf_op jit(solution)/shard_map/all_to_all | solution.py:115
  222.9 4.5 all-to-all-start.6
  227.4 9.0 %fusion.15 = (bf16[4,2,152,2048]{3,2,0,1:T(8,128)(2,1)}, f32[2,4,152,2048]{3,2,1,0:T(8,128)}) fusion(bf16[1,2,512,2048]{3,2,1,0:T(8,128)(2,1)} %all-gather.17.cloned.1.call-done, bf16[4,2,152,512]{3,2,1,0:T(8,128)(2,1)} %all-to-all-done.4), kind=kOutput, calls=%fused_computation.19 | convolution fusion | flops 2562588672 | bytes 20381696 | tf_op jit(solution)/shard_map/sjcd,jdf->sjcf/dot_general | solution.py:168
  236.4 6.4 fusion.87
  245.8 4.3 all-to-all-start.5
  250.1 8.3 %fusion.7 = bf16[4,2,152,2048]{3,2,0,1:T(8,128)(2,1)S(1)} fusion(f32[2,4,152,2048]{3,2,1,0:T(8,128)} %get-tuple-element.165, bf16[1,2,2048,512]{3,2,1,0:T(8,128)(2,1)} %all-gather.19.cloned.1.call-done, bf16[4,2,152,512]{3,2,1,0:T(8,128)(2,1)} %all-to-all-done.6, f32[4,2,152]{2,1,0:T(2,128)S(1)} %fusion.223), kind=kOutput, calls=%fused_computation.9 | convolution fusion | flops 2576908288 | bytes 20386560 | tf_op jit(solution)/shard_map/sjcd,jfd->sjcf/dot_general | solution.py:190
  262.4 3.0 all-to-all-done.5
  265.4 4.5 all-to-all-start.7
  270.0 8.2 %bitcast_convert_fusion.3 = bf16[2,512,2048]{2,1,0:T(8,128)(2,1)} fusion(bf16[4,2,152,512]{3,2,1,0:T(8,128)(2,1)} %all-to-all-done.4, bf16[4,2,152,2048]{3,2,0,1:T(8,128)(2,1)} %copy-done.112), kind=kOutput, calls=%fused_computation.31 | convolution fusion | flops 2552233984 | bytes 10420224 | tf_op jit(solution)/shard_map/sjcd,sjcf->jdf/dot_general | solution.py:198
  280.7 3.2 fusion.147
  296.0 2.9 fusion.130
  325.6 4.5 all-to-all-start.8
  343.1 4.1 convolution_convert_fusion
  347.2 4.6 concatenate.21
  351.8 3.1 copy.580
  354.9 8.7 %fusion.13 = bf16[4,2,152,2048]{3,2,0,1:T(8,128)(2,1)S(1)} fusion(f32[2,4,152,2048]{3,2,1,0:T(8,128)} %get-tuple-element.154, bf16[1,2,2048,512]{3,2,1,0:T(8,128)(2,1)} %all-gather.15.cloned.1.call-done, bf16[4,2,152,512]{3,2,1,0:T(8,128)(2,1)} %all-to-all-done.8), kind=kOutput, calls=%fused_computation.15 | convolution fusion | flops 2575040512 | bytes 20381696 | tf_op jit(solution)/shard_map/sjcd,jfd->sjcf/dot_general | solution.py:190
  367.6 4.3 all-to-all-start.9
  371.9 8.3 %bitcast_convert_fusion.2 = bf16[2,512,2048]{2,1,0:T(8,128)(2,1)} fusion(bf16[4,2,152,512]{3,2,1,0:T(8,128)(2,1)} %all-to-all-done.1, bf16[4,2,152,2048]{3,2,0,1:T(8,128)(2,1)} %copy-done.113), kind=kOutput, calls=%fused_computation.30 | convolution fusion | flops 2552233984 | bytes 10420224 | tf_op jit(solution)/shard_map/sjcd,sjcf->jdf/dot_general | solution.py:198
  380.2 7.1 all-to-all-done.9
  387.2 4.7 all-to-all-start.11
  430.6 3.6 concatenate.20
  435.7 4.2 all-to-all-start.10
  440.2 2.9 reduce_sum.485
  443.1 22.1 %all-to-all-done.10 = bf16[4,8,16,2060]{3,2,1,0:T(8,128)(2,1)S(1)} async-done(((bf16[4,8,16,2060]{3,2,1,0:T(8,128)(2,1)}), bf16[4,8,16,2060]{3,2,1,0:T(8,128)(2,1)S(1)}, u32[]{:S(2)}, u32[]{:S(2)}) %all-to-all-start.10) | async-done | bytes 2109472 | tf_op jit(solution)/shard_map/all_to_all | solution.py:115
  468.9 8.3 %bitcast_convert_fusion = bf16[2,2048,512]{2,1,0:T(8,128)(2,1)} fusion(bf16[4,2,152,2048]{3,2,0,1:T(8,128)(2,1)} %get-tuple-element.164, bf16[4,2,152,512]{3,2,1,0:T(8,128)(2,1)} %all-to-all-done.6, f32[4,2,152]{2,1,0:T(2,128)S(1)} %copy-done.111), kind=kOutput, calls=%fused_computation.28 | convolution fusion | flops 2554101760 | bytes 10425088 | tf_op jit(solution)/shard_map/sjcf,sjcd->jfd/dot_general | solution.py:186
  477.2 8.3 %bitcast_convert_fusion.1 = bf16[2,2048,512]{2,1,0:T(8,128)(2,1)} fusion(bf16[4,2,152,2048]{3,2,0,1:T(8,128)(2,1)} %get-tuple-element.153, bf16[4,2,152,512]{3,2,1,0:T(8,128)(2,1)} %all-to-all-done.8), kind=kOutput, calls=%fused_computation.29 | convolution fusion | flops 2552233984 | bytes 10420224 | tf_op jit(solution)/shard_map/sjcf,sjcd->jfd/dot_general | solution.py:186
  490.4 10.0 %reduce-scatter.6.cloned.1.call-done = bf16[1,16,2,2060]{3,1,2,0:T(8,128)(2,1)} async-done(((bf16[8,16,2,2060]{3,1,2,0:T(8,128)(2,1)}), bf16[1,16,2,2060]{3,1,2,0:T(8,128)(2,1)}) %reduce-scatter.6.cloned.1.call-update) | async-done | bytes 131856 | tf_op jit(solution)/shard_map/reduce_scatter | solution.py:344
  501.5 10.3 %all-gather.4 = bf16[1,64,2,2060]{3,2,0,1:T(2,128)(2,1)S(1)} all-gather(bf16[1,16,2,2060]{3,2,0,1:T(2,128)(2,1)S(1)} %copy.507), channel_id=6, replica_groups=mesh['dp'=8,'expert'=4] {'expert'}, dimensions={1}, use_global_device_ids=true | all-gather | bytes 659200 | tf_op jit(solution)/shard_map/all_gather | solution.py:345
  516.3 34.9 %reduce-scatter.14.cloned.1.call-done = bf16[2,256,512]{2,1,0:T(8,128)(2,1)} async-done(((bf16[2,2048,512]{2,1,0:T(8,128)(2,1)}), bf16[2,256,512]{2,1,0:T(8,128)(2,1)}) %reduce-scatter.14.cloned.1.call-update) | async-done | bytes 524304 | tf_op jit(solution)/shard_map/reduce_scatter | solution.py:189
  551.2 50.7 %reduce-scatter.12.cloned.1.call-done = bf16[2,256,512]{2,1,0:T(8,128)(2,1)} async-done(((bf16[2,2048,512]{2,1,0:T(8,128)(2,1)}), bf16[2,256,512]{2,1,0:T(8,128)(2,1)}) %reduce-scatter.12.cloned.1.call-update) | async-done | bytes 524304 | tf_op jit(solution)/shard_map/reduce_scatter | solution.py:189
  604.6 48.1 %reduce-scatter.10.cloned.1.call-done = bf16[2,512,256]{2,1,0:T(8,128)(2,1)} async-done(((bf16[2,512,2048]{2,1,0:T(8,128)(2,1)}), bf16[2,512,256]{2,1,0:T(8,128)(2,1)}) %reduce-scatter.10.cloned.1.call-update) | async-done | bytes 524304 | tf_op jit(solution)/shard_map/reduce_scatter | solution.py:202
  652.7 50.6 %reduce-scatter.8.cloned.1.call-done = bf16[2,512,256]{2,1,0:T(8,128)(2,1)} async-done(((bf16[2,512,2048]{2,1,0:T(8,128)(2,1)}), bf16[2,512,256]{2,1,0:T(8,128)(2,1)}) %reduce-scatter.8.cloned.1.call-update) | async-done | bytes 524304 | tf_op jit(solution)/shard_map/reduce_scatter | solution.py:202
  (482 shorter events, 220.9 us)
Async XLA Ops:
  7.2 6.8 copy-start.51
  7.2 29.8 %all-gather.11.cloned.1.call-start = ((), (), s32[]{:S(2)}) async-start(), calls=%async_computation.17 | async-start | bytes 1253376 | tf_op jit(solution)/shard_map/all_gather | solution.py:59
  11.6 116.3 %all-gather.13.cloned.1.call-start = ((), (), s32[]{:S(2)}) async-start(), calls=%async_computation.23 | async-start | bytes 4718592 | tf_op jit(solution)/shard_map/all_gather | solution.py:90
  13.9 123.1 %all-gather.15.cloned.1.call-start = ((), (), s32[]{:S(2)}) async-start(), calls=%async_computation.24 | async-start | bytes 4718592 | tf_op jit(solution)/shard_map/all_gather | solution.py:91
  15.0 212.4 %all-gather.17.cloned.1.call-start = ((), (), s32[]{:S(2)}) async-start(), calls=%async_computation.25 | async-start | bytes 4718592 | tf_op jit(solution)/shard_map/all_gather | solution.py:90
  15.6 220.8 %all-gather.19.cloned.1.call-start = ((), (), s32[]{:S(2)}) async-start(), calls=%async_computation.26 | async-start | bytes 4718592 | tf_op jit(solution)/shard_map/all_gather | solution.py:91
  18.8 130.2 %copy-start.57 = (s32[394,1]{0,1:T(1,128)}, s32[394,1]{0,1:T(1,128)S(1)}, u32[]{:S(2)}) copy-start(s32[394,1]{0,1:T(1,128)S(1)} %get-tuple-element.141) | copy-start | bytes 4732
  18.8 130.2 %copy-start.59 = (s32[394,1]{0,1:T(1,128)}, s32[394,1]{0,1:T(1,128)S(1)}, u32[]{:S(2)}) copy-start(s32[394,1]{0,1:T(1,128)S(1)} %get-tuple-element.142) | copy-start | bytes 4732
  20.3 18.4 %copy-start.84 = (s32[8,5]{0,1:T(8,128)}, s32[8,5]{0,1:T(8,128)S(1)}, u32[]{:S(2)}) copy-start(s32[8,5]{0,1:T(8,128)S(1)} %reduce-window.15) | copy-start | bytes 484
  20.4 24.5 %copy-start.61 = (s32[394,1]{0,1:T(1,128)}, s32[394,1]{0,1:T(1,128)S(1)}, u32[]{:S(2)}) copy-start(s32[394,1]{0,1:T(1,128)S(1)} %get-tuple-element.135) | copy-start | bytes 4732
  20.4 24.5 %copy-start.63 = (s32[394,1]{0,1:T(1,128)}, s32[394,1]{0,1:T(1,128)S(1)}, u32[]{:S(2)}) copy-start(s32[394,1]{0,1:T(1,128)S(1)} %get-tuple-element.136) | copy-start | bytes 4732
  21.8 16.8 %copy-start.83 = (s32[8,5]{0,1:T(8,128)}, s32[8,5]{0,1:T(8,128)S(1)}, u32[]{:S(2)}) copy-start(s32[8,5]{0,1:T(8,128)S(1)} %reduce-window.19) | copy-start | bytes 484
  40.3 29.4 %all-to-all-start = ((bf16[4,128,2060]{1,2,0:T(8,128)(2,1)}), bf16[4,128,2060]{1,2,0:T(8,128)(2,1)S(1)}, u32[]{:S(2)}, u32[]{:S(2)}) async-start(bf16[4,128,2060]{1,2,0:T(8,128)(2,1)} %broadcast_in_dim.9), calls=%async_computation | async-start | bytes 4227072 | tf_op jit(solution)/shard_map/all_to_all | solution.py:115
  44.8 119.3 %copy-start.100 = (s32[394]{0:T(512)}, s32[394]{0:T(512)S(1)}, u32[]{:S(2)}) copy-start(s32[394]{0:T(512)S(1)} %get-tuple-element.179) | copy-start | bytes 4732
  44.8 121.7 %copy-start.89 = (s32[394]{0:T(512)}, s32[394]{0:T(512)S(1)}, u32[]{:S(2)}) copy-start(s32[394]{0:T(512)S(1)} %get-tuple-element.178) | copy-start | bytes 4732
  44.9 155.6 %copy-start.103 = (s32[394]{0:T(512)}, s32[394]{0:T(512)S(1)}, u32[]{:S(2)}) copy-start(s32[394]{0:T(512)S(1)} %get-tuple-element.182) | copy-start | bytes 4732
  44.9 155.6 %copy-start.105 = (s32[394]{0:T(512)}, s32[394]{0:T(512)S(1)}, u32[]{:S(2)}) copy-start(s32[394]{0:T(512)S(1)} %get-tuple-element.183) | copy-start | bytes 4732
  72.7 34.6 %all-to-all-start.3 = ((bf16[4,128,2060]{1,2,0:T(8,128)(2,1)}), bf16[4,128,2060]{1,2,0:T(8,128)(2,1)}, u32[]{:S(2)}, u32[]{:S(2)}) async-start(bf16[4,128,2060]{1,2,0:T(8,128)(2,1)} %broadcast_in_dim.11), calls=%async_computation.3 | async-start | bytes 4227072 | tf_op jit(solution)/shard_map/all_to_all | solution.py:115
  82.4 34.7 %copy-start.66 = (bf16[512,12]{0,1:T(8,128)(2,1)}, bf16[512,12]{0,1:T(8,128)(2,1)S(1)}, u32[]{:S(2)}) copy-start(bf16[512,12]{0,1:T(8,128)(2,1)S(1)} %reshape.368) | copy-start | bytes 36868
  82.4 21.4 %copy-start.78 = (f32[1,512]{1,0:T(1,128)}, f32[1,512]{1,0:T(1,128)S(1)}, u32[]{:S(2)}) copy-start(f32[1,512]{1,0:T(1,128)S(1)} %get-tuple-element.143) | copy-start | bytes 6148
  107.3 20.5 %all-to-all-start.1 = ((bf16[4,2,152,512]{3,2,1,0:T(8,128)(2,1)}), bf16[4,2,152,512]{3,2,1,0:T(8,128)(2,1)}, u32[]{:S(2)}, u32[]{:S(2)}) async-start(bf16[4,2,152,512]{3,2,1,0:T(8,128)(2,1)} %bitcast.331), calls=%async_computation.1 | async-start | bytes 2490368 | tf_op jit(solution)/shard_map/all_to_all | solution.py:115
  144.7 19.5 %all-to-all-start.2 = ((bf16[4,2,152,512]{3,2,1,0:T(8,128)(2,1)}), bf16[4,2,152,512]{3,2,1,0:T(8,128)(2,1)}, u32[]{:S(2)}, u32[]{:S(2)}) async-start(bf16[4,2,152,512]{3,2,1,0:T(8,128)(2,1)} %copy.441), calls=%async_computation.2 | async-start | bytes 2490368 | tf_op jit(solution)/shard_map/all_to_all | solution.py:115
  149.6 17.0 %copy-start.85 = (f32[394]{0:T(512)}, f32[394]{0:T(512)S(1)}, u32[]{:S(2)}) copy-start(f32[394]{0:T(512)S(1)} %get-tuple-element.20) | copy-start | bytes 4732
  149.6 17.0 %copy-start.87 = (f32[394]{0:T(512)}, f32[394]{0:T(512)S(1)}, u32[]{:S(2)}) copy-start(f32[394]{0:T(512)S(1)} %get-tuple-element.19) | copy-start | bytes 4732
  154.8 15.7 %copy-start.80 = (f32[1,512]{1,0:T(1,128)}, f32[1,512]{1,0:T(1,128)S(1)}, u32[]{:S(2)}) copy-start(f32[1,512]{1,0:T(1,128)S(1)} %get-tuple-element.180) | copy-start | bytes 6148
  154.8 166.9 %copy-start.75 = (f32[1,512]{1,0:T(1,128)}, f32[1,512]{1,0:T(1,128)S(1)}, u32[]{:S(2)}) copy-start(f32[1,512]{1,0:T(1,128)S(1)} %get-tuple-element.138) | copy-start | bytes 6148
  170.2 151.5 %copy-start.65 = (f32[394]{0:T(512)}, f32[394]{0:T(512)S(1)}, u32[]{:S(2)}) copy-start(f32[394]{0:T(512)S(1)} %broadcast_multiply_fusion.10) | copy-start | bytes 4732
  170.5 151.2 %copy-start.70 = (f32[394]{0:T(512)}, f32[394]{0:T(512)S(1)}, u32[]{:S(2)}) copy-start(f32[394]{0:T(512)S(1)} %add_rsqrt_fusion.2) | copy-start | bytes 4732
  203.2 19.7 %all-to-all-start.4 = ((bf16[4,2,152,512]{3,2,1,0:T(8,128)(2,1)}), bf16[4,2,152,512]{3,2,1,0:T(8,128)(2,1)}, u32[]{:S(2)}, u32[]{:S(2)}) async-start(bf16[4,2,152,512]{3,2,1,0:T(8,128)(2,1)} %bitcast.330), calls=%async_computation.4 | async-start | bytes 2490368 | tf_op jit(solution)/shard_map/all_to_all | solution.py:115
  222.9 22.9 %all-to-all-start.6 = ((bf16[4,2,152,512]{3,2,1,0:T(8,128)(2,1)}), bf16[4,2,152,512]{3,2,1,0:T(8,128)(2,1)}, u32[]{:S(2)}, u32[]{:S(2)}) async-start(bf16[4,2,152,512]{3,2,1,0:T(8,128)(2,1)} %bitcast.328), calls=%async_computation.6 | async-start | bytes 2490368 | tf_op jit(solution)/shard_map/all_to_all | solution.py:115
  245.8 12.7 %copy-start.110 = (f32[4,2,152]{2,1,0:T(2,128)}, f32[4,2,152]{2,1,0:T(2,128)S(1)}, u32[]{:S(2)}) copy-start(f32[4,2,152]{2,1,0:T(2,128)S(1)} %fusion.223) | copy-start | bytes 14596
  245.8 19.6 %all-to-all-start.5 = ((bf16[4,2,152,512]{3,2,1,0:T(8,128)(2,1)}), bf16[4,2,152,512]{3,2,1,0:T(8,128)(2,1)}, u32[]{:S(2)}, u32[]{:S(2)}) async-start(bf16[4,2,152,512]{3,2,1,0:T(8,128)(2,1)} %copy.457), calls=%async_computation.5 | async-start | bytes 2490368 | tf_op jit(solution)/shard_map/all_to_all | solution.py:115
  250.1 8.3 %copy-start.108 = (bf16[1,2,512,2048]{3,2,1,0:T(8,128)(2,1)S(1)}, bf16[1,2,512,2048]{3,2,1,0:T(8,128)(2,1)}, u32[]{:S(2)}) copy-start(bf16[1,2,512,2048]{3,2,1,0:T(8,128)(2,1)} %all-gather.17.cloned.1.call-done) | copy-start | bytes 12582916
  265.4 19.8 %all-to-all-start.7 = ((bf16[4,2,152,512]{3,2,1,0:T(8,128)(2,1)}), bf16[4,2,152,512]{3,2,1,0:T(8,128)(2,1)}, u32[]{:S(2)}, u32[]{:S(2)}) async-start(bf16[4,2,152,512]{3,2,1,0:T(8,128)(2,1)} %copy.460), calls=%async_computation.7 | async-start | bytes 2490368 | tf_op jit(solution)/shard_map/all_to_all | solution.py:115
  270.0 8.3 %copy-start.104 = (s32[394]{0:T(512)S(1)}, s32[394]{0:T(512)}, u32[]{:S(2)}) copy-start(s32[394]{0:T(512)} %copy-done.103) | copy-start | bytes 4732
  325.6 29.4 %all-to-all-start.8 = ((bf16[4,2,152,512]{3,2,1,0:T(8,128)(2,1)}), bf16[4,2,152,512]{3,2,1,0:T(8,128)(2,1)}, u32[]{:S(2)}, u32[]{:S(2)}) async-start(bf16[4,2,152,512]{3,2,1,0:T(8,128)(2,1)} %bitcast.329), calls=%async_computation.8 | async-start | bytes 2490368 | tf_op jit(solution)/shard_map/all_to_all | solution.py:115
  354.9 8.7 %copy-start.107 = (bf16[1,2,512,2048]{3,2,1,0:T(8,128)(2,1)S(1)}, bf16[1,2,512,2048]{3,2,1,0:T(8,128)(2,1)}, u32[]{:S(2)}) copy-start(bf16[1,2,512,2048]{3,2,1,0:T(8,128)(2,1)} %all-gather.13.cloned.1.call-done) | copy-start | bytes 12582916
  367.6 19.7 %all-to-all-start.9 = ((bf16[4,2,152,512]{3,2,1,0:T(8,128)(2,1)}), bf16[4,2,152,512]{3,2,1,0:T(8,128)(2,1)}, u32[]{:S(2)}, u32[]{:S(2)}) async-start(bf16[4,2,152,512]{3,2,1,0:T(8,128)(2,1)} %copy.475), calls=%async_computation.9 | async-start | bytes 2490368 | tf_op jit(solution)/shard_map/all_to_all | solution.py:115
  380.2 11.8 %copy-start.91 = (s32[394]{0:T(512)S(1)}, s32[394]{0:T(512)}, u32[]{:S(2)}) copy-start(s32[394]{0:T(512)} %copy-done.89) | copy-start | bytes 4732
  380.2 11.8 %copy-start.102 = (s32[394]{0:T(512)S(1)}, s32[394]{0:T(512)}, u32[]{:S(2)}) copy-start(s32[394]{0:T(512)} %copy-done.100) | copy-start | bytes 4732
  387.2 48.5 %all-to-all-start.11 = ((bf16[4,8,16,2060]{3,2,1,0:T(8,128)(2,1)}), bf16[4,8,16,2060]{3,2,1,0:T(8,128)(2,1)}, u32[]{:S(2)}, u32[]{:S(2)}) async-start(bf16[4,8,16,2060]{3,2,1,0:T(8,128)(2,1)} %bitcast.309), calls=%async_computation.11 | async-start | bytes 4456448 | tf_op jit(solution)/shard_map/all_to_all | solution.py:115
  435.7 29.4 %all-to-all-start.10 = ((bf16[4,8,16,2060]{3,2,1,0:T(8,128)(2,1)}), bf16[4,8,16,2060]{3,2,1,0:T(8,128)(2,1)S(1)}, u32[]{:S(2)}, u32[]{:S(2)}) async-start(bf16[4,8,16,2060]{3,2,1,0:T(8,128)(2,1)} %bitcast.308), calls=%async_computation.10 | async-start | bytes 4456448 | tf_op jit(solution)/shard_map/all_to_all | solution.py:115
  439.9 60.5 %reduce-scatter.6.cloned.1.call-start = ((), (), s32[]{:S(2)}) async-start(), calls=%async_computation.18 | async-start | bytes 1253376 | tf_op jit(solution)/shard_map/reduce_scatter | solution.py:344
  443.1 25.8 %copy-start.111 = (f32[4,2,152]{2,1,0:T(2,128)S(1)}, f32[4,2,152]{2,1,0:T(2,128)}, u32[]{:S(2)}) copy-start(f32[4,2,152]{2,1,0:T(2,128)} %copy-done.110) | copy-start | bytes 14596
  468.8 82.5 %reduce-scatter.14.cloned.1.call-start = ((), (), s32[]{:S(2)}) async-start(), calls=%async_computation.22 | async-start | bytes 4718592 | tf_op jit(solution)/shard_map/reduce_scatter | solution.py:189
  477.2 124.8 %reduce-scatter.12.cloned.1.call-start = ((), (), s32[]{:S(2)}) async-start(), calls=%async_computation.21 | async-start | bytes 4718592 | tf_op jit(solution)/shard_map/reduce_scatter | solution.py:189
  485.6 167.1 %reduce-scatter.10.cloned.1.call-start = ((), (), s32[]{:S(2)}) async-start(), calls=%async_computation.20 | async-start | bytes 4718592 | tf_op jit(solution)/shard_map/reduce_scatter | solution.py:202
  486.4 216.9 %reduce-scatter.8.cloned.1.call-start = ((), (), s32[]{:S(2)}) async-start(), calls=%async_computation.19 | async-start | bytes 4718592 | tf_op jit(solution)/shard_map/reduce_scatter | solution.py:202
  (90 other events, 249.1 us)
Sparse Core Ops, SparseCore 0:
  11.7 25.2 all-gather.10
  39.2 47.5 all-gather.12
  88.4 45.0 all-gather.14
  134.9 46.6 all-gather.16
  183.0 45.0 all-gather.18
  468.9 31.4 reduce-scatter.5
  502.7 48.4 reduce-scatter.13
  553.5 48.3 reduce-scatter.11
  604.3 48.3 reduce-scatter.9
  654.8 48.3 reduce-scatter.7

commit v4 on v3

--- a/solution.py
+++ b/solution.py
@@ -1,12 +1,16 @@
 import jax
 import jax.numpy as jnp
 from jax import lax
+from jax.experimental import pallas as pl
 from jax.sharding import PartitionSpec as P
 
 HEADS = 8
 HEAD_DIM = 64
 SEQ = 197
+SEQ_PAD = 208
 LAYERS = 2
+ROW_DOTS = (((1,), (1,)), ((), ()))
+COL_DOTS = (((0,), (0,)), ((), ()))
 
 
 EPSILON = 1e-06
@@ -115,24 +119,112 @@
     return lax.all_to_all(block, "expert", split_axis=0, concat_axis=0, tiled=True)
 
 
+def head_of(ref, part, head):
+    start = part * HEADS * HEAD_DIM + head * HEAD_DIM
+    return ref[:, start : start + HEAD_DIM]
+
+
+def masked_scores(query, keyed):
+    scores = lax.dot_general(query, keyed, ROW_DOTS, preferred_element_type=jnp.float32)
+    columns = lax.broadcasted_iota(jnp.int32, scores.shape, 1)
+    return jnp.where(columns < SEQ, scores, -1e30)
+
+
+def attention_kernel(packed_ref, mixed_ref, total_ref):
+    scale = jnp.asarray(HEAD_DIM ** (-0.5), jnp.bfloat16)
+    mixed, totals = [], []
+    for head in range(HEADS):
+        query = head_of(packed_ref, 0, head) * scale
+        scores = masked_scores(query, head_of(packed_ref, 1, head))
+        highest = jnp.max(scores, axis=-1, keepdims=True)
+        powers = jnp.exp(scores - highest)
+        row_total = jnp.sum(powers, axis=-1, keepdims=True)
+        probs = (powers * (1.0 / row_total)).astype(jnp.bfloat16)
+        mixed.append(
+            jnp.dot(
+                probs, head_of(packed_ref, 2, head), preferred_element_type=jnp.float32
+            ).astype(jnp.bfloat16)
+        )
+        totals.append(highest + jnp.log(row_total))
+    mixed_ref[...] = jnp.concatenate(mixed, axis=1)
+    total_ref[...] = jnp.concatenate(totals, axis=1)
+
+
+def attention_back_kernel(packed_ref, grad_ref, total_ref, out_ref):
+    scale = jnp.asarray(HEAD_DIM ** (-0.5), jnp.bfloat16)
+    queries, keys, values = [], [], []
+    for head in range(HEADS):
+        query = head_of(packed_ref, 0, head) * scale
+        keyed = head_of(packed_ref, 1, head)
+        grad_mixed = head_of(grad_ref, 0, head)
+        scores = masked_scores(query, keyed)
+        probs = jnp.exp(scores - total_ref[:, head : head + 1])
+        grad_probs = lax.dot_general(
+            grad_mixed,
+            head_of(packed_ref, 2, head),
+            ROW_DOTS,
+            preferred_element_type=jnp.float32,
+        )
+        values.append(
+            lax.dot_general(
+                probs.astype(jnp.bfloat16),
+                grad_mixed,
+                COL_DOTS,
+                preferred_element_type=jnp.float32,
+            ).astype(jnp.bfloat16)
+        )
+        row_inner = jnp.sum(probs * grad_probs, axis=-1, keepdims=True)
+        grad_scores = (probs * (grad_probs - row_inner)).astype(jnp.bfloat16)
+        grad_query = jnp.dot(grad_scores, keyed, preferred_element_type=jnp.float32)
+        queries.append(grad_query.astype(jnp.bfloat16) * scale)
+        keys.append(
+            lax.dot_general(
+                grad_scores, query, COL_DOTS, preferred_element_type=jnp.float32
+            ).astype(jnp.bfloat16)
+        )
+    out_ref[...] = jnp.concatenate(queries + keys + values, axis=1)
+
+
+def image_block(columns):
+    return pl.BlockSpec((SEQ_PAD, columns), lambda image: (image, 0))
+
+
+def attention(packed):
+    rows, columns = packed.shape
+    width = columns // 3
+    return pl.pallas_call(
+        attention_kernel,
+        grid=(rows // SEQ_PAD,),
+        in_specs=[image_block(columns)],
+        out_specs=[image_block(width), image_block(HEADS)],
+        out_shape=[
+            jax.ShapeDtypeStruct((rows, width), jnp.bfloat16),
+            jax.ShapeDtypeStruct((rows, HEADS), jnp.float32),
+        ],
+        name="attention",
+    )(packed)
+
+
+def attention_back(packed, grad_mixed, totals):
+    rows, columns = packed.shape
+    return pl.pallas_call(
+        attention_back_kernel,
+        grid=(rows // SEQ_PAD,),
+        in_specs=[image_block(columns), image_block(columns // 3), image_block(HEADS)],
+        out_specs=image_block(columns),
+        out_shape=jax.ShapeDtypeStruct((rows, columns), jnp.bfloat16),
+        name="attention_back",
+    )(packed, grad_mixed, totals)
+
+
 def attend_forward(resid, dense, tables):
     qkv_full, proj_full, router_full, gains_wide, shifts_wide = dense
     pick_first_f, pick_second_f, _, _ = tables
-    tok_count, width = resid.shape
-    images = tok_count // SEQ
     attn_norm, unit_a, inv_a = layer_norm(resid, gains_wide[0], shifts_wide[0])
     attn_in = attn_norm.astype(jnp.bfloat16)
     packed = jnp.dot(attn_in, qkv_full, preferred_element_type=jnp.float32)
-    head_shape = (images, SEQ, HEADS, HEAD_DIM)
-    query = (packed[:, :width] * HEAD_DIM ** (-0.5)).astype(jnp.bfloat16).reshape(head_shape)
-    keyed = packed[:, width : 2 * width].astype(jnp.bfloat16).reshape(head_shape)
-    valued = packed[:, 2 * width :].astype(jnp.bfloat16).reshape(head_shape)
-    scores = jnp.einsum("iqhd,ikhd->ihqk", query, keyed, preferred_element_type=jnp.float32)
-    probs, log_total = softmax_rows(scores)
-    mixed = jnp.einsum(
-        "ihqk,ikhd->iqhd", probs.astype(jnp.bfloat16), valued, preferred_element_type=jnp.float32
-    )
-    mixed = mixed.reshape(tok_count, width).astype(jnp.bfloat16)
+    packed = packed.astype(jnp.bfloat16)
+    mixed, totals = attention(packed)
     resid_mid = resid + jnp.dot(mixed, proj_full, preferred_element_type=jnp.float32)
     moe_norm, unit_b, inv_b = layer_norm(resid_mid, gains_wide[1], shifts_wide[1])
     moe_in = moe_norm.astype(jnp.bfloat16)
@@ -143,7 +235,7 @@
     router_probs, gate_first, gate_second = lax.optimization_barrier(
         (router_probs, gate_first, gate_second)
     )
-    attn_saved = (unit_a, inv_a, attn_in, query, keyed, valued, log_total, mixed)
+    attn_saved = (unit_a, inv_a, attn_in, packed, totals, mixed)
     moe_saved = (unit_b, inv_b, moe_in, router_probs, gate_first, gate_second)
     return (resid_mid, attn_saved, moe_saved)
 
@@ -206,10 +298,9 @@
 def tokens_backward(grad_out, grad_back, backs, dense, tables, attn_saved, moe_saved):
     qkv_full, proj_full, router_full, gains_wide, _ = dense
     pick_first_f, pick_second_f, place_first, place_second = tables
-    unit_a, inv_a, attn_in, query, keyed, valued, log_total, mixed = attn_saved
+    unit_a, inv_a, attn_in, packed, totals, mixed = attn_saved
     unit_b, inv_b, moe_in, router_probs, _, _ = moe_saved
-    tok_count, width = grad_out.shape
-    images = tok_count // SEQ
+    width = grad_out.shape[1]
     grad_gate_first = jnp.sum(grad_out * backs[0], axis=1)
     grad_gate_second = jnp.sum(grad_out * backs[1], axis=1)
     grad_back = grad_back.reshape(-1, width)
@@ -226,35 +317,7 @@
     grad_branch = grad_mid.astype(jnp.bfloat16)
     grad_proj = jnp.einsum("td,te->de", mixed, grad_branch, preferred_element_type=jnp.float32)
     grad_mixed = jnp.einsum("te,de->td", grad_branch, proj_full, preferred_element_type=jnp.float32)
-    grad_mixed = grad_mixed.astype(jnp.bfloat16).reshape(images, SEQ, HEADS, HEAD_DIM)
-    scores = jnp.einsum("iqhd,ikhd->ihqk", query, keyed, preferred_element_type=jnp.float32)
-    probs = jnp.exp(scores - log_total)
-    grad_weights = jnp.einsum(
-        "iqhd,ikhd->ihqk", grad_mixed, valued, preferred_element_type=jnp.float32
-    )
-    grad_valued = jnp.einsum(
-        "ihqk,iqhd->ikhd",
-        probs.astype(jnp.bfloat16),
-        grad_mixed,
-        preferred_element_type=jnp.float32,
-    ).astype(jnp.bfloat16)
-    row_inner = jnp.sum(probs * grad_weights, axis=-1, keepdims=True)
-    grad_scores = (probs * (grad_weights - row_inner)).astype(jnp.bfloat16)
-    grad_query = jnp.einsum(
-        "ihqk,ikhd->iqhd", grad_scores, keyed, preferred_element_type=jnp.float32
-    ).astype(jnp.bfloat16)
-    grad_query = grad_query * jnp.asarray(HEAD_DIM ** (-0.5), jnp.bfloat16)
-    grad_keyed = jnp.einsum(
-        "ihqk,iqhd->ikhd", grad_scores, query, preferred_element_type=jnp.float32
-    ).astype(jnp.bfloat16)
-    grad_packed = jnp.concatenate(
-        [
-            grad_query.reshape(tok_count, width),
-            grad_keyed.reshape(tok_count, width),
-            grad_valued.reshape(tok_count, width),
-        ],
-        axis=1,
-    )
+    grad_packed = attention_back(packed, grad_mixed.astype(jnp.bfloat16), totals)
     grad_qkv = jnp.einsum("td,te->de", attn_in, grad_packed, preferred_element_type=jnp.float32)
     grad_attn = jnp.einsum("te,de->td", grad_packed, qkv_full, preferred_element_type=jnp.float32)
     grad_norm_a, gain_a_grad, shift_a_grad = norm_back(grad_attn, unit_a, inv_a, gains_wide[0])
@@ -287,17 +350,19 @@
     peers = lax.axis_size("expert")
     capacity = -(-max(2, 3 * tok_count // experts_total) // 8) * 8
     block_shape = (peers, experts_total // peers, capacity, width)
-    resid = embedded.reshape(tok_count, width).astype(jnp.float32)
-    grad = cotangent.reshape(tok_count, width).astype(jnp.float32)
+    fill = ((0, 0), (0, SEQ_PAD - length), (0, 0))
+    rows = images * SEQ_PAD
+    cot_low = jnp.pad(cotangent, fill).reshape(rows, width)
+    resid = jnp.pad(embedded, fill).reshape(rows, width).astype(jnp.float32)
+    grad = cot_low.astype(jnp.float32)
     dense, experts, tables = [], [], []
     quarters = gather_quarters(w_qkv, w_proj, w_router, norm_gains, norm_shifts)
     for which in range(LAYERS):
         experts.append(gather_experts(which, w_first, w_second))
-        tables.append(
-            route_tables(routes[which].reshape(tok_count, 2), experts_total, capacity)
-        )
+        route = jnp.pad(routes[which], fill, constant_values=experts_total).reshape(rows, 2)
+        tables.append(route_tables(route, experts_total, capacity))
     last = tables[LAYERS - 1]
-    slots = slots_of(cotangent.reshape(tok_count, width), last[2] + last[3], block_shape)
+    slots = slots_of(cot_low, last[2] + last[3], block_shape)
     cot_rows = exchange(slots)
     for which in range(LAYERS):
         dense.append(spread_dense(quarters[which], experts_total))
@@ -321,7 +386,7 @@
         attn_saved.append(attn_part)
         moe_saved.append(moe_part)
         kept.append((incoming, hidden_pre, hidden_act, backs))
-    out_images = resid.reshape(images, length, width).astype(jnp.bfloat16)
+    out_images = resid.reshape(images, SEQ_PAD, width)[:, :length].astype(jnp.bfloat16)
     smalls, firsts, seconds = [None] * LAYERS, [None] * LAYERS, [None] * LAYERS
     for which in reversed(range(LAYERS)):
         incoming, hidden_pre, hidden_act, backs = kept[which]
@@ -344,7 +409,7 @@
     both = lax.psum_scatter(both, "dp", scatter_dimension=0, tiled=True)[0]
     total = lax.all_gather(both, "expert", axis=0, tiled=True)
     total = total.swapaxes(0, 1).astype(jnp.float32)
-    grad_images = grad.reshape(images, length, width)
+    grad_images = grad.reshape(images, SEQ_PAD, width)[:, :length]
     wide = total[:, :, 4 * width :]
     return (
         out_images,

time: 721 us -> 676 us (0.938)
  local copies, waits for them, and re-layouts: 149 us -> 72 us
  waiting for transfers between devices: 294 us -> 328 us
  Pallas kernels: 0 us -> 30.5 us
  matrix products: 162 us -> 138 us
  other arithmetic: 27.3 us -> 19 us
    reshape x25 -> x3, local copies, waits for them, and re-layouts: 42.7 us -> 0.18 us  [the longest x2 0.18 us: whole_step(): jnp.pad(routes[which], fill, constant_values=experts_total).reshape(rows, 2)]
    pallas_call x0 -> x4, Pallas kernels: none -> 30.5 us  [the longest x2 17.8 us: attention_back(): pl.pallas_call(attention_back_kernel, grid=(rows // SEQ_PAD,), in_specs=[...]
    dot_general x12 -> x0, matrix products: 17 us -> none  [the longest x2 4.65 us: tokens_backward(): jnp.einsum('ihqk,iqhd->ikhd', probs.astype(jnp.bfloat16), grad_mixed, pre...]
    all_gather x2, waiting for transfers between devices: 0.01 us -> 15 us  [gather_experts(): second_full = lax.all_gather(w_second[which], 'dp', axis=1, tiled=True)]
    all_to_all x12, waiting for transfers between devices: 84.5 us -> 99.4 us  [exchange(): lax.all_to_all(block, 'expert', split_axis=0, concat_axis=0, tiled=True)]
    convert_element_type x13 -> x0, local copies, waits for them, and re-layouts: 13.9 us -> none  [the longest x4 6.96 us: attend_forward(): mixed = mixed.reshape(tok_count, width).astype(jnp.bfloat16)]
    unnamed x243 -> x154, local copies, waits for them, and re-layouts: 21.9 us -> 9.96 us
  transfers between devices with their start and end apart: 22 -> 22, of which waited for: 14 -> 16; matrix products, arithmetic and copies ran while one was open for 38% -> 29% of each run, Pallas kernels for 0% -> 3%
where the time goes in v4:
time: 676 us; the launch traced here: 667 us
  waiting for transfers between devices  328 us (49%)
  matrix products  138 us (20%)
  local copies, waits for them, and re-layouts  72 us (11%)
  starting transfers between devices  53.4 us (8%)
  Pallas kernels  30.5 us (5%)
  other arithmetic  19 us (3%)
  between operations  15.8 us (2%)
  blocking collectives  10.3 us (2%)
    all_to_all x12, waiting for transfers between devices, exchange(): lax.all_to_all(block, 'expert', split_axis=0, concat_axis=0, tiled=True)  99.4 us
    reduce_scatter x2, waiting for transfers between devices, experts_backward(): lax.psum_scatter(grad_first, 'dp', scatter_dimension=2, tiled=True)  98.6 us
    reduce_scatter x2, waiting for transfers between devices, experts_backward(): lax.psum_scatter(grad_second, 'dp', scatter_dimension=1, tiled=True)  85.3 us
    all_to_all x12, starting transfers between devices, exchange(): lax.all_to_all(block, 'expert', split_axis=0, concat_axis=0, tiled=True)  52.7 us
    dot_general x2, matrix products, experts_hidden(): jnp.einsum('sjcd,jdf->sjcf', incoming, first_full, preferred_element_type...  18.2 us
    pallas_call x2, Pallas kernels, attention_back(): pl.pallas_call(attention_back_kernel, grid=(rows // SEQ_PAD,), in_specs=[...  17.8 us
    all_gather x1, waiting for transfers between devices, gather_quarters(): return lax.all_gather(packed, 'dp', axis=1, tiled=True)  17.4 us
    dot_general x2, matrix products, experts_backward(): jnp.einsum('sjcd,jfd->sjcf', grad_result, second_full, preferred_element_...  17 us
  transfers between devices with their start and end apart: 22, of which 16 were waited for; matrix products, arithmetic and copies ran while one was open for 29% of the time, Pallas kernels for 3%

profile of v4, /device:TPU:0, one launch (start us, length us, event | category | flops | bytes accessed | tf_op | source)
XLA Modules:
  0.0 666.9 jit_solution(9186128653651327603)
XLA Ops:
  19.6 17.4 %all-gather.11.cloned.1.call-done = bf16[2,128,2060]{2,1,0:T(8,128)(2,1)} async-done(((bf16[2,16,2060]{2,1,0:T(8,128)(2,1)}), bf16[2,128,2060]{2,1,0:T(8,128)(2,1)}) %all-gather.11.cloned.1.call-update) | async-done | bytes 1054736 | tf_op jit(solution)/shard_map/all_gather | solution.py:63
  41.0 3.6 all-to-all-start
  48.5 21.8 %all-to-all-done = bf16[4,128,2060]{1,2,0:T(8,128)(2,1)S(1)} async-done(((bf16[4,128,2060]{1,2,0:T(8,128)(2,1)}), bf16[4,128,2060]{1,2,0:T(8,128)(2,1)S(1)}, u32[]{:S(2)}, u32[]{:S(2)}) %all-to-all-start) | async-done | bytes 2109472 | tf_op jit(solution)/shard_map/all_to_all | solution.py:119
  73.3 4.4 all-to-all-start.3
  90.2 6.3 attention.2
  102.7 4.8 all-to-all-start.1
  113.2 9.6 %all-to-all-done.1 = bf16[4,2,152,512]{3,2,1,0:T(8,128)(2,1)} async-done(((bf16[4,2,152,512]{3,2,1,0:T(8,128)(2,1)}), bf16[4,2,152,512]{3,2,1,0:T(8,128)(2,1)}, u32[]{:S(2)}, u32[]{:S(2)}) %all-to-all-start.1) | async-done | bytes 1245216 | tf_op jit(solution)/shard_map/all_to_all | solution.py:119
  122.8 9.1 %fusion.19 = (bf16[4,2,152,2048]{3,2,0,1:T(8,128)(2,1)}, f32[2,4,152,2048]{3,2,1,0:T(8,128)}) fusion(bf16[1,2,512,2048]{3,2,1,0:T(8,128)(2,1)} %all-gather.13.cloned.1.call-done, bf16[4,2,152,512]{3,2,1,0:T(8,128)(2,1)} %all-to-all-done.1), kind=kOutput, calls=%fused_computation.25 | convolution fusion | flops 2562588672 | bytes 20381696 | tf_op jit(solution)/shard_map/sjcd,jdf->sjcf/dot_general | solution.py:260
  132.7 6.4 fusion.69
  140.2 4.3 all-to-all-start.2
  148.0 13.0 %all-to-all-done.2 = bf16[4,2,152,512]{3,2,1,0:T(8,128)(2,1)} async-done(((bf16[4,2,152,512]{3,2,1,0:T(8,128)(2,1)}), bf16[4,2,152,512]{3,2,1,0:T(8,128)(2,1)}, u32[]{:S(2)}, u32[]{:S(2)}) %all-to-all-start.2) | async-done | bytes 1245216 | tf_op jit(solution)/shard_map/all_to_all | solution.py:119
  163.4 3.7 fusion.165
  169.3 6.3 attention.3
  179.6 4.3 all-to-all-start.4
  187.7 11.8 %all-to-all-done.4 = bf16[4,2,152,512]{3,2,1,0:T(8,128)(2,1)} async-done(((bf16[4,2,152,512]{3,2,1,0:T(8,128)(2,1)}), bf16[4,2,152,512]{3,2,1,0:T(8,128)(2,1)}, u32[]{:S(2)}, u32[]{:S(2)}) %all-to-all-start.4) | async-done | bytes 1245216 | tf_op jit(solution)/shard_map/all_to_all | solution.py:119
  199.5 4.5 all-to-all-start.6
  204.0 9.1 %fusion.15 = (bf16[4,2,152,2048]{3,2,0,1:T(8,128)(2,1)}, f32[2,4,152,2048]{3,2,1,0:T(8,128)}) fusion(bf16[1,2,512,2048]{3,2,1,0:T(8,128)(2,1)} %all-gather.17.cloned.1.call-done, bf16[4,2,152,512]{3,2,1,0:T(8,128)(2,1)} %all-to-all-done.4), kind=kOutput, calls=%fused_computation.19 | convolution fusion | flops 2562588672 | bytes 20381696 | tf_op jit(solution)/shard_map/sjcd,jdf->sjcf/dot_general | solution.py:260
  213.1 14.2 %all-gather.19.cloned.1.call-done = bf16[1,2,2048,512]{3,2,1,0:T(8,128)(2,1)} async-done(((bf16[1,2,256,512]{3,2,1,0:T(8,128)(2,1)}), bf16[1,2,2048,512]{3,2,1,0:T(8,128)(2,1)}) %all-gather.19.cloned.1.call-update) | async-done | bytes 4194320 | tf_op jit(solution)/shard_map/all_gather | solution.py:95
  227.3 6.4 fusion.75
  236.7 4.3 all-to-all-start.5
  241.0 8.3 %fusion.7 = bf16[4,2,152,2048]{3,2,0,1:T(8,128)(2,1)S(1)} fusion(f32[2,4,152,2048]{3,2,1,0:T(8,128)} %get-tuple-element.161, bf16[1,2,2048,512]{3,2,1,0:T(8,128)(2,1)} %all-gather.19.cloned.1.call-done, bf16[4,2,152,512]{3,2,1,0:T(8,128)(2,1)} %all-to-all-done.6, f32[4,2,152]{2,1,0:T(2,128)S(1)} %fusion.179), kind=kOutput, calls=%fused_computation.9 | convolution fusion | flops 2576908288 | bytes 20386560 | tf_op jit(solution)/shard_map/sjcd,jfd->sjcf/dot_general | solution.py:282
  253.3 6.4 bitcast_convert_fusion.3
  259.6 4.5 all-to-all-start.7
  266.5 3.3 fusion.113
  269.8 10.8 %all-to-all-done.7 = bf16[4,2,152,512]{3,2,1,0:T(8,128)(2,1)} async-done(((bf16[4,2,152,512]{3,2,1,0:T(8,128)(2,1)}), bf16[4,2,152,512]{3,2,1,0:T(8,128)(2,1)}, u32[]{:S(2)}, u32[]{:S(2)}) %all-to-all-start.7) | async-done | bytes 1245216 | tf_op jit(solution)/shard_map/all_to_all | solution.py:119
  285.4 8.9 %attention_back.2 = bf16[416,1536]{1,0:T(8,128)(2,1)} custom-call(bf16[416,1536]{1,0:T(8,128)(2,1)} %convolution_convert_fusion.5.packed_ref, bf16[416,512]{1,0:T(8,128)(2,1)} %convolution_convert_fusion.10.grad_ref, f32[416,8]{1,0:T(8,128)} %get-tuple-element.31.total_ref), custom_call_target="tpu_custom_call" | custom-call | tf_op jit(solution)/shard_map/attention_back/pallas_call | solution.py:210
  294.3 3.6 multiply_reduce_fusion.1
  301.4 4.8 all-to-all-start.8
  318.2 3.6 convolution_convert_fusion
  321.9 3.6 concatenate.13
  327.0 8.7 %fusion.13 = bf16[4,2,152,2048]{3,2,0,1:T(8,128)(2,1)S(1)} fusion(f32[2,4,152,2048]{3,2,1,0:T(8,128)} %get-tuple-element.154, bf16[1,2,2048,512]{3,2,1,0:T(8,128)(2,1)} %all-gather.15.cloned.1.call-done, bf16[4,2,152,512]{3,2,1,0:T(8,128)(2,1)} %all-to-all-done.8), kind=kOutput, calls=%fused_computation.15 | convolution fusion | flops 2575040512 | bytes 20381696 | tf_op jit(solution)/shard_map/sjcd,jfd->sjcf/dot_general | solution.py:282
  339.7 4.2 all-to-all-start.9
  343.8 8.3 %bitcast_convert_fusion.2 = bf16[2,512,2048]{2,1,0:T(8,128)(2,1)} fusion(bf16[4,2,152,512]{3,2,1,0:T(8,128)(2,1)} %all-to-all-done.1, bf16[4,2,152,2048]{3,2,0,1:T(8,128)(2,1)} %copy-done.70), kind=kOutput, calls=%fused_computation.30 | convolution fusion | flops 2552233984 | bytes 10420224 | tf_op jit(solution)/shard_map/sjcd,sjcf->jdf/dot_general | solution.py:290
  352.1 6.7 %all-to-all-done.9 = bf16[4,2,152,512]{3,2,1,0:T(8,128)(2,1)S(1)} async-done(((bf16[4,2,152,512]{3,2,1,0:T(8,128)(2,1)}), bf16[4,2,152,512]{3,2,1,0:T(8,128)(2,1)S(1)}, u32[]{:S(2)}, u32[]{:S(2)}) %all-to-all-start.9) | async-done | bytes 1245216 | tf_op jit(solution)/shard_map/all_to_all | solution.py:119
  358.8 4.7 all-to-all-start.11
  367.1 8.9 %attention_back.3 = bf16[416,1536]{1,0:T(8,128)(2,1)} custom-call(bf16[416,1536]{1,0:T(8,128)(2,1)} %convolution_convert_fusion.6.packed_ref, bf16[416,512]{1,0:T(8,128)(2,1)} %convolution_convert_fusion.9.grad_ref, f32[416,8]{1,0:T(8,128)} %get-tuple-element.34.total_ref), custom_call_target="tpu_custom_call" | custom-call | tf_op jit(solution)/shard_map/attention_back/pallas_call | solution.py:210
  376.1 3.3 multiply_reduce_fusion.3
  382.7 4.4 concatenate.12
  390.3 4.5 all-to-all-start.10
  396.8 23.8 %all-to-all-done.10 = bf16[4,8,16,2060]{3,2,1,0:T(8,128)(2,1)} async-done(((bf16[4,8,16,2060]{3,2,1,0:T(8,128)(2,1)}), bf16[4,8,16,2060]{3,2,1,0:T(8,128)(2,1)}, u32[]{:S(2)}, u32[]{:S(2)}) %all-to-all-start.10) | async-done | bytes 2109472 | tf_op jit(solution)/shard_map/all_to_all | solution.py:119
  424.0 8.3 %bitcast_convert_fusion = bf16[2,2048,512]{2,1,0:T(8,128)(2,1)} fusion(bf16[4,2,152,2048]{3,2,0,1:T(8,128)(2,1)} %get-tuple-element.160, bf16[4,2,152,512]{3,2,1,0:T(8,128)(2,1)} %all-to-all-done.6, f32[4,2,152]{2,1,0:T(2,128)S(1)} %copy-done.69), kind=kOutput, calls=%fused_computation.28 | convolution fusion | flops 2554101760 | bytes 10425088 | tf_op jit(solution)/shard_map/sjcf,sjcd->jfd/dot_general | solution.py:278
  432.4 8.2 %bitcast_convert_fusion.1 = bf16[2,2048,512]{2,1,0:T(8,128)(2,1)} fusion(bf16[4,2,152,2048]{3,2,0,1:T(8,128)(2,1)} %get-tuple-element.153, bf16[4,2,152,512]{3,2,1,0:T(8,128)(2,1)} %all-to-all-done.8), kind=kOutput, calls=%fused_computation.29 | convolution fusion | flops 2552233984 | bytes 10420224 | tf_op jit(solution)/shard_map/sjcf,sjcd->jfd/dot_general | solution.py:278
  445.4 9.4 %reduce-scatter.6.cloned.1.call-done = bf16[1,16,2,2060]{3,1,2,0:T(8,128)(2,1)} async-done(((bf16[8,16,2,2060]{3,1,2,0:T(8,128)(2,1)}), bf16[1,16,2,2060]{3,1,2,0:T(8,128)(2,1)}) %reduce-scatter.6.cloned.1.call-update) | async-done | bytes 131856 | tf_op jit(solution)/shard_map/reduce_scatter | solution.py:409
  455.8 10.3 %all-gather.4 = bf16[1,64,2,2060]{3,2,0,1:T(2,128)(2,1)S(1)} all-gather(bf16[1,16,2,2060]{3,2,0,1:T(2,128)(2,1)S(1)} %copy.268), channel_id=6, replica_groups=mesh['dp'=8,'expert'=4] {'expert'}, dimensions={1}, use_global_device_ids=true | all-gather | bytes 659200 | tf_op jit(solution)/shard_map/all_gather | solution.py:410
  470.6 34.6 %reduce-scatter.14.cloned.1.call-done = bf16[2,256,512]{2,1,0:T(8,128)(2,1)} async-done(((bf16[2,2048,512]{2,1,0:T(8,128)(2,1)}), bf16[2,256,512]{2,1,0:T(8,128)(2,1)}) %reduce-scatter.14.cloned.1.call-update) | async-done | bytes 524304 | tf_op jit(solution)/shard_map/reduce_scatter | solution.py:281
  505.2 50.7 %reduce-scatter.12.cloned.1.call-done = bf16[2,256,512]{2,1,0:T(8,128)(2,1)} async-done(((bf16[2,2048,512]{2,1,0:T(8,128)(2,1)}), bf16[2,256,512]{2,1,0:T(8,128)(2,1)}) %reduce-scatter.12.cloned.1.call-update) | async-done | bytes 524304 | tf_op jit(solution)/shard_map/reduce_scatter | solution.py:281
  558.6 48.1 %reduce-scatter.10.cloned.1.call-done = bf16[2,512,256]{2,1,0:T(8,128)(2,1)} async-done(((bf16[2,512,2048]{2,1,0:T(8,128)(2,1)}), bf16[2,512,256]{2,1,0:T(8,128)(2,1)}) %reduce-scatter.10.cloned.1.call-update) | async-done | bytes 524304 | tf_op jit(solution)/shard_map/reduce_scatter | solution.py:294
  606.6 50.6 %reduce-scatter.8.cloned.1.call-done = bf16[2,512,256]{2,1,0:T(8,128)(2,1)} async-done(((bf16[2,512,2048]{2,1,0:T(8,128)(2,1)}), bf16[2,512,256]{2,1,0:T(8,128)(2,1)}) %reduce-scatter.8.cloned.1.call-update) | async-done | bytes 524304 | tf_op jit(solution)/shard_map/reduce_scatter | solution.py:294
  (336 shorter events, 130.4 us)
Async XLA Ops:
  7.2 29.8 %all-gather.11.cloned.1.call-start = ((), (), s32[]{:S(2)}) async-start(), calls=%async_computation.17 | async-start | bytes 1253376 | tf_op jit(solution)/shard_map/all_gather | solution.py:63
  11.6 111.2 %all-gather.13.cloned.1.call-start = ((), (), s32[]{:S(2)}) async-start(), calls=%async_computation.23 | async-start | bytes 4718592 | tf_op jit(solution)/shard_map/all_gather | solution.py:94
  13.9 118.8 %all-gather.15.cloned.1.call-start = ((), (), s32[]{:S(2)}) async-start(), calls=%async_computation.24 | async-start | bytes 4718592 | tf_op jit(solution)/shard_map/all_gather | solution.py:95
  15.0 189.0 %all-gather.17.cloned.1.call-start = ((), (), s32[]{:S(2)}) async-start(), calls=%async_computation.25 | async-start | bytes 4718592 | tf_op jit(solution)/shard_map/all_gather | solution.py:94
  15.6 211.7 %all-gather.19.cloned.1.call-start = ((), (), s32[]{:S(2)}) async-start(), calls=%async_computation.26 | async-start | bytes 4718592 | tf_op jit(solution)/shard_map/all_gather | solution.py:95
  41.0 29.3 %all-to-all-start = ((bf16[4,128,2060]{1,2,0:T(8,128)(2,1)}), bf16[4,128,2060]{1,2,0:T(8,128)(2,1)S(1)}, u32[]{:S(2)}, u32[]{:S(2)}) async-start(bf16[4,128,2060]{1,2,0:T(8,128)(2,1)} %broadcast_in_dim.9), calls=%async_computation | async-start | bytes 4227072 | tf_op jit(solution)/shard_map/all_to_all | solution.py:119
  44.7 43.0 %copy-start.39 = (f32[2,208]{1,0:T(2,128)}, f32[2,208]{1,0:T(2,128)S(1)}, u32[]{:S(2)}) copy-start(f32[2,208]{1,0:T(2,128)S(1)} %broadcast_multiply_fusion.11) | copy-start | bytes 4996
  45.1 51.6 %copy-start.1 = (f32[2,208,512]{2,1,0:T(8,128)}, f32[2,208,512]{2,1,0:T(8,128)S(1)}, u32[]{:S(2)}) copy-start(f32[2,208,512]{2,1,0:T(8,128)S(1)} %pad_convert_fusion) | copy-start | bytes 2555908
  45.1 42.6 %copy-start.46 = (f32[2,208]{1,0:T(2,128)}, f32[2,208]{1,0:T(2,128)S(1)}, u32[]{:S(2)}) copy-start(f32[2,208]{1,0:T(2,128)S(1)} %add_rsqrt_fusion.3) | copy-start | bytes 4996
  73.3 29.5 %all-to-all-start.3 = ((bf16[4,128,2060]{1,2,0:T(8,128)(2,1)}), bf16[4,128,2060]{1,2,0:T(8,128)(2,1)}, u32[]{:S(2)}, u32[]{:S(2)}) async-start(bf16[4,128,2060]{1,2,0:T(8,128)(2,1)} %broadcast_in_dim.11), calls=%async_computation.3 | async-start | bytes 4227072 | tf_op jit(solution)/shard_map/all_to_all | solution.py:119
  87.8 10.9 %copy-start.37 = (f32[1,512]{1,0:T(1,128)}, f32[1,512]{1,0:T(1,128)S(1)}, u32[]{:S(2)}) copy-start(f32[1,512]{1,0:T(1,128)S(1)} %get-tuple-element.147) | copy-start | bytes 6148
  98.9 12.1 %copy-start.7 = (bf16[416,512]{1,0:T(8,128)(2,1)}, bf16[416,512]{1,0:T(8,128)(2,1)S(1)}, u32[]{:S(2)}) copy-start(bf16[416,512]{1,0:T(8,128)(2,1)S(1)} %add_convert_fusion.4) | copy-start | bytes 1277956
  102.7 20.1 %all-to-all-start.1 = ((bf16[4,2,152,512]{3,2,1,0:T(8,128)(2,1)}), bf16[4,2,152,512]{3,2,1,0:T(8,128)(2,1)}, u32[]{:S(2)}, u32[]{:S(2)}) async-start(bf16[4,2,152,512]{3,2,1,0:T(8,128)(2,1)} %bitcast.23), calls=%async_computation.1 | async-start | bytes 2490368 | tf_op jit(solution)/shard_map/all_to_all | solution.py:119
  140.2 20.8 %all-to-all-start.2 = ((bf16[4,2,152,512]{3,2,1,0:T(8,128)(2,1)}), bf16[4,2,152,512]{3,2,1,0:T(8,128)(2,1)}, u32[]{:S(2)}, u32[]{:S(2)}) async-start(bf16[4,2,152,512]{3,2,1,0:T(8,128)(2,1)} %copy.232), calls=%async_computation.2 | async-start | bytes 2490368 | tf_op jit(solution)/shard_map/all_to_all | solution.py:119
  145.1 15.9 %copy-start.60 = (s32[416]{0:T(512)S(1)}, s32[416]{0:T(512)}, u32[]{:S(2)}) copy-start(s32[416]{0:T(512)} %get-tuple-element.171) | copy-start | bytes 4996
  147.9 27.8 %copy-start.5 = (bf16[8,4,16,512]{3,2,1,0:T(8,128)(2,1)}, bf16[8,4,16,512]{3,2,1,0:T(8,128)(2,1)S(1)}, u32[]{:S(2)}) copy-start(bf16[8,4,16,512]{3,2,1,0:T(8,128)(2,1)S(1)} %copy.237) | copy-start | bytes 1572868
  148.0 19.4 %copy-start.64 = (f32[1,512]{1,0:T(1,128)}, f32[1,512]{1,0:T(1,128)S(1)}, u32[]{:S(2)}) copy-start(f32[1,512]{1,0:T(1,128)S(1)} %get-tuple-element.172) | copy-start | bytes 6148
  148.0 150.0 %copy-start.56 = (f32[1,512]{1,0:T(1,128)}, f32[1,512]{1,0:T(1,128)S(1)}, u32[]{:S(2)}) copy-start(f32[1,512]{1,0:T(1,128)S(1)} %get-tuple-element.142) | copy-start | bytes 6148
  167.1 130.8 %copy-start.41 = (f32[416]{0:T(512)}, f32[416]{0:T(512)S(1)}, u32[]{:S(2)}) copy-start(f32[416]{0:T(512)S(1)} %broadcast_multiply_fusion.9) | copy-start | bytes 4996
  167.4 130.6 %copy-start.50 = (f32[416]{0:T(512)}, f32[416]{0:T(512)S(1)}, u32[]{:S(2)}) copy-start(f32[416]{0:T(512)S(1)} %add_rsqrt_fusion.1) | copy-start | bytes 4996
  177.7 9.7 %copy-start.9 = (bf16[416,512]{1,0:T(8,128)(2,1)}, bf16[416,512]{1,0:T(8,128)(2,1)S(1)}, u32[]{:S(2)}) copy-start(bf16[416,512]{1,0:T(8,128)(2,1)S(1)} %add_convert_fusion.2) | copy-start | bytes 1277956
  177.8 7.6 %copy-start.28 = (bf16[2,197,512]{2,0,1:T(2,128)(2,1)S(1)}, bf16[2,197,512]{2,0,1:T(2,128)(2,1)}, u32[]{:S(2)}) copy-start(bf16[2,197,512]{2,0,1:T(2,128)(2,1)} %param.11) | copy-start | bytes 1210372
  179.6 19.8 %all-to-all-start.4 = ((bf16[4,2,152,512]{3,2,1,0:T(8,128)(2,1)}), bf16[4,2,152,512]{3,2,1,0:T(8,128)(2,1)}, u32[]{:S(2)}, u32[]{:S(2)}) async-start(bf16[4,2,152,512]{3,2,1,0:T(8,128)(2,1)} %bitcast.296), calls=%async_computation.4 | async-start | bytes 2490368 | tf_op jit(solution)/shard_map/all_to_all | solution.py:119
  185.4 81.0 %copy-start.16 = (bf16[2,208,512]{2,1,0:T(8,128)(2,1)}, bf16[2,208,512]{2,1,0:T(8,128)(2,1)S(1)}, u32[]{:S(2)}) copy-start(bf16[2,208,512]{2,1,0:T(8,128)(2,1)S(1)} %pad.25.clone) | copy-start | bytes 1277956
  199.5 37.2 %all-to-all-start.6 = ((bf16[4,2,152,512]{3,2,1,0:T(8,128)(2,1)}), bf16[4,2,152,512]{3,2,1,0:T(8,128)(2,1)}, u32[]{:S(2)}, u32[]{:S(2)}) async-start(bf16[4,2,152,512]{3,2,1,0:T(8,128)(2,1)} %bitcast.295), calls=%async_computation.6 | async-start | bytes 2490368 | tf_op jit(solution)/shard_map/all_to_all | solution.py:119
  236.7 12.6 %copy-start.68 = (f32[4,2,152]{2,1,0:T(2,128)}, f32[4,2,152]{2,1,0:T(2,128)S(1)}, u32[]{:S(2)}) copy-start(f32[4,2,152]{2,1,0:T(2,128)S(1)} %fusion.179) | copy-start | bytes 14596
  236.7 23.0 %all-to-all-start.5 = ((bf16[4,2,152,512]{3,2,1,0:T(8,128)(2,1)}), bf16[4,2,152,512]{3,2,1,0:T(8,128)(2,1)}, u32[]{:S(2)}, u32[]{:S(2)}) async-start(bf16[4,2,152,512]{3,2,1,0:T(8,128)(2,1)} %copy.240), calls=%async_computation.5 | async-start | bytes 2490368 | tf_op jit(solution)/shard_map/all_to_all | solution.py:119
  241.0 8.3 %copy-start.66 = (bf16[1,2,512,2048]{3,2,1,0:T(8,128)(2,1)S(1)}, bf16[1,2,512,2048]{3,2,1,0:T(8,128)(2,1)}, u32[]{:S(2)}) copy-start(bf16[1,2,512,2048]{3,2,1,0:T(8,128)(2,1)} %all-gather.17.cloned.1.call-done) | copy-start | bytes 12582916
  259.6 20.9 %all-to-all-start.7 = ((bf16[4,2,152,512]{3,2,1,0:T(8,128)(2,1)}), bf16[4,2,152,512]{3,2,1,0:T(8,128)(2,1)}, u32[]{:S(2)}, u32[]{:S(2)}) async-start(bf16[4,2,152,512]{3,2,1,0:T(8,128)(2,1)} %copy.244), calls=%async_computation.7 | async-start | bytes 2490368 | tf_op jit(solution)/shard_map/all_to_all | solution.py:119
  269.8 12.9 %copy-start.30 = (bf16[416,8]{0,1:T(8,128)(2,1)}, bf16[416,8]{0,1:T(8,128)(2,1)S(1)}, u32[]{:S(2)}) copy-start(bf16[416,8]{0,1:T(8,128)(2,1)S(1)} %fusion.149) | copy-start | bytes 19972
  301.4 25.6 %all-to-all-start.8 = ((bf16[4,2,152,512]{3,2,1,0:T(8,128)(2,1)}), bf16[4,2,152,512]{3,2,1,0:T(8,128)(2,1)}, u32[]{:S(2)}, u32[]{:S(2)}) async-start(bf16[4,2,152,512]{3,2,1,0:T(8,128)(2,1)} %bitcast.294), calls=%async_computation.8 | async-start | bytes 2490368 | tf_op jit(solution)/shard_map/all_to_all | solution.py:119
  327.0 8.7 %copy-start.65 = (bf16[1,2,512,2048]{3,2,1,0:T(8,128)(2,1)S(1)}, bf16[1,2,512,2048]{3,2,1,0:T(8,128)(2,1)}, u32[]{:S(2)}) copy-start(bf16[1,2,512,2048]{3,2,1,0:T(8,128)(2,1)} %all-gather.13.cloned.1.call-done) | copy-start | bytes 12582916
  339.7 19.2 %all-to-all-start.9 = ((bf16[4,2,152,512]{3,2,1,0:T(8,128)(2,1)}), bf16[4,2,152,512]{3,2,1,0:T(8,128)(2,1)S(1)}, u32[]{:S(2)}, u32[]{:S(2)}) async-start(bf16[4,2,152,512]{3,2,1,0:T(8,128)(2,1)} %copy.247), calls=%async_computation.9 | async-start | bytes 2490368 | tf_op jit(solution)/shard_map/all_to_all | solution.py:119
  352.1 11.4 %copy-start.53 = (s32[416]{0:T(512)S(1)}, s32[416]{0:T(512)}, u32[]{:S(2)}) copy-start(s32[416]{0:T(512)} %get-tuple-element.170) | copy-start | bytes 4996
  352.1 11.4 %copy-start.61 = (s32[416]{0:T(512)S(1)}, s32[416]{0:T(512)}, u32[]{:S(2)}) copy-start(s32[416]{0:T(512)} %get-tuple-element.171) | copy-start | bytes 4996
  358.8 31.5 %all-to-all-start.11 = ((bf16[4,8,16,2060]{3,2,1,0:T(8,128)(2,1)}), bf16[4,8,16,2060]{3,2,1,0:T(8,128)(2,1)}, u32[]{:S(2)}, u32[]{:S(2)}) async-start(bf16[4,8,16,2060]{3,2,1,0:T(8,128)(2,1)} %bitcast.267), calls=%async_computation.11 | async-start | bytes 4456448 | tf_op jit(solution)/shard_map/all_to_all | solution.py:119
  365.9 10.2 %copy-start.2 = (f32[2,208,512]{2,1,0:T(8,128)S(1)}, f32[2,208,512]{2,1,0:T(8,128)}, u32[]{:S(2)}) copy-start(f32[2,208,512]{2,1,0:T(8,128)} %copy-done.1) | copy-start | bytes 2555908
  365.9 10.2 %copy-start.20 = (bf16[8,4,16,1536]{3,2,1,0:T(8,128)(2,1)S(1)}, bf16[8,4,16,1536]{3,2,1,0:T(8,128)(2,1)}, u32[]{:S(2)}) copy-start(bf16[8,4,16,1536]{3,2,1,0:T(8,128)(2,1)} %copy-done.19) | copy-start | bytes 4718596
  365.9 10.2 %copy-start.43 = (f32[1,512]{1,0:T(1,128)S(1)}, f32[1,512]{1,0:T(1,128)}, u32[]{:S(2)}) copy-start(f32[1,512]{1,0:T(1,128)} %copy-done.42) | copy-start | bytes 6148
  365.9 10.2 %copy-start.48 = (f32[416]{0:T(512)S(1)}, f32[416]{0:T(512)}, u32[]{:S(2)}) copy-start(f32[416]{0:T(512)} %rsqrt.40) | copy-start | bytes 4996
  365.9 10.2 %copy-start.49 = (f32[416]{0:T(512)S(1)}, f32[416]{0:T(512)}, u32[]{:S(2)}) copy-start(f32[416]{0:T(512)} %div.95) | copy-start | bytes 4996
  390.3 30.3 %all-to-all-start.10 = ((bf16[4,8,16,2060]{3,2,1,0:T(8,128)(2,1)}), bf16[4,8,16,2060]{3,2,1,0:T(8,128)(2,1)}, u32[]{:S(2)}, u32[]{:S(2)}) async-start(bf16[4,8,16,2060]{3,2,1,0:T(8,128)(2,1)} %bitcast.275), calls=%async_computation.10 | async-start | bytes 4456448 | tf_op jit(solution)/shard_map/all_to_all | solution.py:119
  394.8 60.0 %reduce-scatter.6.cloned.1.call-start = ((), (), s32[]{:S(2)}) async-start(), calls=%async_computation.18 | async-start | bytes 1253376 | tf_op jit(solution)/shard_map/reduce_scatter | solution.py:409
  396.8 27.2 %copy-start.69 = (f32[4,2,152]{2,1,0:T(2,128)S(1)}, f32[4,2,152]{2,1,0:T(2,128)}, u32[]{:S(2)}) copy-start(f32[4,2,152]{2,1,0:T(2,128)} %copy-done.68) | copy-start | bytes 14596
  423.8 81.4 %reduce-scatter.14.cloned.1.call-start = ((), (), s32[]{:S(2)}) async-start(), calls=%async_computation.22 | async-start | bytes 4718592 | tf_op jit(solution)/shard_map/reduce_scatter | solution.py:281
  432.3 123.6 %reduce-scatter.12.cloned.1.call-start = ((), (), s32[]{:S(2)}) async-start(), calls=%async_computation.21 | async-start | bytes 4718592 | tf_op jit(solution)/shard_map/reduce_scatter | solution.py:281
  440.6 166.0 %reduce-scatter.10.cloned.1.call-start = ((), (), s32[]{:S(2)}) async-start(), calls=%async_computation.20 | async-start | bytes 4718592 | tf_op jit(solution)/shard_map/reduce_scatter | solution.py:294
  441.4 215.8 %reduce-scatter.8.cloned.1.call-start = ((), (), s32[]{:S(2)}) async-start(), calls=%async_computation.19 | async-start | bytes 4718592 | tf_op jit(solution)/shard_map/reduce_scatter | solution.py:294
  (45 other events, 135.6 us)
Sparse Core Ops, SparseCore 0:
  11.7 25.2 all-gather.10
  38.5 47.3 all-gather.12
  87.6 45.0 all-gather.14
  134.1 46.6 all-gather.16
  182.2 45.0 all-gather.18
  423.9 30.8 reduce-scatter.5
  457.1 48.0 reduce-scatter.13
  507.5 48.3 reduce-scatter.11
  558.2 48.3 reduce-scatter.9
  608.8 48.3 reduce-scatter.7

commit v5 on v4

--- a/solution.py
+++ b/solution.py
@@ -91,9 +91,13 @@
 
 
 def gather_experts(which, w_first, w_second):
+    if which == 0:
+        both = jnp.stack([jnp.swapaxes(w_first[which], 1, 2), w_second[which]])
+        both = lax.all_gather(both, "dp", axis=2, tiled=True)
+        return (both[0], both[1])
     first_full = lax.all_gather(w_first[which], "dp", axis=2, tiled=True)
     second_full = lax.all_gather(w_second[which], "dp", axis=1, tiled=True)
-    return (first_full, second_full)
+    return (jnp.swapaxes(first_full, 1, 2), second_full)
 
 
 def route_tables(route, experts_total, capacity):
@@ -258,7 +262,7 @@
 
 def experts_hidden(incoming, first_full):
     hidden_pre = jnp.einsum(
-        "sjcd,jdf->sjcf", incoming, first_full, preferred_element_type=jnp.float32
+        "sjcd,jfd->sjcf", incoming, first_full, preferred_element_type=jnp.float32
     )
     return (hidden_pre, gelu_value(hidden_pre).astype(jnp.bfloat16))
 
@@ -284,7 +288,7 @@
     )
     grad_pre = (grad_act * gelu_slope(hidden_pre)).astype(jnp.bfloat16)
     grad_rows = jnp.einsum(
-        "sjcf,jdf->sjcd", grad_pre, first_full, preferred_element_type=jnp.float32
+        "sjcf,jfd->sjcd", grad_pre, first_full, preferred_element_type=jnp.float32
     ).astype(jnp.bfloat16)
     grad_back = exchange(grad_rows)
     grad_first = jnp.einsum(
@@ -336,9 +340,12 @@
     piece = width // (peers * shares)
     columns = small.shape[1]
     small = small.reshape(shares, peers, piece, columns).swapaxes(0, 1)
+    return (grad_in, small)
+
+
+def sum_small(small):
     small = exchange(small)
-    small = jnp.sum(small.astype(jnp.float32), axis=0).astype(low)
-    return (grad_in, small)
+    return jnp.sum(small.astype(jnp.float32), axis=0).astype(jnp.bfloat16)
 
 
 def whole_step(
@@ -393,6 +400,9 @@
         if which < LAYERS - 1:
             slots = gated_slots(grad, moe_saved[which], tables[which], block_shape)
             grad_result = exchange(slots)
+            grad_result, smalls[which + 1] = lax.optimization_barrier(
+                (grad_result, smalls[which + 1])
+            )
         grad_back, firsts[which], seconds[which] = experts_backward(
             grad_result, incoming, hidden_pre, hidden_act, experts[which]
         )
@@ -405,6 +415,8 @@
             attn_saved[which],
             moe_saved[which],
         )
+    for which in reversed(range(LAYERS)):
+        smalls[which] = sum_small(smalls[which])
     both = jnp.stack(smalls, axis=2)
     both = lax.psum_scatter(both, "dp", scatter_dimension=0, tiled=True)[0]
     total = lax.all_gather(both, "expert", axis=0, tiled=True)

time: 676 us -> 670 us (level)
  waiting for transfers between devices: 328 us -> 319 us
    all_gather x2 -> x1, waiting for transfers between devices: 15 us -> 2.03 us  [gather_experts(): second_full = lax.all_gather(w_second[which], 'dp', axis=1, tiled=True)]
  transfers between devices with their start and end apart: 22 -> 21, of which waited for: 16 -> 17; matrix products, arithmetic and copies ran while one was open for 29% -> 26% of each run, Pallas kernels for 3% -> 3%
where the time goes in v5:
time: 670 us; the launch traced here: 661 us
  waiting for transfers between devices  319 us (48%)
  matrix products  140 us (21%)
  local copies, waits for them, and re-layouts  71.4 us (11%)
  starting transfers between devices  53 us (8%)
  Pallas kernels  30.9 us (5%)
  other arithmetic  20.1 us (3%)
  between operations  15.5 us (2%)
  blocking collectives  10.6 us (2%)
    all_to_all x12, waiting for transfers between devices, exchange(): lax.all_to_all(block, 'expert', split_axis=0, concat_axis=0, tiled=True)  105 us
    reduce_scatter x2, waiting for transfers between devices, experts_backward(): lax.psum_scatter(grad_first, 'dp', scatter_dimension=2, tiled=True)  98.8 us
    reduce_scatter x2, waiting for transfers between devices, experts_backward(): lax.psum_scatter(grad_second, 'dp', scatter_dimension=1, tiled=True)  84.9 us
    all_to_all x12, starting transfers between devices, exchange(): lax.all_to_all(block, 'expert', split_axis=0, concat_axis=0, tiled=True)  52.4 us
    pallas_call x2, Pallas kernels, attention_back(): pl.pallas_call(attention_back_kernel, grid=(rows // SEQ_PAD,), in_specs=[...  18.2 us
    dot_general x2, matrix products, experts_backward(): jnp.einsum('sjcd,jfd->sjcf', grad_result, second_full, preferred_element_...  17.2 us
    dot_general x2, matrix products, experts_hidden(): jnp.einsum('sjcd,jfd->sjcf', incoming, first_full, preferred_element_type...  17.1 us
    dot_general x2, matrix products, experts_backward(): jnp.einsum('sjcf,sjcd->jfd', hidden_act, grad_result, preferred_element_t...  16.6 us
  transfers between devices with their start and end apart: 21, of which 17 were waited for; matrix products, arithmetic and copies ran while one was open for 26% of the time, Pallas kernels for 3%

profile of v5, /device:TPU:0, one launch (start us, length us, event | category | flops | bytes accessed | tf_op | source)
XLA Modules:
  0.0 661.0 jit_solution(13584572827064799441)
XLA Ops:
  20.6 16.5 %all-gather.8.cloned.1.call-done = bf16[2,128,2060]{2,1,0:T(8,128)(2,1)} async-done(((bf16[2,16,2060]{2,1,0:T(8,128)(2,1)}), bf16[2,128,2060]{2,1,0:T(8,128)(2,1)}) %all-gather.8.cloned.1.call-update) | async-done | bytes 1054736 | tf_op jit(solution)/shard_map/all_gather | solution.py:63
  41.1 3.6 all-to-all-start
  48.7 21.8 %all-to-all-done = bf16[4,128,2060]{1,2,0:T(8,128)(2,1)S(1)} async-done(((bf16[4,128,2060]{1,2,0:T(8,128)(2,1)}), bf16[4,128,2060]{1,2,0:T(8,128)(2,1)S(1)}, u32[]{:S(2)}, u32[]{:S(2)}) %all-to-all-start) | async-done | bytes 2109472 | tf_op jit(solution)/shard_map/all_to_all | solution.py:123
  73.4 4.5 all-to-all-start.3
  89.8 6.3 attention.2
  102.9 4.7 all-to-all-start.1
  115.6 7.4 %all-to-all-done.1 = bf16[4,2,152,512]{3,2,1,0:T(8,128)(2,1)} async-done(((bf16[4,2,152,512]{3,2,1,0:T(8,128)(2,1)}), bf16[4,2,152,512]{3,2,1,0:T(8,128)(2,1)}, u32[]{:S(2)}, u32[]{:S(2)}) %all-to-all-start.1) | async-done | bytes 1245216 | tf_op jit(solution)/shard_map/all_to_all | solution.py:123
  123.0 8.0 %fusion.19 = (bf16[4,2,152,2048]{3,2,0,1:T(8,128)(2,1)S(1)}, f32[2,2048,4,152]{1,3,2,0:T(8,128)}) fusion(bf16[4,2,152,512]{3,2,1,0:T(8,128)(2,1)} %all-to-all-done.1, bf16[2,2,2048,512]{3,2,1,0:T(8,128)(2,1)} %all-gather.10.cloned.1.call-done), kind=kOutput, calls=%fused_computation.25 | convolution fusion | flops 2562588672 | bytes 20381696 | tf_op jit(solution)/shard_map/sjcd,jfd->sjcf/dot_general | solution.py:264
  134.9 4.3 all-to-all-start.2
  142.7 11.9 %all-to-all-done.2 = bf16[4,2,152,512]{3,2,1,0:T(8,128)(2,1)} async-done(((bf16[4,2,152,512]{3,2,1,0:T(8,128)(2,1)}), bf16[4,2,152,512]{3,2,1,0:T(8,128)(2,1)}, u32[]{:S(2)}, u32[]{:S(2)}) %all-to-all-start.2) | async-done | bytes 1245216 | tf_op jit(solution)/shard_map/all_to_all | solution.py:123
  157.0 3.6 fusion.153
  162.8 6.3 attention.3
  173.1 4.5 all-to-all-start.4
  179.8 13.0 %all-to-all-done.4 = bf16[4,2,152,512]{3,2,1,0:T(8,128)(2,1)} async-done(((bf16[4,2,152,512]{3,2,1,0:T(8,128)(2,1)}), bf16[4,2,152,512]{3,2,1,0:T(8,128)(2,1)}, u32[]{:S(2)}, u32[]{:S(2)}) %all-to-all-start.4) | async-done | bytes 1245216 | tf_op jit(solution)/shard_map/all_to_all | solution.py:123
  192.9 4.3 all-to-all-start.6
  199.0 9.0 %fusion.15 = (bf16[4,2,152,2048]{3,2,0,1:T(8,128)(2,1)}, f32[2,4,152,2048]{3,2,1,0:T(8,128)}) fusion(bf16[1,2,512,2048]{3,2,1,0:T(8,128)(2,1)} %all-gather.12.cloned.1.call-done, bf16[4,2,152,512]{3,2,1,0:T(8,128)(2,1)} %all-to-all-done.4), kind=kOutput, calls=%fused_computation.19 | convolution fusion | flops 2562588672 | bytes 20381696 | tf_op jit(solution)/shard_map/sjcd,jfd->sjcf/dot_general | solution.py:264
  208.0 4.5 all-to-all-done.6
  214.6 8.3 %fusion.7 = bf16[4,2,152,2048]{3,2,0,1:T(8,128)(2,1)S(1)} fusion(f32[2,4,152,2048]{3,2,1,0:T(8,128)} %get-tuple-element.165, bf16[1,2,2048,512]{3,2,1,0:T(8,128)(2,1)} %all-gather.14.cloned.1.call-done, bf16[4,2,152,512]{3,2,1,0:T(8,128)(2,1)} %all-to-all-done.6, f32[4,2,152]{2,1,0:T(2,128)S(1)} %fusion.167), kind=kOutput, calls=%fused_computation.9 | convolution fusion | flops 2576908288 | bytes 20386560 | tf_op jit(solution)/shard_map/sjcd,jfd->sjcf/dot_general | solution.py:286
  226.8 4.3 all-to-all-start.7
  231.1 6.4 fusion.61
  238.7 8.9 %all-to-all-done.7 = bf16[4,2,152,512]{3,2,1,0:T(8,128)(2,1)} async-done(((bf16[4,2,152,512]{3,2,1,0:T(8,128)(2,1)}), bf16[4,2,152,512]{3,2,1,0:T(8,128)(2,1)}, u32[]{:S(2)}, u32[]{:S(2)}) %all-to-all-start.7) | async-done | bytes 1245216 | tf_op jit(solution)/shard_map/all_to_all | solution.py:123
  247.6 4.5 all-to-all-start.5
  252.1 8.2 %bitcast_convert_fusion.3 = bf16[2,512,2048]{2,1,0:T(8,128)(2,1)} fusion(bf16[4,2,152,512]{3,2,1,0:T(8,128)(2,1)} %all-to-all-done.4, bf16[4,2,152,2048]{3,2,0,1:T(8,128)(2,1)} %copy-done.72), kind=kOutput, calls=%fused_computation.31 | convolution fusion | flops 2552233984 | bytes 10420224 | tf_op jit(solution)/shard_map/sjcd,sjcf->jdf/dot_general | solution.py:294
  263.3 4.4 all-to-all-done.5
  270.0 3.3 fusion.101
  276.1 9.3 %attention_back.2 = bf16[416,1536]{1,0:T(8,128)(2,1)} custom-call(bf16[416,1536]{1,0:T(8,128)(2,1)} %convolution_convert_fusion.5.packed_ref, bf16[416,512]{1,0:T(8,128)(2,1)} %convolution_convert_fusion.10.grad_ref, f32[416,8]{1,0:T(8,128)} %get-tuple-element.33.total_ref), custom_call_target="tpu_custom_call" | custom-call | tf_op jit(solution)/shard_map/attention_back/pallas_call | solution.py:214
  285.5 3.6 multiply_reduce_fusion.7
  292.7 4.4 all-to-all-start.8
  308.5 3.6 convolution_convert_fusion.1
  312.2 3.6 concatenate.12
  317.3 8.9 %fusion.13 = bf16[4,2,152,2048]{3,2,0,1:T(8,128)(2,1)S(1)} fusion(f32[2,2048,4,152]{1,3,2,0:T(8,128)} %get-tuple-element.158, bf16[2,2,2048,512]{3,2,1,0:T(8,128)(2,1)} %all-gather.10.cloned.1.call-done, bf16[4,2,152,512]{3,2,1,0:T(8,128)(2,1)} %all-to-all-done.8), kind=kOutput, calls=%fused_computation.15 | convolution fusion | flops 2575040512 | bytes 20381696 | tf_op jit(solution)/shard_map/sjcd,jfd->sjcf/dot_general | solution.py:286
  326.2 6.7 %fusion.65 = bf16[4,2,152,512]{3,2,0,1:T(8,128)(2,1)S(1)} fusion(bf16[4,2,152,2048]{3,2,0,1:T(8,128)(2,1)S(1)} %fusion.13, bf16[2,2,2048,512]{3,2,1,0:T(8,128)(2,1)} %all-gather.10.cloned.1.call-done), kind=kOutput, calls=%fused_computation.82 | convolution fusion | flops 2550759424 | bytes 10420224 | tf_op jit(solution)/shard_map/sjcf,jfd->sjcd/dot_general | solution.py:290
  334.1 4.3 all-to-all-start.9
  338.5 8.3 %bitcast_convert_fusion.2 = bf16[2,512,2048]{2,1,0:T(8,128)(2,1)} fusion(bf16[4,2,152,512]{3,2,1,0:T(8,128)(2,1)} %all-to-all-done.1, bf16[4,2,152,2048]{3,2,0,1:T(8,128)(2,1)} %copy-done.73), kind=kOutput, calls=%fused_computation.30 | convolution fusion | flops 2552233984 | bytes 10420224 | tf_op jit(solution)/shard_map/sjcd,sjcf->jdf/dot_general | solution.py:294
  346.8 6.4 all-to-all-done.9
  353.2 4.5 all-to-all-start.11
  361.3 8.9 %attention_back.3 = bf16[416,1536]{1,0:T(8,128)(2,1)} custom-call(bf16[416,1536]{1,0:T(8,128)(2,1)} %convolution_convert_fusion.6.packed_ref, bf16[416,512]{1,0:T(8,128)(2,1)} %convolution_convert_fusion.9.grad_ref, f32[416,8]{1,0:T(8,128)} %get-tuple-element.37.total_ref), custom_call_target="tpu_custom_call" | custom-call | tf_op jit(solution)/shard_map/attention_back/pallas_call | solution.py:214
  376.9 4.4 concatenate.13
  384.5 4.5 all-to-all-start.10
  391.3 23.6 %all-to-all-done.10 = bf16[4,8,16,2060]{3,2,1,0:T(8,128)(2,1)} async-done(((bf16[4,8,16,2060]{3,2,1,0:T(8,128)(2,1)}), bf16[4,8,16,2060]{3,2,1,0:T(8,128)(2,1)}, u32[]{:S(2)}, u32[]{:S(2)}) %all-to-all-start.10) | async-done | bytes 2109472 | tf_op jit(solution)/shard_map/all_to_all | solution.py:123
  418.1 8.4 %bitcast_convert_fusion = bf16[2,2048,512]{2,1,0:T(8,128)(2,1)} fusion(bf16[4,2,152,2048]{3,2,0,1:T(8,128)(2,1)} %get-tuple-element.164, bf16[4,2,152,512]{3,2,1,0:T(8,128)(2,1)} %all-to-all-done.6, f32[4,2,152]{2,1,0:T(2,128)S(1)} %copy-done.71), kind=kOutput, calls=%fused_computation.28 | convolution fusion | flops 2554101760 | bytes 10425088 | tf_op jit(solution)/shard_map/sjcf,sjcd->jfd/dot_general | solution.py:282
  426.6 8.2 %bitcast_convert_fusion.1 = bf16[2,2048,512]{2,1,0:T(8,128)(2,1)} fusion(bf16[4,2,152,2048]{3,2,0,1:T(8,128)(2,1)} %copy-done.69, bf16[4,2,152,512]{3,2,1,0:T(8,128)(2,1)} %all-to-all-done.8), kind=kOutput, calls=%fused_computation.29 | convolution fusion | flops 2552233984 | bytes 10420224 | tf_op jit(solution)/shard_map/sjcf,sjcd->jfd/dot_general | solution.py:282
  439.6 9.5 %reduce-scatter.6.cloned.1.call-done = bf16[1,16,2,2060]{3,1,2,0:T(8,128)(2,1)} async-done(((bf16[8,16,2,2060]{3,1,2,0:T(8,128)(2,1)}), bf16[1,16,2,2060]{3,1,2,0:T(8,128)(2,1)}) %reduce-scatter.6.cloned.1.call-update) | async-done | bytes 131856 | tf_op jit(solution)/shard_map/reduce_scatter | solution.py:421
  450.1 10.6 %all-gather.2 = bf16[1,64,2,2060]{3,2,0,1:T(2,128)(2,1)S(1)} all-gather(bf16[1,16,2,2060]{3,2,0,1:T(2,128)(2,1)S(1)} %copy.274), channel_id=4, replica_groups=mesh['dp'=8,'expert'=4] {'expert'}, dimensions={1}, use_global_device_ids=true | all-gather | bytes 659200 | tf_op jit(solution)/shard_map/all_gather | solution.py:422
  465.2 34.2 %reduce-scatter.14.cloned.1.call-done = bf16[2,256,512]{2,1,0:T(8,128)(2,1)} async-done(((bf16[2,2048,512]{2,1,0:T(8,128)(2,1)}), bf16[2,256,512]{2,1,0:T(8,128)(2,1)}) %reduce-scatter.14.cloned.1.call-update) | async-done | bytes 524304 | tf_op jit(solution)/shard_map/reduce_scatter | solution.py:285
  499.4 50.7 %reduce-scatter.12.cloned.1.call-done = bf16[2,256,512]{2,1,0:T(8,128)(2,1)} async-done(((bf16[2,2048,512]{2,1,0:T(8,128)(2,1)}), bf16[2,256,512]{2,1,0:T(8,128)(2,1)}) %reduce-scatter.12.cloned.1.call-update) | async-done | bytes 524304 | tf_op jit(solution)/shard_map/reduce_scatter | solution.py:285
  552.8 48.1 %reduce-scatter.10.cloned.1.call-done = bf16[2,512,256]{2,1,0:T(8,128)(2,1)} async-done(((bf16[2,512,2048]{2,1,0:T(8,128)(2,1)}), bf16[2,512,256]{2,1,0:T(8,128)(2,1)}) %reduce-scatter.10.cloned.1.call-update) | async-done | bytes 524304 | tf_op jit(solution)/shard_map/reduce_scatter | solution.py:298
  600.8 50.7 %reduce-scatter.8.cloned.1.call-done = bf16[2,512,256]{2,1,0:T(8,128)(2,1)} async-done(((bf16[2,512,2048]{2,1,0:T(8,128)(2,1)}), bf16[2,512,256]{2,1,0:T(8,128)(2,1)}) %reduce-scatter.8.cloned.1.call-update) | async-done | bytes 524304 | tf_op jit(solution)/shard_map/reduce_scatter | solution.py:298
  (341 shorter events, 137.3 us)
Async XLA Ops:
  7.2 29.9 %all-gather.8.cloned.1.call-start = ((), (), s32[]{:S(2)}) async-start(), calls=%async_computation.17 | async-start | bytes 1253376 | tf_op jit(solution)/shard_map/all_gather | solution.py:63
  11.6 111.4 %all-gather.10.cloned.1.call-start = ((), (), s32[]{:S(2)}) async-start(), calls=%async_computation.18 | async-start | bytes 9437184 | tf_op jit(solution)/shard_map/all_gather | solution.py:96
  15.9 183.1 %all-gather.12.cloned.1.call-start = ((), (), s32[]{:S(2)}) async-start(), calls=%async_computation.24 | async-start | bytes 4718592 | tf_op jit(solution)/shard_map/all_gather | solution.py:98
  16.7 197.9 %all-gather.14.cloned.1.call-start = ((), (), s32[]{:S(2)}) async-start(), calls=%async_computation.25 | async-start | bytes 4718592 | tf_op jit(solution)/shard_map/all_gather | solution.py:99
  41.1 29.3 %all-to-all-start = ((bf16[4,128,2060]{1,2,0:T(8,128)(2,1)}), bf16[4,128,2060]{1,2,0:T(8,128)(2,1)S(1)}, u32[]{:S(2)}, u32[]{:S(2)}) async-start(bf16[4,128,2060]{1,2,0:T(8,128)(2,1)} %broadcast_in_dim.9), calls=%async_computation | async-start | bytes 4227072 | tf_op jit(solution)/shard_map/all_to_all | solution.py:123
  45.9 50.2 %copy-start.1 = (f32[2,208,512]{2,1,0:T(8,128)}, f32[2,208,512]{2,1,0:T(8,128)S(1)}, u32[]{:S(2)}) copy-start(f32[2,208,512]{2,1,0:T(8,128)S(1)} %pad_convert_fusion) | copy-start | bytes 2555908
  46.0 40.9 %copy-start.46 = (f32[2,208]{1,0:T(2,128)}, f32[2,208]{1,0:T(2,128)S(1)}, u32[]{:S(2)}) copy-start(f32[2,208]{1,0:T(2,128)S(1)} %add_rsqrt_fusion.3) | copy-start | bytes 4996
  73.4 29.5 %all-to-all-start.3 = ((bf16[4,128,2060]{1,2,0:T(8,128)(2,1)}), bf16[4,128,2060]{1,2,0:T(8,128)(2,1)}, u32[]{:S(2)}, u32[]{:S(2)}) async-start(bf16[4,128,2060]{1,2,0:T(8,128)(2,1)} %broadcast_in_dim.11), calls=%async_computation.3 | async-start | bytes 4227072 | tf_op jit(solution)/shard_map/all_to_all | solution.py:123
  86.8 9.4 %copy-start.3 = (bf16[8,4,16,512]{3,2,1,0:T(8,128)(2,1)}, bf16[8,4,16,512]{3,2,1,0:T(8,128)(2,1)S(1)}, u32[]{:S(2)}) copy-start(bf16[8,4,16,512]{3,2,1,0:T(8,128)(2,1)S(1)} %copy.234) | copy-start | bytes 1572868
  86.8 11.1 %copy-start.39 = (f32[1,512]{1,0:T(1,128)}, f32[1,512]{1,0:T(1,128)S(1)}, u32[]{:S(2)}) copy-start(f32[1,512]{1,0:T(1,128)S(1)} %get-tuple-element.151) | copy-start | bytes 6148
  98.2 15.3 %copy-start.7 = (bf16[416,512]{1,0:T(8,128)(2,1)}, bf16[416,512]{1,0:T(8,128)(2,1)S(1)}, u32[]{:S(2)}) copy-start(bf16[416,512]{1,0:T(8,128)(2,1)S(1)} %add_convert_fusion.4) | copy-start | bytes 1277956
  98.2 9.5 %copy-start.58 = (s32[416]{0:T(512)S(1)}, s32[416]{0:T(512)}, u32[]{:S(2)}) copy-start(s32[416]{0:T(512)} %get-tuple-element.115) | copy-start | bytes 4996
  98.2 9.5 %copy-start.59 = (s32[416]{0:T(512)S(1)}, s32[416]{0:T(512)}, u32[]{:S(2)}) copy-start(s32[416]{0:T(512)} %get-tuple-element.116) | copy-start | bytes 4996
  98.2 10.8 %copy-start.47 = (f32[2,208]{1,0:T(2,128)S(1)}, f32[2,208]{1,0:T(2,128)}, u32[]{:S(2)}) copy-start(f32[2,208]{1,0:T(2,128)} %copy-done.46) | copy-start | bytes 4996
  98.2 11.4 %copy-start.30 = (bf16[2,197,512]{2,0,1:T(2,128)(2,1)S(1)}, bf16[2,197,512]{2,0,1:T(2,128)(2,1)}, u32[]{:S(2)}) copy-start(bf16[2,197,512]{2,0,1:T(2,128)(2,1)} %param.11) | copy-start | bytes 1210372
  102.9 20.1 %all-to-all-start.1 = ((bf16[4,2,152,512]{3,2,1,0:T(8,128)(2,1)}), bf16[4,2,152,512]{3,2,1,0:T(8,128)(2,1)}, u32[]{:S(2)}, u32[]{:S(2)}) async-start(bf16[4,2,152,512]{3,2,1,0:T(8,128)(2,1)} %bitcast.32), calls=%async_computation.1 | async-start | bytes 2490368 | tf_op jit(solution)/shard_map/all_to_all | solution.py:123
  134.9 19.7 %all-to-all-start.2 = ((bf16[4,2,152,512]{3,2,1,0:T(8,128)(2,1)}), bf16[4,2,152,512]{3,2,1,0:T(8,128)(2,1)}, u32[]{:S(2)}, u32[]{:S(2)}) async-start(bf16[4,2,152,512]{3,2,1,0:T(8,128)(2,1)} %copy.238), calls=%async_computation.2 | async-start | bytes 2490368 | tf_op jit(solution)/shard_map/all_to_all | solution.py:123
  139.8 14.8 %copy-start.61 = (s32[416]{0:T(512)S(1)}, s32[416]{0:T(512)}, u32[]{:S(2)}) copy-start(s32[416]{0:T(512)} %get-tuple-element.175) | copy-start | bytes 4996
  142.6 26.5 %copy-start.5 = (bf16[8,4,16,512]{3,2,1,0:T(8,128)(2,1)}, bf16[8,4,16,512]{3,2,1,0:T(8,128)(2,1)S(1)}, u32[]{:S(2)}) copy-start(bf16[8,4,16,512]{3,2,1,0:T(8,128)(2,1)S(1)} %copy.243) | copy-start | bytes 1572868
  142.7 18.2 %copy-start.66 = (f32[1,512]{1,0:T(1,128)}, f32[1,512]{1,0:T(1,128)S(1)}, u32[]{:S(2)}) copy-start(f32[1,512]{1,0:T(1,128)S(1)} %get-tuple-element.176) | copy-start | bytes 6148
  142.7 146.5 %copy-start.56 = (f32[1,512]{1,0:T(1,128)}, f32[1,512]{1,0:T(1,128)S(1)}, u32[]{:S(2)}) copy-start(f32[1,512]{1,0:T(1,128)S(1)} %get-tuple-element.146) | copy-start | bytes 6148
  160.5 128.6 %copy-start.41 = (f32[416]{0:T(512)}, f32[416]{0:T(512)S(1)}, u32[]{:S(2)}) copy-start(f32[416]{0:T(512)S(1)} %broadcast_multiply_fusion.9) | copy-start | bytes 4996
  160.8 128.3 %copy-start.50 = (f32[416]{0:T(512)}, f32[416]{0:T(512)S(1)}, u32[]{:S(2)}) copy-start(f32[416]{0:T(512)S(1)} %add_rsqrt_fusion.1) | copy-start | bytes 4996
  171.1 8.4 %copy-start.9 = (bf16[416,512]{1,0:T(8,128)(2,1)}, bf16[416,512]{1,0:T(8,128)(2,1)S(1)}, u32[]{:S(2)}) copy-start(bf16[416,512]{1,0:T(8,128)(2,1)S(1)} %add_convert_fusion.2) | copy-start | bytes 1277956
  173.1 19.8 %all-to-all-start.4 = ((bf16[4,2,152,512]{3,2,1,0:T(8,128)(2,1)}), bf16[4,2,152,512]{3,2,1,0:T(8,128)(2,1)}, u32[]{:S(2)}, u32[]{:S(2)}) async-start(bf16[4,2,152,512]{3,2,1,0:T(8,128)(2,1)} %bitcast.301), calls=%async_computation.4 | async-start | bytes 2490368 | tf_op jit(solution)/shard_map/all_to_all | solution.py:123
  192.9 19.7 %all-to-all-start.6 = ((bf16[4,2,152,512]{3,2,1,0:T(8,128)(2,1)}), bf16[4,2,152,512]{3,2,1,0:T(8,128)(2,1)}, u32[]{:S(2)}, u32[]{:S(2)}) async-start(bf16[4,2,152,512]{3,2,1,0:T(8,128)(2,1)} %bitcast.299), calls=%async_computation.6 | async-start | bytes 2490368 | tf_op jit(solution)/shard_map/all_to_all | solution.py:123
  199.0 15.6 %copy-start.70 = (f32[4,2,152]{2,1,0:T(2,128)}, f32[4,2,152]{2,1,0:T(2,128)S(1)}, u32[]{:S(2)}) copy-start(f32[4,2,152]{2,1,0:T(2,128)S(1)} %fusion.167) | copy-start | bytes 14596
  214.6 8.3 %copy-start.68 = (bf16[1,2,512,2048]{3,2,1,0:T(8,128)(2,1)S(1)}, bf16[1,2,512,2048]{3,2,1,0:T(8,128)(2,1)}, u32[]{:S(2)}) copy-start(bf16[1,2,512,2048]{3,2,1,0:T(8,128)(2,1)} %all-gather.12.cloned.1.call-done) | copy-start | bytes 12582916
  226.8 20.8 %all-to-all-start.7 = ((bf16[4,2,152,512]{3,2,1,0:T(8,128)(2,1)}), bf16[4,2,152,512]{3,2,1,0:T(8,128)(2,1)}, u32[]{:S(2)}, u32[]{:S(2)}) async-start(bf16[4,2,152,512]{3,2,1,0:T(8,128)(2,1)} %copy.250), calls=%async_computation.7 | async-start | bytes 2490368 | tf_op jit(solution)/shard_map/all_to_all | solution.py:123
  247.6 20.1 %all-to-all-start.5 = ((bf16[4,2,152,512]{3,2,1,0:T(8,128)(2,1)}), bf16[4,2,152,512]{3,2,1,0:T(8,128)(2,1)}, u32[]{:S(2)}, u32[]{:S(2)}) async-start(bf16[4,2,152,512]{3,2,1,0:T(8,128)(2,1)} %copy.246), calls=%async_computation.5 | async-start | bytes 2490368 | tf_op jit(solution)/shard_map/all_to_all | solution.py:123
  252.1 8.2 %copy-start.65 = (s32[416]{0:T(512)S(1)}, s32[416]{0:T(512)}, u32[]{:S(2)}) copy-start(s32[416]{0:T(512)} %get-tuple-element.178) | copy-start | bytes 4996
  292.7 24.6 %all-to-all-start.8 = ((bf16[4,2,152,512]{3,2,1,0:T(8,128)(2,1)}), bf16[4,2,152,512]{3,2,1,0:T(8,128)(2,1)}, u32[]{:S(2)}, u32[]{:S(2)}) async-start(bf16[4,2,152,512]{3,2,1,0:T(8,128)(2,1)} %bitcast.298), calls=%async_computation.8 | async-start | bytes 2490368 | tf_op jit(solution)/shard_map/all_to_all | solution.py:123
  334.1 19.0 %all-to-all-start.9 = ((bf16[4,2,152,512]{3,2,1,0:T(8,128)(2,1)}), bf16[4,2,152,512]{3,2,1,0:T(8,128)(2,1)S(1)}, u32[]{:S(2)}, u32[]{:S(2)}) async-start(bf16[4,2,152,512]{3,2,1,0:T(8,128)(2,1)} %copy.260), calls=%async_computation.9 | async-start | bytes 2490368 | tf_op jit(solution)/shard_map/all_to_all | solution.py:123
  346.8 10.9 %copy-start.53 = (s32[416]{0:T(512)S(1)}, s32[416]{0:T(512)}, u32[]{:S(2)}) copy-start(s32[416]{0:T(512)} %get-tuple-element.174) | copy-start | bytes 4996
  346.8 10.9 %copy-start.62 = (s32[416]{0:T(512)S(1)}, s32[416]{0:T(512)}, u32[]{:S(2)}) copy-start(s32[416]{0:T(512)} %get-tuple-element.175) | copy-start | bytes 4996
  353.2 31.3 %all-to-all-start.11 = ((bf16[4,8,16,2060]{3,2,1,0:T(8,128)(2,1)}), bf16[4,8,16,2060]{3,2,1,0:T(8,128)(2,1)}, u32[]{:S(2)}, u32[]{:S(2)}) async-start(bf16[4,8,16,2060]{3,2,1,0:T(8,128)(2,1)} %bitcast.271), calls=%async_computation.11 | async-start | bytes 4456448 | tf_op jit(solution)/shard_map/all_to_all | solution.py:123
  360.0 10.2 %copy-start.2 = (f32[2,208,512]{2,1,0:T(8,128)S(1)}, f32[2,208,512]{2,1,0:T(8,128)}, u32[]{:S(2)}) copy-start(f32[2,208,512]{2,1,0:T(8,128)} %copy-done.1) | copy-start | bytes 2555908
  360.0 10.2 %copy-start.21 = (bf16[8,4,16,1536]{3,2,1,0:T(8,128)(2,1)S(1)}, bf16[8,4,16,1536]{3,2,1,0:T(8,128)(2,1)}, u32[]{:S(2)}) copy-start(bf16[8,4,16,1536]{3,2,1,0:T(8,128)(2,1)} %copy-done.20) | copy-start | bytes 4718596
  360.1 10.2 %copy-start.43 = (f32[1,512]{1,0:T(1,128)S(1)}, f32[1,512]{1,0:T(1,128)}, u32[]{:S(2)}) copy-start(f32[1,512]{1,0:T(1,128)} %copy-done.42) | copy-start | bytes 6148
  360.1 10.1 %copy-start.48 = (f32[416]{0:T(512)S(1)}, f32[416]{0:T(512)}, u32[]{:S(2)}) copy-start(f32[416]{0:T(512)} %div.95) | copy-start | bytes 4996
  360.1 10.1 %copy-start.49 = (f32[416]{0:T(512)S(1)}, f32[416]{0:T(512)}, u32[]{:S(2)}) copy-start(f32[416]{0:T(512)} %rsqrt.40) | copy-start | bytes 4996
  384.5 30.4 %all-to-all-start.10 = ((bf16[4,8,16,2060]{3,2,1,0:T(8,128)(2,1)}), bf16[4,8,16,2060]{3,2,1,0:T(8,128)(2,1)}, u32[]{:S(2)}, u32[]{:S(2)}) async-start(bf16[4,8,16,2060]{3,2,1,0:T(8,128)(2,1)} %bitcast.275), calls=%async_computation.10 | async-start | bytes 4456448 | tf_op jit(solution)/shard_map/all_to_all | solution.py:123
  389.1 60.0 %reduce-scatter.6.cloned.1.call-start = ((), (), s32[]{:S(2)}) async-start(), calls=%async_computation.19 | async-start | bytes 1253376 | tf_op jit(solution)/shard_map/reduce_scatter | solution.py:421
  391.3 26.8 %copy-start.71 = (f32[4,2,152]{2,1,0:T(2,128)S(1)}, f32[4,2,152]{2,1,0:T(2,128)}, u32[]{:S(2)}) copy-start(f32[4,2,152]{2,1,0:T(2,128)} %copy-done.70) | copy-start | bytes 14596
  418.1 81.3 %reduce-scatter.14.cloned.1.call-start = ((), (), s32[]{:S(2)}) async-start(), calls=%async_computation.23 | async-start | bytes 4718592 | tf_op jit(solution)/shard_map/reduce_scatter | solution.py:285
  426.5 123.6 %reduce-scatter.12.cloned.1.call-start = ((), (), s32[]{:S(2)}) async-start(), calls=%async_computation.22 | async-start | bytes 4718592 | tf_op jit(solution)/shard_map/reduce_scatter | solution.py:285
  434.8 166.0 %reduce-scatter.10.cloned.1.call-start = ((), (), s32[]{:S(2)}) async-start(), calls=%async_computation.21 | async-start | bytes 4718592 | tf_op jit(solution)/shard_map/reduce_scatter | solution.py:298
  435.6 215.9 %reduce-scatter.8.cloned.1.call-start = ((), (), s32[]{:S(2)}) async-start(), calls=%async_computation.20 | async-start | bytes 4718592 | tf_op jit(solution)/shard_map/reduce_scatter | solution.py:298
  (47 other events, 150.3 us)
Sparse Core Ops, SparseCore 0:
  11.7 25.3 all-gather.7
  38.7 81.3 all-gather.9
  121.7 46.3 all-gather.11
  169.5 45.0 all-gather.13
  418.2 30.8 reduce-scatter.5
  451.2 48.0 reduce-scatter.13
  501.6 48.4 reduce-scatter.11
  552.4 48.3 reduce-scatter.9
  603.1 48.3 reduce-scatter.7

commit v6 on v5

--- a/solution.py
+++ b/solution.py
@@ -336,16 +336,32 @@
         ],
         axis=1,
     )
-    peers, shares = lax.axis_size("expert"), lax.axis_size("dp")
-    piece = width // (peers * shares)
-    columns = small.shape[1]
-    small = small.reshape(shares, peers, piece, columns).swapaxes(0, 1)
+    peers, chips = lax.axis_size("expert"), lax.axis_size("dp") // 2
+    small = small.reshape(chips, 2, peers, width // (2 * chips * peers), small.shape[1])
+    small = small.transpose(1, 2, 0, 3, 4)
     return (grad_in, small)
 
 
+def halve(block, bit, step):
+    size = lax.axis_size("dp")
+    kept = lax.dynamic_index_in_dim(block, bit, 0, keepdims=False)
+    sent = lax.dynamic_index_in_dim(block, 1 - bit, 0, keepdims=False)
+    moved = lax.ppermute(sent, "dp", [(source, source ^ step) for source in range(size)])
+    return (kept.astype(jnp.float32) + moved.astype(jnp.float32)).astype(jnp.bfloat16)
+
+
 def sum_small(small):
+    place = lax.axis_index("dp")
+    small = halve(small, place % 2, 1)
     small = exchange(small)
-    return jnp.sum(small.astype(jnp.float32), axis=0).astype(jnp.bfloat16)
+    small = jnp.sum(small.astype(jnp.float32), axis=0).astype(jnp.bfloat16)
+    step = 2
+    while small.shape[0] > 1:
+        chips, rows, columns = small.shape
+        block = small.reshape(chips // 2, 2, rows, columns).swapaxes(0, 1)
+        small = halve(block, (place // step) % 2, step)
+        step = 2 * step
+    return small[0]
 
 
 def whole_step(
@@ -417,8 +433,7 @@
         )
     for which in reversed(range(LAYERS)):
         smalls[which] = sum_small(smalls[which])
-    both = jnp.stack(smalls, axis=2)
-    both = lax.psum_scatter(both, "dp", scatter_dimension=0, tiled=True)[0]
+    both = jnp.stack(smalls, axis=1)
     total = lax.all_gather(both, "expert", axis=0, tiled=True)
     total = total.swapaxes(0, 1).astype(jnp.float32)
     grad_images = grad.reshape(images, SEQ_PAD, width)[:, :length]

time: 670 us -> 507 us (0.76)
  waiting for transfers between devices: 319 us -> 150 us
    reduce_scatter x2, waiting for transfers between devices: 84.9 us -> 0.01 us  [experts_backward(): lax.psum_scatter(grad_second, 'dp', scatter_dimension=1, tiled=True)]
    reduce_scatter x2, waiting for transfers between devices: 98.8 us -> 17.2 us  [experts_backward(): lax.psum_scatter(grad_first, 'dp', scatter_dimension=2, tiled=True)]
    ppermute x0 -> x6, waiting for transfers between devices: none -> 11.6 us  [halve(): lax.ppermute(sent, 'dp', [(source, source ^ step) for source in range(siz...]
    reduce_scatter x1 -> x0, waiting for transfers between devices: 9.48 us -> none  [whole_step(): both = lax.psum_scatter(both, 'dp', scatter_dimension=0, tiled=True)[0]]
  transfers between devices with their start and end apart: 21 -> 26, of which waited for: 17 -> 16; matrix products, arithmetic and copies ran while one was open for 26% -> 45% of each run, Pallas kernels for 3% -> 6%
where the time goes in v6:
time: 507 us; the launch traced here: 498 us
  waiting for transfers between devices  150 us (30%)
  matrix products  141 us (28%)
  local copies, waits for them, and re-layouts  69.4 us (14%)
  starting transfers between devices  56.6 us (11%)
  Pallas kernels  31.1 us (6%)
  other arithmetic  23.6 us (5%)
  between operations  15.9 us (3%)
  blocking collectives  9.74 us (2%)
    all_to_all x12, waiting for transfers between devices, exchange(): lax.all_to_all(block, 'expert', split_axis=0, concat_axis=0, tiled=True)  103 us
    all_to_all x12, starting transfers between devices, exchange(): lax.all_to_all(block, 'expert', split_axis=0, concat_axis=0, tiled=True)  51.1 us
    pallas_call x2, Pallas kernels, attention_back(): pl.pallas_call(attention_back_kernel, grid=(rows // SEQ_PAD,), in_specs=[...  18.4 us
    dot_general x2, matrix products, experts_backward(): jnp.einsum('sjcd,jfd->sjcf', grad_result, second_full, preferred_element_...  17.5 us
    reduce_scatter x2, waiting for transfers between devices, experts_backward(): lax.psum_scatter(grad_first, 'dp', scatter_dimension=2, tiled=True)  17.2 us
    dot_general x2, matrix products, experts_hidden(): jnp.einsum('sjcd,jfd->sjcf', incoming, first_full, preferred_element_type...  17.1 us
    dot_general x2, matrix products, experts_backward(): jnp.einsum('sjcf,sjcd->jfd', hidden_act, grad_result, preferred_element_t...  16.7 us
    dot_general x2, matrix products, experts_backward(): jnp.einsum('sjcd,sjcf->jdf', incoming, grad_pre, preferred_element_type=j...  16.7 us
  transfers between devices with their start and end apart: 26, of which 16 were waited for; matrix products, arithmetic and copies ran while one was open for 45% of the time, Pallas kernels for 6%

profile of v6, /device:TPU:0, one launch (start us, length us, event | category | flops | bytes accessed | tf_op | source)
XLA Modules:
  0.0 497.6 jit_solution(4705187666299793102)
XLA Ops:
  20.7 16.3 %all-gather.7.cloned.1.call-done = bf16[2,128,2060]{2,1,0:T(8,128)(2,1)} async-done(((bf16[2,16,2060]{2,1,0:T(8,128)(2,1)}), bf16[2,128,2060]{2,1,0:T(8,128)(2,1)}) %all-gather.7.cloned.1.call-update) | async-done | bytes 1054736 | tf_op jit(solution)/shard_map/all_gather | solution.py:63
  41.1 3.6 all-to-all-start
  48.6 21.8 %all-to-all-done = bf16[4,128,2060]{1,2,0:T(8,128)(2,1)S(1)} async-done(((bf16[4,128,2060]{1,2,0:T(8,128)(2,1)}), bf16[4,128,2060]{1,2,0:T(8,128)(2,1)S(1)}, u32[]{:S(2)}, u32[]{:S(2)}) %all-to-all-start) | async-done | bytes 2109472 | tf_op jit(solution)/shard_map/all_to_all | solution.py:123
  73.4 4.4 all-to-all-start.3
  89.6 6.3 %attention.2 = (bf16[416,512]{1,0:T(8,128)(2,1)}, f32[416,8]{1,0:T(8,128)}) custom-call(bf16[416,1536]{1,0:T(8,128)(2,1)} %convolution_convert_fusion.6.packed_ref), custom_call_target="tpu_custom_call" | custom-call | tf_op jit(solution)/shard_map/attention/pallas_call | solution.py:199
  102.9 4.7 all-to-all-start.1
  114.3 8.6 %all-to-all-done.1 = bf16[4,2,152,512]{3,2,1,0:T(8,128)(2,1)} async-done(((bf16[4,2,152,512]{3,2,1,0:T(8,128)(2,1)}), bf16[4,2,152,512]{3,2,1,0:T(8,128)(2,1)}, u32[]{:S(2)}, u32[]{:S(2)}) %all-to-all-start.1) | async-done | bytes 1245216 | tf_op jit(solution)/shard_map/all_to_all | solution.py:123
  122.9 8.0 %fusion.19 = (bf16[4,2,152,2048]{3,2,0,1:T(8,128)(2,1)S(1)}, f32[2,2048,4,152]{1,3,2,0:T(8,128)}) fusion(bf16[4,2,152,512]{3,2,1,0:T(8,128)(2,1)} %all-to-all-done.1, bf16[2,2,2048,512]{3,2,1,0:T(8,128)(2,1)} %all-gather.9.cloned.1.call-done), kind=kOutput, calls=%fused_computation.25 | convolution fusion | flops 2562588672 | bytes 20381696 | tf_op jit(solution)/shard_map/sjcd,jfd->sjcf/dot_general | solution.py:264
  134.9 4.3 all-to-all-start.2
  142.7 11.9 %all-to-all-done.2 = bf16[4,2,152,512]{3,2,1,0:T(8,128)(2,1)} async-done(((bf16[4,2,152,512]{3,2,1,0:T(8,128)(2,1)}), bf16[4,2,152,512]{3,2,1,0:T(8,128)(2,1)}, u32[]{:S(2)}, u32[]{:S(2)}) %all-to-all-start.2) | async-done | bytes 1245216 | tf_op jit(solution)/shard_map/all_to_all | solution.py:123
  156.9 3.6 fusion.159
  162.8 6.3 %attention.3 = (bf16[416,512]{1,0:T(8,128)(2,1)}, f32[416,8]{1,0:T(8,128)}) custom-call(bf16[416,1536]{1,0:T(8,128)(2,1)} %convolution_convert_fusion.5.packed_ref), custom_call_target="tpu_custom_call" | custom-call | tf_op jit(solution)/shard_map/attention/pallas_call | solution.py:199
  173.1 4.5 all-to-all-start.4
  179.8 13.0 %all-to-all-done.4 = bf16[4,2,152,512]{3,2,1,0:T(8,128)(2,1)} async-done(((bf16[4,2,152,512]{3,2,1,0:T(8,128)(2,1)}), bf16[4,2,152,512]{3,2,1,0:T(8,128)(2,1)}, u32[]{:S(2)}, u32[]{:S(2)}) %all-to-all-start.4) | async-done | bytes 1245216 | tf_op jit(solution)/shard_map/all_to_all | solution.py:123
  192.9 4.3 all-to-all-start.6
  199.0 9.0 %fusion.15 = (bf16[4,2,152,2048]{3,2,0,1:T(8,128)(2,1)}, f32[2,4,152,2048]{3,2,1,0:T(8,128)}) fusion(bf16[1,2,512,2048]{3,2,1,0:T(8,128)(2,1)} %all-gather.11.cloned.1.call-done, bf16[4,2,152,512]{3,2,1,0:T(8,128)(2,1)} %all-to-all-done.4), kind=kOutput, calls=%fused_computation.19 | convolution fusion | flops 2562588672 | bytes 20381696 | tf_op jit(solution)/shard_map/sjcd,jfd->sjcf/dot_general | solution.py:264
  208.0 4.5 all-to-all-done.6
  212.5 8.3 %bitcast_convert_fusion = bf16[2,2048,512]{2,1,0:T(8,128)(2,1)} fusion(bf16[4,2,152,2048]{3,2,0,1:T(8,128)(2,1)} %get-tuple-element.157, bf16[4,2,152,512]{3,2,1,0:T(8,128)(2,1)} %all-to-all-done.6, f32[4,2,152]{2,1,0:T(2,128)S(1)} %fusion.173), kind=kOutput, calls=%fused_computation.28 | convolution fusion | flops 2554101760 | bytes 10425088 | tf_op jit(solution)/shard_map/sjcf,sjcd->jfd/dot_general | solution.py:282
  220.9 8.4 %fusion.7 = bf16[4,2,152,2048]{3,2,0,1:T(8,128)(2,1)S(1)} fusion(f32[2,4,152,2048]{3,2,1,0:T(8,128)} %get-tuple-element.158, bf16[1,2,2048,512]{3,2,1,0:T(8,128)(2,1)} %all-gather.13.cloned.1.call-done, bf16[4,2,152,512]{3,2,1,0:T(8,128)(2,1)} %all-to-all-done.6, f32[4,2,152]{2,1,0:T(2,128)S(1)} %fusion.173), kind=kOutput, calls=%fused_computation.9 | convolution fusion | flops 2576908288 | bytes 20386560 | tf_op jit(solution)/shard_map/sjcd,jfd->sjcf/dot_general | solution.py:286
  233.3 4.5 all-to-all-start.7
  237.8 6.5 %fusion.63 = bf16[4,2,152,512]{3,2,0,1:T(8,128)(2,1)S(1)} fusion(bf16[4,2,152,2048]{3,2,0,1:T(8,128)(2,1)} %get-tuple-element.157, bf16[1,2,2048,512]{3,2,1,0:T(8,128)(2,1)} %all-gather.13.cloned.1.call-done), kind=kOutput, calls=%fused_computation.83 | convolution fusion | flops 2550759424 | bytes 10420224 | tf_op jit(solution)/shard_map/sjcf,jfd->sjcd/dot_general | solution.py:271
  245.5 7.5 %all-to-all-done.7 = bf16[4,2,152,512]{3,2,1,0:T(8,128)(2,1)} async-done(((bf16[4,2,152,512]{3,2,1,0:T(8,128)(2,1)}), bf16[4,2,152,512]{3,2,1,0:T(8,128)(2,1)}, u32[]{:S(2)}, u32[]{:S(2)}) %all-to-all-start.7) | async-done | bytes 1245216 | tf_op jit(solution)/shard_map/all_to_all | solution.py:123
  253.0 4.3 all-to-all-start.5
  257.3 8.3 %bitcast_convert_fusion.3 = bf16[2,512,2048]{2,1,0:T(8,128)(2,1)} fusion(bf16[4,2,152,512]{3,2,1,0:T(8,128)(2,1)} %all-to-all-done.4, bf16[4,2,152,2048]{3,2,0,1:T(8,128)(2,1)} %copy-done.73), kind=kOutput, calls=%fused_computation.31 | convolution fusion | flops 2552233984 | bytes 10420224 | tf_op jit(solution)/shard_map/sjcd,sjcf->jdf/dot_general | solution.py:294
  265.6 7.1 %all-to-all-done.5 = bf16[4,2,152,512]{3,2,1,0:T(8,128)(2,1)} async-done(((bf16[4,2,152,512]{3,2,1,0:T(8,128)(2,1)}), bf16[4,2,152,512]{3,2,1,0:T(8,128)(2,1)}, u32[]{:S(2)}, u32[]{:S(2)}) %all-to-all-start.5) | async-done | bytes 1245216 | tf_op jit(solution)/shard_map/all_to_all | solution.py:123
  274.9 3.3 fusion.103
  283.0 9.3 %attention_back.2 = bf16[416,1536]{1,0:T(8,128)(2,1)} custom-call(bf16[416,1536]{1,0:T(8,128)(2,1)} %convolution_convert_fusion.5.packed_ref, bf16[416,512]{1,0:T(8,128)(2,1)} %convolution_convert_fusion.10.grad_ref, f32[416,8]{1,0:T(8,128)} %get-tuple-element.33.total_ref), custom_call_target="tpu_custom_call" | custom-call | tf_op jit(solution)/shard_map/attention_back/pallas_call | solution.py:214
  292.4 3.6 multiply_reduce_fusion.7
  300.1 4.4 all-to-all-start.8
  313.2 3.6 convolution_convert_fusion.1
  316.9 3.6 concatenate.12
  322.0 8.3 %bitcast_convert_fusion.1 = bf16[2,2048,512]{2,1,0:T(8,128)(2,1)} fusion(bf16[4,2,152,2048]{3,2,0,1:T(8,128)(2,1)} %copy-done.72, bf16[4,2,152,512]{3,2,1,0:T(8,128)(2,1)} %all-to-all-done.8), kind=kOutput, calls=%fused_computation.29 | convolution fusion | flops 2552233984 | bytes 10420224 | tf_op jit(solution)/shard_map/sjcf,sjcd->jfd/dot_general | solution.py:282
  331.8 9.1 %fusion.13 = bf16[4,2,152,2048]{3,2,0,1:T(8,128)(2,1)S(1)} fusion(f32[2,2048,4,152]{1,3,2,0:T(8,128)} %get-tuple-element.151, bf16[2,2,2048,512]{3,2,1,0:T(8,128)(2,1)} %all-gather.9.cloned.1.call-done, bf16[4,2,152,512]{3,2,1,0:T(8,128)(2,1)} %all-to-all-done.8), kind=kOutput, calls=%fused_computation.15 | convolution fusion | flops 2575040512 | bytes 20381696 | tf_op jit(solution)/shard_map/sjcd,jfd->sjcf/dot_general | solution.py:286
  340.9 6.8 %fusion.67 = bf16[4,2,152,512]{3,2,0,1:T(8,128)(2,1)S(1)} fusion(bf16[4,2,152,2048]{3,2,0,1:T(8,128)(2,1)S(1)} %fusion.13, bf16[2,2,2048,512]{3,2,1,0:T(8,128)(2,1)} %all-gather.9.cloned.1.call-done), kind=kOutput, calls=%fused_computation.85 | convolution fusion | flops 2550759424 | bytes 10420224 | tf_op jit(solution)/shard_map/sjcf,jfd->sjcd/dot_general | solution.py:290
  348.9 4.3 all-to-all-start.9
  354.3 8.4 %bitcast_convert_fusion.2 = bf16[2,512,2048]{2,1,0:T(8,128)(2,1)} fusion(bf16[4,2,152,512]{3,2,1,0:T(8,128)(2,1)} %all-to-all-done.1, bf16[4,2,152,2048]{3,2,0,1:T(8,128)(2,1)} %copy-done.74), kind=kOutput, calls=%fused_computation.30 | convolution fusion | flops 2552233984 | bytes 10420224 | tf_op jit(solution)/shard_map/sjcd,sjcf->jdf/dot_general | solution.py:294
  362.7 5.8 %all-to-all-done.9 = bf16[4,2,152,512]{3,2,1,0:T(8,128)(2,1)} async-done(((bf16[4,2,152,512]{3,2,1,0:T(8,128)(2,1)}), bf16[4,2,152,512]{3,2,1,0:T(8,128)(2,1)}, u32[]{:S(2)}, u32[]{:S(2)}) %all-to-all-start.9) | async-done | bytes 1245216 | tf_op jit(solution)/shard_map/all_to_all | solution.py:123
  373.3 9.1 %attention_back.3 = bf16[416,1536]{1,0:T(8,128)(2,1)} custom-call(bf16[416,1536]{1,0:T(8,128)(2,1)} %convolution_convert_fusion.6.packed_ref, bf16[416,512]{1,0:T(8,128)(2,1)} %convolution_convert_fusion.9.grad_ref, f32[416,8]{1,0:T(8,128)} %get-tuple-element.37.total_ref), custom_call_target="tpu_custom_call" | custom-call | tf_op jit(solution)/shard_map/attention_back/pallas_call | solution.py:214
  387.2 3.7 convolution_convert_fusion
  390.9 4.4 concatenate.13
  398.1 4.3 all-to-all-start.11
  406.4 9.8 %all-to-all-done.11 = bf16[4,4,16,2060]{3,2,1,0:T(8,128)(2,1)} async-done(((bf16[4,4,16,2060]{3,2,1,0:T(8,128)(2,1)}), bf16[4,4,16,2060]{3,2,1,0:T(8,128)(2,1)}, u32[]{:S(2)}, u32[]{:S(2)}) %all-to-all-start.11) | async-done | bytes 1054752 | tf_op jit(solution)/shard_map/all_to_all | solution.py:123
  421.5 3.5 all-to-all-start.10
  428.2 10.5 %all-to-all-done.10 = bf16[4,4,16,2060]{3,2,1,0:T(8,128)(2,1)S(1)} async-done(((bf16[4,4,16,2060]{3,2,1,0:T(8,128)(2,1)}), bf16[4,4,16,2060]{3,2,1,0:T(8,128)(2,1)S(1)}, u32[]{:S(2)}, u32[]{:S(2)}) %all-to-all-start.10) | async-done | bytes 1054752 | tf_op jit(solution)/shard_map/all_to_all | solution.py:123
  441.4 4.6 collective-permute-done.1
  448.2 6.1 %collective-permute-done.2 = bf16[1,16,2060]{2,1,0:T(8,128)(2,1)S(1)} collective-permute-done((bf16[1,16,2060]{2,1,0:T(8,128)(2,1)S(1)}, bf16[1,16,2060]{2,1,0:T(8,128)(2,1)S(1)}, u32[]{:S(2)}, u32[]{:S(2)}) %collective-permute-start.2) | collective-permute-done | bytes 65952 | tf_op jit(solution)/shard_map/ppermute | solution.py:349
  454.4 9.7 %all_gather.19 = bf16[64,2,2060]{2,0,1:T(8,128)(2,1)S(1)} all-gather(bf16[16,2,2060]{2,0,1:T(8,128)(2,1)S(1)} %pad_maximum_fusion.1), channel_id=1, replica_groups=mesh['dp'=8,'expert'=4] {'expert'}, dimensions={0}, use_global_device_ids=true | all-gather | bytes 659200 | tf_op jit(solution)/shard_map/all_gather | solution.py:437
  470.6 17.2 %reduce-scatter.5.cloned.1.call-done = bf16[2,512,256]{2,1,0:T(8,128)(2,1)} async-done(((bf16[2,512,2048]{2,1,0:T(8,128)(2,1)}), bf16[2,512,256]{2,1,0:T(8,128)(2,1)}) %reduce-scatter.5.cloned.1.call-update) | async-done | bytes 524304 | tf_op jit(solution)/shard_map/reduce_scatter | solution.py:298
  (361 shorter events, 138.1 us)
Async XLA Ops:
  7.2 29.8 %all-gather.7.cloned.1.call-start = ((), (), s32[]{:S(2)}) async-start(), calls=%async_computation.16 | async-start | bytes 1253376 | tf_op jit(solution)/shard_map/all_gather | solution.py:63
  11.6 111.3 %all-gather.9.cloned.1.call-start = ((), (), s32[]{:S(2)}) async-start(), calls=%async_computation.17 | async-start | bytes 9437184 | tf_op jit(solution)/shard_map/all_gather | solution.py:96
  16.0 183.0 %all-gather.11.cloned.1.call-start = ((), (), s32[]{:S(2)}) async-start(), calls=%async_computation.22 | async-start | bytes 4718592 | tf_op jit(solution)/shard_map/all_gather | solution.py:98
  16.7 204.2 %all-gather.13.cloned.1.call-start = ((), (), s32[]{:S(2)}) async-start(), calls=%async_computation.23 | async-start | bytes 4718592 | tf_op jit(solution)/shard_map/all_gather | solution.py:99
  17.6 121.6 %copy-start.31 = (s32[416,1]{0,1:T(1,128)}, s32[416,1]{0,1:T(1,128)S(1)}, u32[]{:S(2)}) copy-start(s32[416,1]{0,1:T(1,128)S(1)} %get-tuple-element.142) | copy-start | bytes 4996
  17.6 121.7 %copy-start.33 = (s32[416,1]{0,1:T(1,128)}, s32[416,1]{0,1:T(1,128)S(1)}, u32[]{:S(2)}) copy-start(s32[416,1]{0,1:T(1,128)S(1)} %get-tuple-element.143) | copy-start | bytes 4996
  41.1 29.3 %all-to-all-start = ((bf16[4,128,2060]{1,2,0:T(8,128)(2,1)}), bf16[4,128,2060]{1,2,0:T(8,128)(2,1)S(1)}, u32[]{:S(2)}, u32[]{:S(2)}) async-start(bf16[4,128,2060]{1,2,0:T(8,128)(2,1)} %broadcast_in_dim.9), calls=%async_computation | async-start | bytes 4227072 | tf_op jit(solution)/shard_map/all_to_all | solution.py:123
  45.5 41.3 %copy-start.43 = (f32[2,208]{1,0:T(2,128)}, f32[2,208]{1,0:T(2,128)S(1)}, u32[]{:S(2)}) copy-start(f32[2,208]{1,0:T(2,128)S(1)} %broadcast_multiply_fusion.11) | copy-start | bytes 4996
  45.9 50.1 %copy-start.2 = (f32[2,208,512]{2,1,0:T(8,128)}, f32[2,208,512]{2,1,0:T(8,128)S(1)}, u32[]{:S(2)}) copy-start(f32[2,208,512]{2,1,0:T(8,128)S(1)} %pad_convert_fusion) | copy-start | bytes 2555908
  45.9 40.9 %copy-start.50 = (f32[2,208]{1,0:T(2,128)}, f32[2,208]{1,0:T(2,128)S(1)}, u32[]{:S(2)}) copy-start(f32[2,208]{1,0:T(2,128)S(1)} %add_rsqrt_fusion.3) | copy-start | bytes 4996
  73.4 29.5 %all-to-all-start.3 = ((bf16[4,128,2060]{1,2,0:T(8,128)(2,1)}), bf16[4,128,2060]{1,2,0:T(8,128)(2,1)}, u32[]{:S(2)}, u32[]{:S(2)}) async-start(bf16[4,128,2060]{1,2,0:T(8,128)(2,1)} %broadcast_in_dim.11), calls=%async_computation.3 | async-start | bytes 4227072 | tf_op jit(solution)/shard_map/all_to_all | solution.py:123
  85.1 27.0 %copy-start.35 = (bf16[512,12]{0,1:T(8,128)(2,1)}, bf16[512,12]{0,1:T(8,128)(2,1)S(1)}, u32[]{:S(2)}) copy-start(bf16[512,12]{0,1:T(8,128)(2,1)S(1)} %reshape.339) | copy-start | bytes 36868
  86.7 11.1 %copy-start.41 = (f32[1,512]{1,0:T(1,128)}, f32[1,512]{1,0:T(1,128)S(1)}, u32[]{:S(2)}) copy-start(f32[1,512]{1,0:T(1,128)S(1)} %get-tuple-element.144) | copy-start | bytes 6148
  98.0 14.0 %copy-start.8 = (bf16[416,512]{1,0:T(8,128)(2,1)}, bf16[416,512]{1,0:T(8,128)(2,1)S(1)}, u32[]{:S(2)}) copy-start(bf16[416,512]{1,0:T(8,128)(2,1)S(1)} %add_convert_fusion.4) | copy-start | bytes 1277956
  98.0 9.6 %copy-start.62 = (s32[416]{0:T(512)S(1)}, s32[416]{0:T(512)}, u32[]{:S(2)}) copy-start(s32[416]{0:T(512)} %get-tuple-element.106) | copy-start | bytes 4996
  98.1 10.2 %copy-start.29 = (bf16[2,197,512]{2,0,1:T(2,128)(2,1)S(1)}, bf16[2,197,512]{2,0,1:T(2,128)(2,1)}, u32[]{:S(2)}) copy-start(bf16[2,197,512]{2,0,1:T(2,128)(2,1)} %param.11) | copy-start | bytes 1210372
  102.9 20.1 %all-to-all-start.1 = ((bf16[4,2,152,512]{3,2,1,0:T(8,128)(2,1)}), bf16[4,2,152,512]{3,2,1,0:T(8,128)(2,1)}, u32[]{:S(2)}, u32[]{:S(2)}) async-start(bf16[4,2,152,512]{3,2,1,0:T(8,128)(2,1)} %bitcast.32), calls=%async_computation.1 | async-start | bytes 2490368 | tf_op jit(solution)/shard_map/all_to_all | solution.py:123
  134.9 19.6 %all-to-all-start.2 = ((bf16[4,2,152,512]{3,2,1,0:T(8,128)(2,1)}), bf16[4,2,152,512]{3,2,1,0:T(8,128)(2,1)}, u32[]{:S(2)}, u32[]{:S(2)}) async-start(bf16[4,2,152,512]{3,2,1,0:T(8,128)(2,1)} %copy.184), calls=%async_computation.2 | async-start | bytes 2490368 | tf_op jit(solution)/shard_map/all_to_all | solution.py:123
  139.8 14.8 %copy-start.65 = (s32[416]{0:T(512)S(1)}, s32[416]{0:T(512)}, u32[]{:S(2)}) copy-start(s32[416]{0:T(512)} %get-tuple-element.168) | copy-start | bytes 4996
  142.6 26.6 %copy-start.6 = (bf16[8,4,16,512]{3,2,1,0:T(8,128)(2,1)}, bf16[8,4,16,512]{3,2,1,0:T(8,128)(2,1)S(1)}, u32[]{:S(2)}) copy-start(bf16[8,4,16,512]{3,2,1,0:T(8,128)(2,1)S(1)} %copy.189) | copy-start | bytes 1572868
  142.6 18.2 %copy-start.69 = (f32[1,512]{1,0:T(1,128)}, f32[1,512]{1,0:T(1,128)S(1)}, u32[]{:S(2)}) copy-start(f32[1,512]{1,0:T(1,128)S(1)} %get-tuple-element.169) | copy-start | bytes 6148
  142.7 153.3 %copy-start.60 = (f32[1,512]{1,0:T(1,128)}, f32[1,512]{1,0:T(1,128)S(1)}, u32[]{:S(2)}) copy-start(f32[1,512]{1,0:T(1,128)S(1)} %get-tuple-element.139) | copy-start | bytes 6148
  160.5 135.4 %copy-start.45 = (f32[416]{0:T(512)}, f32[416]{0:T(512)S(1)}, u32[]{:S(2)}) copy-start(f32[416]{0:T(512)S(1)} %broadcast_multiply_fusion.9) | copy-start | bytes 4996
  160.8 135.2 %copy-start.54 = (f32[416]{0:T(512)}, f32[416]{0:T(512)S(1)}, u32[]{:S(2)}) copy-start(f32[416]{0:T(512)S(1)} %add_rsqrt_fusion.1) | copy-start | bytes 4996
  173.1 19.8 %all-to-all-start.4 = ((bf16[4,2,152,512]{3,2,1,0:T(8,128)(2,1)}), bf16[4,2,152,512]{3,2,1,0:T(8,128)(2,1)}, u32[]{:S(2)}, u32[]{:S(2)}) async-start(bf16[4,2,152,512]{3,2,1,0:T(8,128)(2,1)} %bitcast.321), calls=%async_computation.4 | async-start | bytes 2490368 | tf_op jit(solution)/shard_map/all_to_all | solution.py:123
  192.9 19.6 %all-to-all-start.6 = ((bf16[4,2,152,512]{3,2,1,0:T(8,128)(2,1)}), bf16[4,2,152,512]{3,2,1,0:T(8,128)(2,1)}, u32[]{:S(2)}, u32[]{:S(2)}) async-start(bf16[4,2,152,512]{3,2,1,0:T(8,128)(2,1)} %bitcast.320), calls=%async_computation.6 | async-start | bytes 2490368 | tf_op jit(solution)/shard_map/all_to_all | solution.py:123
  197.1 270.8 %reduce-scatter.11.cloned.1.call-start = ((), (), s32[]{:S(2)}) async-start(), calls=%async_computation.21 | async-start | bytes 4718592 | tf_op jit(solution)/shard_map/reduce_scatter | solution.py:285
  233.3 19.7 %all-to-all-start.7 = ((bf16[4,2,152,512]{3,2,1,0:T(8,128)(2,1)}), bf16[4,2,152,512]{3,2,1,0:T(8,128)(2,1)}, u32[]{:S(2)}, u32[]{:S(2)}) async-start(bf16[4,2,152,512]{3,2,1,0:T(8,128)(2,1)} %copy.196), calls=%async_computation.7 | async-start | bytes 2490368 | tf_op jit(solution)/shard_map/all_to_all | solution.py:123
  253.0 19.7 %all-to-all-start.5 = ((bf16[4,2,152,512]{3,2,1,0:T(8,128)(2,1)}), bf16[4,2,152,512]{3,2,1,0:T(8,128)(2,1)}, u32[]{:S(2)}, u32[]{:S(2)}) async-start(bf16[4,2,152,512]{3,2,1,0:T(8,128)(2,1)} %copy.192), calls=%async_computation.5 | async-start | bytes 2490368 | tf_op jit(solution)/shard_map/all_to_all | solution.py:123
  300.1 11.9 %copy-start.21 = (bf16[416,512]{1,0:T(8,128)(2,1)S(1)}, bf16[416,512]{1,0:T(8,128)(2,1)}, u32[]{:S(2)}) copy-start(bf16[416,512]{1,0:T(8,128)(2,1)} %get-tuple-element.28) | copy-start | bytes 1277956
  300.1 22.0 %all-to-all-start.8 = ((bf16[4,2,152,512]{3,2,1,0:T(8,128)(2,1)}), bf16[4,2,152,512]{3,2,1,0:T(8,128)(2,1)}, u32[]{:S(2)}, u32[]{:S(2)}) async-start(bf16[4,2,152,512]{3,2,1,0:T(8,128)(2,1)} %bitcast.319), calls=%async_computation.8 | async-start | bytes 2490368 | tf_op jit(solution)/shard_map/all_to_all | solution.py:123
  304.5 163.5 %reduce-scatter.9.cloned.1.call-start = ((), (), s32[]{:S(2)}) async-start(), calls=%async_computation.20 | async-start | bytes 4718592 | tf_op jit(solution)/shard_map/reduce_scatter | solution.py:285
  330.4 140.2 %reduce-scatter.7.cloned.1.call-start = ((), (), s32[]{:S(2)}) async-start(), calls=%async_computation.19 | async-start | bytes 4718592 | tf_op jit(solution)/shard_map/reduce_scatter | solution.py:298
  348.9 19.6 %all-to-all-start.9 = ((bf16[4,2,152,512]{3,2,1,0:T(8,128)(2,1)}), bf16[4,2,152,512]{3,2,1,0:T(8,128)(2,1)}, u32[]{:S(2)}, u32[]{:S(2)}) async-start(bf16[4,2,152,512]{3,2,1,0:T(8,128)(2,1)} %copy.206), calls=%async_computation.9 | async-start | bytes 2490368 | tf_op jit(solution)/shard_map/all_to_all | solution.py:123
  353.2 134.7 %reduce-scatter.5.cloned.1.call-start = ((), (), s32[]{:S(2)}) async-start(), calls=%async_computation.18 | async-start | bytes 4718592 | tf_op jit(solution)/shard_map/reduce_scatter | solution.py:298
  354.3 14.1 %copy-start.57 = (s32[416]{0:T(512)S(1)}, s32[416]{0:T(512)}, u32[]{:S(2)}) copy-start(s32[416]{0:T(512)} %get-tuple-element.167) | copy-start | bytes 4996
  354.3 14.1 %copy-start.66 = (s32[416]{0:T(512)S(1)}, s32[416]{0:T(512)}, u32[]{:S(2)}) copy-start(s32[416]{0:T(512)} %get-tuple-element.168) | copy-start | bytes 4996
  354.3 40.9 %collective-permute-start.3 = (bf16[4,4,16,2060]{3,2,1,0:T(8,128)(2,1)}, bf16[4,4,16,2060]{3,2,1,0:T(8,128)(2,1)}, u32[]{:S(2)}, u32[]{:S(2)}) collective-permute-start(bf16[4,4,16,2060]{3,2,1,0:T(8,128)(2,1)} %dynamic-slice_bitcast_fusion), channel_id=1, source_target_pairs={{0,4},{4,0},{8,12},{12,8},{16,20},{20,16},{24,28},{28,24},{1,5},{5... | collective-permute-start | bytes 3164168 | tf_op jit(solution)/shard_map/ppermute | solution.py:349
  372.1 10.4 %copy-start.3 = (f32[2,208,512]{2,1,0:T(8,128)S(1)}, f32[2,208,512]{2,1,0:T(8,128)}, u32[]{:S(2)}) copy-start(f32[2,208,512]{2,1,0:T(8,128)} %copy-done.2) | copy-start | bytes 2555908
  372.1 10.4 %copy-start.23 = (bf16[8,4,16,1536]{3,2,1,0:T(8,128)(2,1)S(1)}, bf16[8,4,16,1536]{3,2,1,0:T(8,128)(2,1)}, u32[]{:S(2)}) copy-start(bf16[8,4,16,1536]{3,2,1,0:T(8,128)(2,1)} %copy-done.22) | copy-start | bytes 4718596
  372.1 10.3 %copy-start.47 = (f32[1,512]{1,0:T(1,128)S(1)}, f32[1,512]{1,0:T(1,128)}, u32[]{:S(2)}) copy-start(f32[1,512]{1,0:T(1,128)} %copy-done.46) | copy-start | bytes 6148
  398.1 18.1 %all-to-all-start.11 = ((bf16[4,4,16,2060]{3,2,1,0:T(8,128)(2,1)}), bf16[4,4,16,2060]{3,2,1,0:T(8,128)(2,1)}, u32[]{:S(2)}, u32[]{:S(2)}) async-start(bf16[4,4,16,2060]{3,2,1,0:T(8,128)(2,1)} %fusion.50), calls=%async_computation.11 | async-start | bytes 2228224 | tf_op jit(solution)/shard_map/all_to_all | solution.py:123
  405.3 13.7 %collective-permute-start = (bf16[4,4,16,2060]{3,2,1,0:T(8,128)(2,1)}, bf16[4,4,16,2060]{3,2,1,0:T(8,128)(2,1)}, u32[]{:S(2)}, u32[]{:S(2)}) collective-permute-start(bf16[4,4,16,2060]{3,2,1,0:T(8,128)(2,1)} %bitcast.293), channel_id=1, source_target_pairs={{0,4},{4,0},{8,12},{12,8},{16,20},{20,16},{24,28},{28,24},{1,5},{5... | collective-permute-start | bytes 3164168 | tf_op jit(solution)/shard_map/ppermute | solution.py:349
  417.6 10.5 %collective-permute-start.4 = (bf16[2,16,2060]{2,1,0:T(8,128)(2,1)S(1)}, bf16[2,16,2060]{2,1,0:T(8,128)(2,1)S(1)}, u32[]{:S(2)}, u32[]{:S(2)}) collective-permute-start(bf16[2,16,2060]{2,1,0:T(8,128)(2,1)S(1)} %dynamic-slice_bitcast_fusion.1), channel_id=1, source_target_pairs={{0,8},{4,12},{8,0},{12,4},{16,24},{20,28},{24,16},{28,20},{1,9},{5... | collective-permute-start | bytes 395528 | tf_op jit(solution)/shard_map/ppermute | solution.py:349
  421.5 17.1 %all-to-all-start.10 = ((bf16[4,4,16,2060]{3,2,1,0:T(8,128)(2,1)}), bf16[4,4,16,2060]{3,2,1,0:T(8,128)(2,1)S(1)}, u32[]{:S(2)}, u32[]{:S(2)}) async-start(bf16[4,4,16,2060]{3,2,1,0:T(8,128)(2,1)} %fusion.51), calls=%async_computation.10 | async-start | bytes 2228224 | tf_op jit(solution)/shard_map/all_to_all | solution.py:123
  438.8 7.2 %collective-permute-start.1 = (bf16[2,16,2060]{2,1,0:T(8,128)(2,1)S(1)}, bf16[2,16,2060]{2,1,0:T(8,128)(2,1)S(1)}, u32[]{:S(2)}, u32[]{:S(2)}) collective-permute-start(bf16[2,16,2060]{2,1,0:T(8,128)(2,1)S(1)} %dynamic-slice_bitcast_fusion.2), channel_id=1, source_target_pairs={{0,8},{4,12},{8,0},{12,4},{16,24},{20,28},{24,16},{28,20},{1,9},{5... | collective-permute-start | bytes 395528 | tf_op jit(solution)/shard_map/ppermute | solution.py:349
  439.6 8.5 %collective-permute-start.5 = (bf16[1,16,2060]{2,1,0:T(8,128)(2,1)S(1)}, bf16[1,16,2060]{2,1,0:T(8,128)(2,1)S(1)}, u32[]{:S(2)}, u32[]{:S(2)}) collective-permute-start(bf16[1,16,2060]{2,1,0:T(8,128)(2,1)S(1)} %constant_dynamic-slice_fusion), channel_id=1, source_target_pairs={{0,16},{4,20},{8,24},{12,28},{16,0},{20,4},{24,8},{28,12},{1,17},{... | collective-permute-start | bytes 197768 | tf_op jit(solution)/shard_map/ppermute | solution.py:349
  446.1 8.2 %collective-permute-start.2 = (bf16[1,16,2060]{2,1,0:T(8,128)(2,1)S(1)}, bf16[1,16,2060]{2,1,0:T(8,128)(2,1)S(1)}, u32[]{:S(2)}, u32[]{:S(2)}) collective-permute-start(bf16[1,16,2060]{2,1,0:T(8,128)(2,1)S(1)} %constant_dynamic-slice_fusion.1), channel_id=1, source_target_pairs={{0,16},{4,20},{8,24},{12,28},{16,0},{20,4},{24,8},{28,12},{1,17},{... | collective-permute-start | bytes 197768 | tf_op jit(solution)/shard_map/ppermute | solution.py:349
  (53 other events, 174.1 us)
Sparse Core Ops, SparseCore 0:
  11.7 25.2 all-gather.6
  38.6 81.4 all-gather.8
  121.7 46.3 all-gather.10
  169.5 45.0 all-gather.12
  221.0 48.8 reduce-scatter.10
  330.5 50.2 reduce-scatter.8
  383.1 51.3 reduce-scatter.6
  436.8 51.0 reduce-scatter.4

commit v7 on v6

--- a/solution.py
+++ b/solution.py
@@ -59,19 +59,34 @@
         [w_qkv, w_proj, w_router, jnp.swapaxes(norm_gains, 1, 2), jnp.swapaxes(norm_shifts, 1, 2)],
         axis=2,
     )
-    packed = lax.dynamic_slice_in_dim(packed, rank * piece, piece, axis=1)
-    return lax.all_gather(packed, "dp", axis=1, tiled=True)
-
-
-def spread_dense(quarter, experts):
-    peers, shares = lax.axis_size("expert"), lax.axis_size("dp")
-    rows, columns = quarter.shape
-    parts = exchange(jnp.broadcast_to(quarter[None], (peers, rows, columns)))
-    width = peers * rows
-    parts = parts.reshape(peers, shares, rows // shares, columns)
+    block = lax.dynamic_slice_in_dim(packed, rank * piece, piece, axis=1)[None]
+    place, size, step = lax.axis_index("dp"), lax.axis_size("dp"), 2
+    while step < size:
+        moved = lax.ppermute(block, "dp", [(source, source ^ step) for source in range(size)])
+        upper = (place // step) % 2 == 1
+        first, second = jnp.where(upper, moved, block), jnp.where(upper, block, moved)
+        block = jnp.concatenate([first, second], axis=0)
+        step = 2 * step
+    return block
+
+
+def spread_quarter(quarter):
+    parts = jnp.broadcast_to(quarter[None], (lax.axis_size("expert"),) + quarter.shape)
+    return exchange(parts)
+
+
+def join_cores(parts, experts):
+    size = lax.axis_size("dp")
+    peers, chips, rows, columns = parts.shape
+    other = lax.ppermute(parts, "dp", [(source, source ^ 1) for source in range(size)])
+    core = lax.axis_index("dp") % 2
+    width = 2 * peers * chips * rows
+    own = lax.broadcasted_iota(jnp.int32, (1, 2, 1, 1, 1), 1) == core
 
     def whole(start, stop):
-        return parts[..., start:stop].swapaxes(0, 1).reshape(width, stop - start)
+        mine = parts[..., start:stop].swapaxes(0, 1)[:, None]
+        theirs = other[..., start:stop].swapaxes(0, 1)[:, None]
+        return jnp.where(own, mine, theirs).reshape(width, stop - start)
 
     base = 4 * width
     wide = whole(base, columns)
@@ -387,13 +402,18 @@
     last = tables[LAYERS - 1]
     slots = slots_of(cot_low, last[2] + last[3], block_shape)
     cot_rows = exchange(slots)
+    parts = []
     for which in range(LAYERS):
-        dense.append(spread_dense(quarters[which], experts_total))
+        parts.append(spread_quarter(quarters[:, which]))
+    dense.append(join_cores(parts[0], experts_total))
     attn_saved, moe_saved, kept = [], [], []
     grad_result = None
     for which in range(LAYERS):
         table = tables[which]
         resid_mid, attn_part, moe_part = attend_forward(resid, dense[which], table)
+        if which < LAYERS - 1:
+            parts[which + 1], resid_mid = lax.optimization_barrier((parts[which + 1], resid_mid))
+            dense.append(join_cores(parts[which + 1], experts_total))
         outgoing = slots_of(moe_part[2], table[2] + table[3], block_shape)
         incoming = exchange(outgoing)
         hidden_pre, hidden_act = experts_hidden(incoming, experts[which][0])
@@ -434,6 +454,9 @@
     for which in reversed(range(LAYERS)):
         smalls[which] = sum_small(smalls[which])
     both = jnp.stack(smalls, axis=1)
+    grad_first = jnp.stack(firsts).astype(jnp.float32)
+    grad_second = jnp.stack(seconds).astype(jnp.float32)
+    both, grad_first, grad_second = lax.optimization_barrier((both, grad_first, grad_second))
     total = lax.all_gather(both, "expert", axis=0, tiled=True)
     total = total.swapaxes(0, 1).astype(jnp.float32)
     grad_images = grad.reshape(images, SEQ_PAD, width)[:, :length]
@@ -446,8 +469,8 @@
         wide[:, :, :experts_total],
         jnp.swapaxes(wide[:, :, experts_total : experts_total + 2], 1, 2),
         jnp.swapaxes(wide[:, :, experts_total + 2 :], 1, 2),
-        jnp.stack(firsts).astype(jnp.float32),
-        jnp.stack(seconds).astype(jnp.float32),
+        grad_first,
+        grad_second,
     )
 
 

time: 507 us -> 524 us (1.034)
  waiting for transfers between devices: 150 us -> 164 us
  other arithmetic: 23.6 us -> 33.5 us
  local copies, waits for them, and re-layouts: 69.4 us -> 59.8 us
    ppermute x0 -> x4, waiting for transfers between devices: none -> 32.3 us  [the longest x2 32.3 us: gather_quarters(): lax.ppermute(block, 'dp', [(source, source ^ step) for source in range(si...]
    all_to_all x12, waiting for transfers between devices: 103 us -> 86.1 us  [exchange(): lax.all_to_all(block, 'expert', split_axis=0, concat_axis=0, tiled=True)]
    all_gather x1 -> x0, waiting for transfers between devices: 16.3 us -> none  [gather_quarters(): return lax.all_gather(packed, 'dp', axis=1, tiled=True)]
    reduce_scatter x2, waiting for transfers between devices: 17.2 us -> 29 us  [experts_backward(): lax.psum_scatter(grad_first, 'dp', scatter_dimension=2, tiled=True)]
    select_n x0 -> x8, other arithmetic: none -> 7.89 us  [the longest x6 7.76 us: whole(): return jnp.where(own, mine, theirs).reshape(width, stop - start)]
    ppermute x0 -> x4, starting transfers between devices: none -> 6.37 us  [the longest x2 5.77 us: gather_quarters(): lax.ppermute(block, 'dp', [(source, source ^ step) for source in range(si...]
    all_to_all x2 -> x0, local copies, waits for them, and re-layouts: 5.88 us -> none  [exchange(): lax.all_to_all(block, 'expert', split_axis=0, concat_axis=0, tiled=True)]
  transfers between devices with their start and end apart: 26 -> 29, of which waited for: 16 -> 16; matrix products, arithmetic and copies ran while one was open for 45% -> 43% of each run, Pallas kernels for 6% -> 6%
where the time goes in v7:
time: 524 us; the launch traced here: 515 us
  waiting for transfers between devices  164 us (31%)
  matrix products  140 us (27%)
  starting transfers between devices  60 us (11%)
  local copies, waits for them, and re-layouts  59.8 us (11%)
  other arithmetic  33.5 us (6%)
  Pallas kernels  31.3 us (6%)
  between operations  16 us (3%)
  blocking collectives  10.2 us (2%)
    all_to_all x12, waiting for transfers between devices, exchange(): lax.all_to_all(block, 'expert', split_axis=0, concat_axis=0, tiled=True)  86.1 us
    all_to_all x12, starting transfers between devices, exchange(): lax.all_to_all(block, 'expert', split_axis=0, concat_axis=0, tiled=True)  51.4 us
    ppermute x2, waiting for transfers between devices, gather_quarters(): lax.ppermute(block, 'dp', [(source, source ^ step) for source in range(si...  32.3 us
    reduce_scatter x2, waiting for transfers between devices, experts_backward(): lax.psum_scatter(grad_first, 'dp', scatter_dimension=2, tiled=True)  29 us
    pallas_call x2, Pallas kernels, attention_back(): pl.pallas_call(attention_back_kernel, grid=(rows // SEQ_PAD,), in_specs=[...  18.6 us
    dot_general x2, matrix products, experts_backward(): jnp.einsum('sjcd,jfd->sjcf', grad_result, second_full, preferred_element_...  17.8 us
    dot_general x2, matrix products, experts_hidden(): jnp.einsum('sjcd,jfd->sjcf', incoming, first_full, preferred_element_type...  17 us
    dot_general x2, matrix products, experts_backward(): jnp.einsum('sjcd,sjcf->jdf', incoming, grad_pre, preferred_element_type=j...  16.7 us
  transfers between devices with their start and end apart: 29, of which 16 were waited for; matrix products, arithmetic and copies ran while one was open for 43% of the time, Pallas kernels for 6%

profile of v7, /device:TPU:0, one launch (start us, length us, event | category | flops | bytes accessed | tf_op | source)
XLA Modules:
  0.0 514.6 jit_solution(520297267218386535)
XLA Ops:
  23.5 32.3 %collective-permute-done.1 = bf16[2,2,16,2060]{3,2,0,1:T(8,128)(2,1)S(1)} collective-permute-done((bf16[2,2,16,2060]{3,2,0,1:T(8,128)(2,1)S(1)}, bf16[2,2,16,2060]{3,2,0,1:T(8,128)(2,1)S(1)}, u32[]{:S(2)}, u32[]{:S(2)}) %collective-permute-start.1) | collective-permute-done | bytes 263712 | tf_op jit(solution)/shard_map/ppermute | solution.py:65
  57.7 3.7 all-to-all-start.1
  64.3 8.4 %all-to-all-done.1 = bf16[4,4,16,2060]{3,2,1,0:T(8,128)(2,1)S(1)} async-done(((bf16[4,4,16,2060]{3,2,1,0:T(8,128)(2,1)}), bf16[4,4,16,2060]{3,2,1,0:T(8,128)(2,1)S(1)}, u32[]{:S(2)}, u32[]{:S(2)}) %all-to-all-start.1) | async-done | bytes 1054752 | tf_op jit(solution)/shard_map/all_to_all | solution.py:138
  75.4 4.2 all-to-all-start
  93.9 6.4 %attention.2 = (bf16[416,512]{1,0:T(8,128)(2,1)}, f32[416,8]{1,0:T(8,128)}) custom-call(bf16[416,1536]{1,0:T(8,128)(2,1)} %convolution_convert_fusion.6.packed_ref), custom_call_target="tpu_custom_call" | custom-call | tf_op jit(solution)/shard_map/attention/pallas_call | solution.py:214
  106.2 4.9 all-to-all-start.2
  115.8 11.8 %all-to-all-done.2 = bf16[4,2,152,512]{3,2,1,0:T(8,128)(2,1)} async-done(((bf16[4,2,152,512]{3,2,1,0:T(8,128)(2,1)}), bf16[4,2,152,512]{3,2,1,0:T(8,128)(2,1)}, u32[]{:S(2)}, u32[]{:S(2)}) %all-to-all-start.2) | async-done | bytes 1245216 | tf_op jit(solution)/shard_map/all_to_all | solution.py:138
  127.6 8.0 %fusion.19 = (bf16[4,2,152,2048]{3,2,0,1:T(8,128)(2,1)S(1)}, f32[2,2048,4,152]{1,3,2,0:T(8,128)}) fusion(bf16[4,2,152,512]{3,2,1,0:T(8,128)(2,1)} %all-to-all-done.2, bf16[2,2,2048,512]{3,2,1,0:T(8,128)(2,1)} %all-gather.6.cloned.1.call-done), kind=kOutput, calls=%fused_computation.25 | convolution fusion | flops 2562588672 | bytes 20381696 | tf_op jit(solution)/shard_map/sjcd,jfd->sjcf/dot_general | solution.py:279
  139.6 4.4 all-to-all-start.3
  147.2 4.3 bitcast_select_fusion
  151.6 8.1 %all-to-all-done.3 = bf16[4,2,152,512]{3,2,1,0:T(8,128)(2,1)} async-done(((bf16[4,2,152,512]{3,2,1,0:T(8,128)(2,1)}), bf16[4,2,152,512]{3,2,1,0:T(8,128)(2,1)}, u32[]{:S(2)}, u32[]{:S(2)}) %all-to-all-start.3) | async-done | bytes 1245216 | tf_op jit(solution)/shard_map/all_to_all | solution.py:138
  162.0 3.9 fusion.162
  168.2 6.3 %attention.3 = (bf16[416,512]{1,0:T(8,128)(2,1)}, f32[416,8]{1,0:T(8,128)}) custom-call(bf16[416,1536]{1,0:T(8,128)(2,1)} %convolution_convert_fusion.5.packed_ref), custom_call_target="tpu_custom_call" | custom-call | tf_op jit(solution)/shard_map/attention/pallas_call | solution.py:214
  178.5 4.6 all-to-all-start.4
  185.4 12.9 %all-to-all-done.4 = bf16[4,2,152,512]{3,2,1,0:T(8,128)(2,1)} async-done(((bf16[4,2,152,512]{3,2,1,0:T(8,128)(2,1)}), bf16[4,2,152,512]{3,2,1,0:T(8,128)(2,1)}, u32[]{:S(2)}, u32[]{:S(2)}) %all-to-all-start.4) | async-done | bytes 1245216 | tf_op jit(solution)/shard_map/all_to_all | solution.py:138
  198.2 4.3 all-to-all-start.6
  204.4 8.9 %fusion.15 = (bf16[4,2,152,2048]{3,2,0,1:T(8,128)(2,1)}, f32[2,4,152,2048]{3,2,1,0:T(8,128)}) fusion(bf16[1,2,512,2048]{3,2,1,0:T(8,128)(2,1)} %all-gather.8.cloned.1.call-done, bf16[4,2,152,512]{3,2,1,0:T(8,128)(2,1)} %all-to-all-done.4), kind=kOutput, calls=%fused_computation.19 | convolution fusion | flops 2562588672 | bytes 20381696 | tf_op jit(solution)/shard_map/sjcd,jfd->sjcf/dot_general | solution.py:279
  213.3 4.5 all-to-all-done.6
  217.8 8.3 %bitcast_convert_fusion = bf16[2,2048,512]{2,1,0:T(8,128)(2,1)} fusion(bf16[4,2,152,2048]{3,2,0,1:T(8,128)(2,1)} %get-tuple-element.164, bf16[4,2,152,512]{3,2,1,0:T(8,128)(2,1)} %all-to-all-done.6, f32[4,2,152]{2,1,0:T(2,128)S(1)} %fusion.176), kind=kOutput, calls=%fused_computation.28 | convolution fusion | flops 2554101760 | bytes 10425088 | tf_op jit(solution)/shard_map/sjcf,sjcd->jfd/dot_general | solution.py:297
  226.2 8.4 %fusion.7 = bf16[4,2,152,2048]{3,2,0,1:T(8,128)(2,1)S(1)} fusion(f32[2,4,152,2048]{3,2,1,0:T(8,128)} %get-tuple-element.165, bf16[1,2,2048,512]{3,2,1,0:T(8,128)(2,1)} %all-gather.10.cloned.1.call-done, bf16[4,2,152,512]{3,2,1,0:T(8,128)(2,1)} %all-to-all-done.6, f32[4,2,152]{2,1,0:T(2,128)S(1)} %fusion.176), kind=kOutput, calls=%fused_computation.9 | convolution fusion | flops 2576908288 | bytes 20386560 | tf_op jit(solution)/shard_map/sjcd,jfd->sjcf/dot_general | solution.py:301
  238.7 4.5 all-to-all-start.7
  243.2 6.5 %fusion.63 = bf16[4,2,152,512]{3,2,0,1:T(8,128)(2,1)S(1)} fusion(bf16[4,2,152,2048]{3,2,0,1:T(8,128)(2,1)} %get-tuple-element.164, bf16[1,2,2048,512]{3,2,1,0:T(8,128)(2,1)} %all-gather.10.cloned.1.call-done), kind=kOutput, calls=%fused_computation.84 | convolution fusion | flops 2550759424 | bytes 10420224 | tf_op jit(solution)/shard_map/sjcf,jfd->sjcd/dot_general | solution.py:286
  250.9 7.5 %all-to-all-done.7 = bf16[4,2,152,512]{3,2,1,0:T(8,128)(2,1)} async-done(((bf16[4,2,152,512]{3,2,1,0:T(8,128)(2,1)}), bf16[4,2,152,512]{3,2,1,0:T(8,128)(2,1)}, u32[]{:S(2)}, u32[]{:S(2)}) %all-to-all-start.7) | async-done | bytes 1245216 | tf_op jit(solution)/shard_map/all_to_all | solution.py:138
  258.5 4.3 all-to-all-start.5
  262.8 8.3 %bitcast_convert_fusion.3 = bf16[2,512,2048]{2,1,0:T(8,128)(2,1)} fusion(bf16[4,2,152,512]{3,2,1,0:T(8,128)(2,1)} %all-to-all-done.4, bf16[4,2,152,2048]{3,2,0,1:T(8,128)(2,1)} %copy-done.81), kind=kOutput, calls=%fused_computation.31 | convolution fusion | flops 2552233984 | bytes 10420224 | tf_op jit(solution)/shard_map/sjcd,sjcf->jdf/dot_general | solution.py:309
  271.1 7.0 %all-to-all-done.5 = bf16[4,2,152,512]{3,2,1,0:T(8,128)(2,1)} async-done(((bf16[4,2,152,512]{3,2,1,0:T(8,128)(2,1)}), bf16[4,2,152,512]{3,2,1,0:T(8,128)(2,1)}, u32[]{:S(2)}, u32[]{:S(2)}) %all-to-all-start.5) | async-done | bytes 1245216 | tf_op jit(solution)/shard_map/all_to_all | solution.py:138
  280.4 3.3 fusion.103
  288.5 9.3 %attention_back.2 = bf16[416,1536]{1,0:T(8,128)(2,1)} custom-call(bf16[416,1536]{1,0:T(8,128)(2,1)} %convolution_convert_fusion.5.packed_ref, bf16[416,512]{1,0:T(8,128)(2,1)} %convolution_convert_fusion.10.grad_ref, f32[416,8]{1,0:T(8,128)} %get-tuple-element.40.total_ref), custom_call_target="tpu_custom_call" | custom-call | tf_op jit(solution)/shard_map/attention_back/pallas_call | solution.py:229
  297.9 3.6 multiply_reduce_fusion.7
  305.6 4.4 all-to-all-start.8
  322.0 3.6 concatenate.20
  327.2 8.3 %bitcast_convert_fusion.1 = bf16[2,2048,512]{2,1,0:T(8,128)(2,1)} fusion(bf16[4,2,152,2048]{3,2,0,1:T(8,128)(2,1)} %copy-done.80, bf16[4,2,152,512]{3,2,1,0:T(8,128)(2,1)} %all-to-all-done.8), kind=kOutput, calls=%fused_computation.29 | convolution fusion | flops 2552233984 | bytes 10420224 | tf_op jit(solution)/shard_map/sjcf,sjcd->jfd/dot_general | solution.py:297
  336.9 9.4 %fusion.13 = bf16[4,2,152,2048]{3,2,0,1:T(8,128)(2,1)S(1)} fusion(f32[2,2048,4,152]{1,3,2,0:T(8,128)} %get-tuple-element.158, bf16[2,2,2048,512]{3,2,1,0:T(8,128)(2,1)} %all-gather.6.cloned.1.call-done, bf16[4,2,152,512]{3,2,1,0:T(8,128)(2,1)} %all-to-all-done.8), kind=kOutput, calls=%fused_computation.15 | convolution fusion | flops 2575040512 | bytes 20381696 | tf_op jit(solution)/shard_map/sjcd,jfd->sjcf/dot_general | solution.py:301
  346.3 6.7 %fusion.67 = bf16[4,2,152,512]{3,2,0,1:T(8,128)(2,1)S(1)} fusion(bf16[4,2,152,2048]{3,2,0,1:T(8,128)(2,1)S(1)} %fusion.13, bf16[2,2,2048,512]{3,2,1,0:T(8,128)(2,1)} %all-gather.6.cloned.1.call-done), kind=kOutput, calls=%fused_computation.86 | convolution fusion | flops 2550759424 | bytes 10420224 | tf_op jit(solution)/shard_map/sjcf,jfd->sjcd/dot_general | solution.py:305
  354.2 4.3 all-to-all-start.9
  359.7 8.4 %bitcast_convert_fusion.2 = bf16[2,512,2048]{2,1,0:T(8,128)(2,1)} fusion(bf16[4,2,152,512]{3,2,1,0:T(8,128)(2,1)} %all-to-all-done.2, bf16[4,2,152,2048]{3,2,0,1:T(8,128)(2,1)} %copy-done.82), kind=kOutput, calls=%fused_computation.30 | convolution fusion | flops 2552233984 | bytes 10420224 | tf_op jit(solution)/shard_map/sjcd,sjcf->jdf/dot_general | solution.py:309
  368.1 5.6 %all-to-all-done.9 = bf16[4,2,152,512]{3,2,1,0:T(8,128)(2,1)} async-done(((bf16[4,2,152,512]{3,2,1,0:T(8,128)(2,1)}), bf16[4,2,152,512]{3,2,1,0:T(8,128)(2,1)}, u32[]{:S(2)}, u32[]{:S(2)}) %all-to-all-start.9) | async-done | bytes 1245216 | tf_op jit(solution)/shard_map/all_to_all | solution.py:138
  378.8 9.3 %attention_back.3 = bf16[416,1536]{1,0:T(8,128)(2,1)} custom-call(bf16[416,1536]{1,0:T(8,128)(2,1)} %convolution_convert_fusion.6.packed_ref, bf16[416,512]{1,0:T(8,128)(2,1)} %convolution_convert_fusion.9.grad_ref, f32[416,8]{1,0:T(8,128)} %get-tuple-element.44.total_ref), custom_call_target="tpu_custom_call" | custom-call | tf_op jit(solution)/shard_map/attention_back/pallas_call | solution.py:229
  388.1 3.3 multiply_reduce_fusion.1
  395.0 4.4 concatenate.21
  402.2 4.2 all-to-all-start.11
  410.5 10.1 %all-to-all-done.11 = bf16[4,4,16,2060]{3,2,1,0:T(8,128)(2,1)} async-done(((bf16[4,4,16,2060]{3,2,1,0:T(8,128)(2,1)}), bf16[4,4,16,2060]{3,2,1,0:T(8,128)(2,1)}, u32[]{:S(2)}, u32[]{:S(2)}) %all-to-all-start.11) | async-done | bytes 1054752 | tf_op jit(solution)/shard_map/all_to_all | solution.py:138
  424.6 3.5 all-to-all-start.10
  431.7 10.3 %all-to-all-done.10 = bf16[4,4,16,2060]{3,2,1,0:T(8,128)(2,1)S(1)} async-done(((bf16[4,4,16,2060]{3,2,1,0:T(8,128)(2,1)}), bf16[4,4,16,2060]{3,2,1,0:T(8,128)(2,1)S(1)}, u32[]{:S(2)}, u32[]{:S(2)}) %all-to-all-start.10) | async-done | bytes 1054752 | tf_op jit(solution)/shard_map/all_to_all | solution.py:138
  444.0 6.8 %collective-permute-done.5 = bf16[2,16,2060]{2,1,0:T(8,128)(2,1)S(1)} collective-permute-done((bf16[2,16,2060]{2,1,0:T(8,128)(2,1)S(1)}, bf16[2,16,2060]{2,1,0:T(8,128)(2,1)S(1)}, u32[]{:S(2)}, u32[]{:S(2)}) %collective-permute-start.5) | collective-permute-done | bytes 131872 | tf_op jit(solution)/shard_map/ppermute | solution.py:364
  454.2 4.8 collective-permute-done.6
  461.8 29.0 %reduce-scatter.5.cloned.1.call-done = bf16[2,512,256]{2,1,0:T(8,128)(2,1)} async-done(((bf16[2,512,2048]{2,1,0:T(8,128)(2,1)}), bf16[2,512,256]{2,1,0:T(8,128)(2,1)}) %reduce-scatter.5.cloned.1.call-update) | async-done | bytes 524304 | tf_op jit(solution)/shard_map/reduce_scatter | solution.py:313
  493.5 10.2 %all_gather.15 = bf16[64,2,2060]{2,0,1:T(8,128)(2,1)S(1)} all-gather(bf16[16,2,2060]{2,0,1:T(8,128)(2,1)S(1)} %pad_maximum_fusion.3), channel_id=1, replica_groups=mesh['dp'=8,'expert'=4] {'expert'}, dimensions={0}, use_global_device_ids=true | all-gather | bytes 659200 | tf_op jit(solution)/shard_map/all_gather | solution.py:460
  (399 shorter events, 138.9 us)
Async XLA Ops:
  7.2 120.4 %all-gather.6.cloned.1.call-start = ((), (), s32[]{:S(2)}) async-start(), calls=%async_computation.16 | async-start | bytes 9437184 | tf_op jit(solution)/shard_map/all_gather | solution.py:111
  11.6 192.7 %all-gather.8.cloned.1.call-start = ((), (), s32[]{:S(2)}) async-start(), calls=%async_computation.21 | async-start | bytes 4718592 | tf_op jit(solution)/shard_map/all_gather | solution.py:113
  12.4 213.8 %all-gather.10.cloned.1.call-start = ((), (), s32[]{:S(2)}) async-start(), calls=%async_computation.22 | async-start | bytes 4718592 | tf_op jit(solution)/shard_map/all_gather | solution.py:114
  13.1 7.3 %collective-permute-start = (bf16[1,2,16,2060]{3,2,0,1:T(8,128)(2,1)S(1)}, bf16[1,2,16,2060]{3,2,0,1:T(8,128)(2,1)S(1)}, u32[]{:S(2)}, u32[]{:S(2)}) collective-permute-start(bf16[1,2,16,2060]{3,2,0,1:T(8,128)(2,1)S(1)} %dynamic-slice_bitcast_fusion.3), channel_id=1, source_target_pairs={{0,8},{4,12},{8,0},{12,4},{16,24},{20,28},{24,16},{28,20},{1,9},{5... | collective-permute-start | bytes 395528 | tf_op jit(solution)/shard_map/ppermute | solution.py:65
  17.6 45.5 %copy-start.37 = (s32[416,1]{0,1:T(1,128)}, s32[416,1]{0,1:T(1,128)S(1)}, u32[]{:S(2)}) copy-start(s32[416,1]{0,1:T(1,128)S(1)} %get-tuple-element.148) | copy-start | bytes 4996
  17.6 46.1 %copy-start.34 = (s32[416,1]{0,1:T(1,128)}, s32[416,1]{0,1:T(1,128)S(1)}, u32[]{:S(2)}) copy-start(s32[416,1]{0,1:T(1,128)S(1)} %get-tuple-element.147) | copy-start | bytes 4996
  19.1 53.6 %copy-start.40 = (s32[416,1]{0,1:T(1,128)}, s32[416,1]{0,1:T(1,128)S(1)}, u32[]{:S(2)}) copy-start(s32[416,1]{0,1:T(1,128)S(1)} %get-tuple-element.141) | copy-start | bytes 4996
  19.1 53.6 %copy-start.42 = (s32[416,1]{0,1:T(1,128)}, s32[416,1]{0,1:T(1,128)S(1)}, u32[]{:S(2)}) copy-start(s32[416,1]{0,1:T(1,128)S(1)} %get-tuple-element.142) | copy-start | bytes 4996
  20.4 81.1 %copy-start.1 = (f32[2,208,512]{2,1,0:T(8,128)}, f32[2,208,512]{2,1,0:T(8,128)S(1)}, u32[]{:S(2)}) copy-start(f32[2,208,512]{2,1,0:T(8,128)S(1)} %pad_convert_fusion) | copy-start | bytes 2555908
  20.5 35.3 %collective-permute-start.1 = (bf16[2,2,16,2060]{3,2,0,1:T(8,128)(2,1)S(1)}, bf16[2,2,16,2060]{3,2,0,1:T(8,128)(2,1)S(1)}, u32[]{:S(2)}, u32[]{:S(2)}) collective-permute-start(bf16[2,2,16,2060]{3,2,0,1:T(8,128)(2,1)S(1)} %pad_maximum_fusion.2), channel_id=1, source_target_pairs={{0,16},{4,20},{8,24},{12,28},{16,0},{20,4},{24,8},{28,12},{1,17},{... | collective-permute-start | bytes 791048 | tf_op jit(solution)/shard_map/ppermute | solution.py:65
  57.7 15.0 %all-to-all-start.1 = ((bf16[4,4,16,2060]{3,2,1,0:T(8,128)(2,1)}), bf16[4,4,16,2060]{3,2,1,0:T(8,128)(2,1)S(1)}, u32[]{:S(2)}, u32[]{:S(2)}) async-start(bf16[4,4,16,2060]{3,2,1,0:T(8,128)(2,1)} %broadcast_in_dim.227), calls=%async_computation.1 | async-start | bytes 2228224 | tf_op jit(solution)/shard_map/all_to_all | solution.py:138
  72.7 11.8 %collective-permute-start.2 = (bf16[4,4,16,2060]{3,2,1,0:T(8,128)(2,1)S(1)}, bf16[4,4,16,2060]{3,2,1,0:T(8,128)(2,1)S(1)}, u32[]{:S(2)}, u32[]{:S(2)}) collective-permute-start(bf16[4,4,16,2060]{3,2,1,0:T(8,128)(2,1)S(1)} %all-to-all-done.1), channel_id=1, source_target_pairs={{0,4},{4,0},{8,12},{12,8},{16,20},{20,16},{24,28},{28,24},{1,5},{5... | collective-permute-start | bytes 3164168 | tf_op jit(solution)/shard_map/ppermute | solution.py:81
  75.4 28.1 %all-to-all-start = ((bf16[4,4,16,2060]{3,2,1,0:T(8,128)(2,1)}), bf16[4,4,16,2060]{3,2,1,0:T(8,128)(2,1)}, u32[]{:S(2)}, u32[]{:S(2)}) async-start(bf16[4,4,16,2060]{3,2,1,0:T(8,128)(2,1)} %broadcast_in_dim.222), calls=%async_computation | async-start | bytes 2228224 | tf_op jit(solution)/shard_map/all_to_all | solution.py:138
  88.8 22.4 %copy-start.44 = (bf16[512,12]{0,1:T(8,128)(2,1)}, bf16[512,12]{0,1:T(8,128)(2,1)S(1)}, u32[]{:S(2)}) copy-start(bf16[512,12]{0,1:T(8,128)(2,1)S(1)} %broadcast_select_fusion.6) | copy-start | bytes 36868
  88.8 15.3 %copy-start.50 = (f32[1,512]{1,0:T(1,128)}, f32[1,512]{1,0:T(1,128)S(1)}, u32[]{:S(2)}) copy-start(f32[1,512]{1,0:T(1,128)S(1)} %get-tuple-element.149) | copy-start | bytes 6148
  92.0 9.2 %copy-start.54 = (pred[512]{0:T(512)(128)(4,1)S(1)}, pred[512]{0:T(512)(128)(4,1)}, u32[]{:S(2)}) copy-start(pred[512]{0:T(512)(128)(4,1)} %broadcast_in_dim.224) | copy-start | bytes 1540
  103.5 9.2 %collective-permute-start.3 = (bf16[4,4,16,2060]{3,2,1,0:T(8,128)(2,1)}, bf16[4,4,16,2060]{3,2,1,0:T(8,128)(2,1)}, u32[]{:S(2)}, u32[]{:S(2)}) collective-permute-start(bf16[4,4,16,2060]{3,2,1,0:T(8,128)(2,1)} %all-to-all-done), channel_id=1, source_target_pairs={{0,4},{4,0},{8,12},{12,8},{16,20},{20,16},{24,28},{28,24},{1,5},{5... | collective-permute-start | bytes 3164168 | tf_op jit(solution)/shard_map/ppermute | solution.py:81
  106.2 21.4 %all-to-all-start.2 = ((bf16[4,2,152,512]{3,2,1,0:T(8,128)(2,1)}), bf16[4,2,152,512]{3,2,1,0:T(8,128)(2,1)}, u32[]{:S(2)}, u32[]{:S(2)}) async-start(bf16[4,2,152,512]{3,2,1,0:T(8,128)(2,1)} %bitcast.346), calls=%async_computation.2 | async-start | bytes 2490368 | tf_op jit(solution)/shard_map/all_to_all | solution.py:138
  139.6 20.1 %all-to-all-start.3 = ((bf16[4,2,152,512]{3,2,1,0:T(8,128)(2,1)}), bf16[4,2,152,512]{3,2,1,0:T(8,128)(2,1)}, u32[]{:S(2)}, u32[]{:S(2)}) async-start(bf16[4,2,152,512]{3,2,1,0:T(8,128)(2,1)} %copy.159), calls=%async_computation.3 | async-start | bytes 2490368 | tf_op jit(solution)/shard_map/all_to_all | solution.py:138
  151.6 149.9 %copy-start.64 = (f32[1,512]{1,0:T(1,128)}, f32[1,512]{1,0:T(1,128)S(1)}, u32[]{:S(2)}) copy-start(f32[1,512]{1,0:T(1,128)S(1)} %get-tuple-element.144) | copy-start | bytes 6148
  151.6 14.6 %copy-start.73 = (f32[1,512]{1,0:T(1,128)}, f32[1,512]{1,0:T(1,128)S(1)}, u32[]{:S(2)}) copy-start(f32[1,512]{1,0:T(1,128)S(1)} %get-tuple-element.146) | copy-start | bytes 6148
  165.9 135.6 %copy-start.55 = (f32[416]{0:T(512)}, f32[416]{0:T(512)S(1)}, u32[]{:S(2)}) copy-start(f32[416]{0:T(512)S(1)} %broadcast_multiply_fusion.9) | copy-start | bytes 4996
  166.2 135.3 %copy-start.63 = (f32[416]{0:T(512)}, f32[416]{0:T(512)S(1)}, u32[]{:S(2)}) copy-start(f32[416]{0:T(512)S(1)} %add_rsqrt_fusion.1) | copy-start | bytes 4996
  176.5 8.5 %copy-start.9 = (bf16[416,512]{1,0:T(8,128)(2,1)}, bf16[416,512]{1,0:T(8,128)(2,1)S(1)}, u32[]{:S(2)}) copy-start(bf16[416,512]{1,0:T(8,128)(2,1)S(1)} %add_convert_fusion.2) | copy-start | bytes 1277956
  178.5 19.7 %all-to-all-start.4 = ((bf16[4,2,152,512]{3,2,1,0:T(8,128)(2,1)}), bf16[4,2,152,512]{3,2,1,0:T(8,128)(2,1)}, u32[]{:S(2)}, u32[]{:S(2)}) async-start(bf16[4,2,152,512]{3,2,1,0:T(8,128)(2,1)} %bitcast.348), calls=%async_computation.4 | async-start | bytes 2490368 | tf_op jit(solution)/shard_map/all_to_all | solution.py:138
  198.2 19.6 %all-to-all-start.6 = ((bf16[4,2,152,512]{3,2,1,0:T(8,128)(2,1)}), bf16[4,2,152,512]{3,2,1,0:T(8,128)(2,1)}, u32[]{:S(2)}, u32[]{:S(2)}) async-start(bf16[4,2,152,512]{3,2,1,0:T(8,128)(2,1)} %bitcast.347), calls=%async_computation.6 | async-start | bytes 2490368 | tf_op jit(solution)/shard_map/all_to_all | solution.py:138
  202.5 256.6 %reduce-scatter.11.cloned.1.call-start = ((), (), s32[]{:S(2)}) async-start(), calls=%async_computation.20 | async-start | bytes 4718592 | tf_op jit(solution)/shard_map/reduce_scatter | solution.py:300
  238.7 19.8 %all-to-all-start.7 = ((bf16[4,2,152,512]{3,2,1,0:T(8,128)(2,1)}), bf16[4,2,152,512]{3,2,1,0:T(8,128)(2,1)}, u32[]{:S(2)}, u32[]{:S(2)}) async-start(bf16[4,2,152,512]{3,2,1,0:T(8,128)(2,1)} %copy.172), calls=%async_computation.7 | async-start | bytes 2490368 | tf_op jit(solution)/shard_map/all_to_all | solution.py:138
  258.5 19.7 %all-to-all-start.5 = ((bf16[4,2,152,512]{3,2,1,0:T(8,128)(2,1)}), bf16[4,2,152,512]{3,2,1,0:T(8,128)(2,1)}, u32[]{:S(2)}, u32[]{:S(2)}) async-start(bf16[4,2,152,512]{3,2,1,0:T(8,128)(2,1)} %copy.168), calls=%async_computation.5 | async-start | bytes 2490368 | tf_op jit(solution)/shard_map/all_to_all | solution.py:138
  305.6 12.1 %copy-start.20 = (bf16[416,512]{1,0:T(8,128)(2,1)S(1)}, bf16[416,512]{1,0:T(8,128)(2,1)}, u32[]{:S(2)}) copy-start(bf16[416,512]{1,0:T(8,128)(2,1)} %get-tuple-element.35) | copy-start | bytes 1277956
  305.6 21.6 %all-to-all-start.8 = ((bf16[4,2,152,512]{3,2,1,0:T(8,128)(2,1)}), bf16[4,2,152,512]{3,2,1,0:T(8,128)(2,1)}, u32[]{:S(2)}, u32[]{:S(2)}) async-start(bf16[4,2,152,512]{3,2,1,0:T(8,128)(2,1)} %bitcast.345), calls=%async_computation.8 | async-start | bytes 2490368 | tf_op jit(solution)/shard_map/all_to_all | solution.py:138
  310.0 149.1 %reduce-scatter.9.cloned.1.call-start = ((), (), s32[]{:S(2)}) async-start(), calls=%async_computation.19 | async-start | bytes 4718592 | tf_op jit(solution)/shard_map/reduce_scatter | solution.py:300
  335.6 126.2 %reduce-scatter.7.cloned.1.call-start = ((), (), s32[]{:S(2)}) async-start(), calls=%async_computation.18 | async-start | bytes 4718592 | tf_op jit(solution)/shard_map/reduce_scatter | solution.py:313
  354.2 19.4 %all-to-all-start.9 = ((bf16[4,2,152,512]{3,2,1,0:T(8,128)(2,1)}), bf16[4,2,152,512]{3,2,1,0:T(8,128)(2,1)}, u32[]{:S(2)}, u32[]{:S(2)}) async-start(bf16[4,2,152,512]{3,2,1,0:T(8,128)(2,1)} %copy.182), calls=%async_computation.9 | async-start | bytes 2490368 | tf_op jit(solution)/shard_map/all_to_all | solution.py:138
  358.5 132.3 %reduce-scatter.5.cloned.1.call-start = ((), (), s32[]{:S(2)}) async-start(), calls=%async_computation.17 | async-start | bytes 4718592 | tf_op jit(solution)/shard_map/reduce_scatter | solution.py:313
  359.7 13.9 %copy-start.62 = (s32[416]{0:T(512)S(1)}, s32[416]{0:T(512)}, u32[]{:S(2)}) copy-start(s32[416]{0:T(512)} %multiply_add_fusion.5) | copy-start | bytes 4996
  359.7 13.9 %copy-start.70 = (s32[416]{0:T(512)S(1)}, s32[416]{0:T(512)}, u32[]{:S(2)}) copy-start(s32[416]{0:T(512)} %multiply_add_fusion.6) | copy-start | bytes 4996
  359.7 39.7 %collective-permute-start.7 = (bf16[4,4,16,2060]{3,2,1,0:T(8,128)(2,1)}, bf16[4,4,16,2060]{3,2,1,0:T(8,128)(2,1)}, u32[]{:S(2)}, u32[]{:S(2)}) collective-permute-start(bf16[4,4,16,2060]{3,2,1,0:T(8,128)(2,1)} %dynamic-slice_bitcast_fusion), channel_id=1, source_target_pairs={{0,4},{4,0},{8,12},{12,8},{16,20},{20,16},{24,28},{28,24},{1,5},{5... | collective-permute-start | bytes 3164168 | tf_op jit(solution)/shard_map/ppermute | solution.py:364
  378.8 9.3 %copy-start.2 = (f32[2,208,512]{2,1,0:T(8,128)S(1)}, f32[2,208,512]{2,1,0:T(8,128)}, u32[]{:S(2)}) copy-start(f32[2,208,512]{2,1,0:T(8,128)} %copy-done.1) | copy-start | bytes 2555908
  378.8 9.3 %copy-start.21 = (bf16[512,1536]{1,0:T(8,128)(2,1)S(1)}, bf16[512,1536]{1,0:T(8,128)(2,1)}, u32[]{:S(2)}) copy-start(bf16[512,1536]{1,0:T(8,128)(2,1)} %get-tuple-element.153) | copy-start | bytes 4718596
  378.8 9.3 %copy-start.57 = (f32[1,512]{1,0:T(1,128)S(1)}, f32[1,512]{1,0:T(1,128)}, u32[]{:S(2)}) copy-start(f32[1,512]{1,0:T(1,128)} %copy-done.56) | copy-start | bytes 6148
  402.2 18.3 %all-to-all-start.11 = ((bf16[4,4,16,2060]{3,2,1,0:T(8,128)(2,1)}), bf16[4,4,16,2060]{3,2,1,0:T(8,128)(2,1)}, u32[]{:S(2)}, u32[]{:S(2)}) async-start(bf16[4,4,16,2060]{3,2,1,0:T(8,128)(2,1)} %fusion.50), calls=%async_computation.11 | async-start | bytes 2228224 | tf_op jit(solution)/shard_map/all_to_all | solution.py:138
  409.4 12.8 %collective-permute-start.4 = (bf16[4,4,16,2060]{3,2,1,0:T(8,128)(2,1)}, bf16[4,4,16,2060]{3,2,1,0:T(8,128)(2,1)}, u32[]{:S(2)}, u32[]{:S(2)}) collective-permute-start(bf16[4,4,16,2060]{3,2,1,0:T(8,128)(2,1)} %bitcast.332), channel_id=1, source_target_pairs={{0,4},{4,0},{8,12},{12,8},{16,20},{20,16},{24,28},{28,24},{1,5},{5... | collective-permute-start | bytes 3164168 | tf_op jit(solution)/shard_map/ppermute | solution.py:364
  422.0 9.6 %collective-permute-start.8 = (bf16[2,16,2060]{2,1,0:T(8,128)(2,1)S(1)}, bf16[2,16,2060]{2,1,0:T(8,128)(2,1)S(1)}, u32[]{:S(2)}, u32[]{:S(2)}) collective-permute-start(bf16[2,16,2060]{2,1,0:T(8,128)(2,1)S(1)} %dynamic-slice_bitcast_fusion.1), channel_id=1, source_target_pairs={{0,8},{4,12},{8,0},{12,4},{16,24},{20,28},{24,16},{28,20},{1,9},{5... | collective-permute-start | bytes 395528 | tf_op jit(solution)/shard_map/ppermute | solution.py:364
  424.6 17.4 %all-to-all-start.10 = ((bf16[4,4,16,2060]{3,2,1,0:T(8,128)(2,1)}), bf16[4,4,16,2060]{3,2,1,0:T(8,128)(2,1)S(1)}, u32[]{:S(2)}, u32[]{:S(2)}) async-start(bf16[4,4,16,2060]{3,2,1,0:T(8,128)(2,1)} %fusion.51), calls=%async_computation.10 | async-start | bytes 2228224 | tf_op jit(solution)/shard_map/all_to_all | solution.py:138
  442.2 8.6 %collective-permute-start.5 = (bf16[2,16,2060]{2,1,0:T(8,128)(2,1)S(1)}, bf16[2,16,2060]{2,1,0:T(8,128)(2,1)S(1)}, u32[]{:S(2)}, u32[]{:S(2)}) collective-permute-start(bf16[2,16,2060]{2,1,0:T(8,128)(2,1)S(1)} %dynamic-slice_bitcast_fusion.2), channel_id=1, source_target_pairs={{0,8},{4,12},{8,0},{12,4},{16,24},{20,28},{24,16},{28,20},{1,9},{5... | collective-permute-start | bytes 395528 | tf_op jit(solution)/shard_map/ppermute | solution.py:364
  444.0 10.2 %collective-permute-start.9 = (bf16[1,16,2060]{2,1,0:T(8,128)(2,1)S(1)}, bf16[1,16,2060]{2,1,0:T(8,128)(2,1)S(1)}, u32[]{:S(2)}, u32[]{:S(2)}) collective-permute-start(bf16[1,16,2060]{2,1,0:T(8,128)(2,1)S(1)} %constant_dynamic-slice_fusion), channel_id=1, source_target_pairs={{0,16},{4,20},{8,24},{12,28},{16,0},{20,4},{24,8},{28,12},{1,17},{... | collective-permute-start | bytes 197768 | tf_op jit(solution)/shard_map/ppermute | solution.py:364
  450.9 8.2 %collective-permute-start.6 = (bf16[1,16,2060]{2,1,0:T(8,128)(2,1)S(1)}, bf16[1,16,2060]{2,1,0:T(8,128)(2,1)S(1)}, u32[]{:S(2)}, u32[]{:S(2)}) collective-permute-start(bf16[1,16,2060]{2,1,0:T(8,128)(2,1)S(1)} %constant_dynamic-slice_fusion.1), channel_id=1, source_target_pairs={{0,16},{4,20},{8,24},{12,28},{16,0},{20,4},{24,8},{28,12},{1,17},{... | collective-permute-start | bytes 197768 | tf_op jit(solution)/shard_map/ppermute | solution.py:364
  (64 other events, 208.0 us)
Sparse Core Ops, SparseCore 0:
  11.7 93.2 all-gather.5
  106.6 48.1 all-gather.7
  156.4 45.0 all-gather.9
  226.3 47.1 reduce-scatter.10
  335.6 48.4 reduce-scatter.8
  386.3 51.3 reduce-scatter.6
  440.0 50.7 reduce-scatter.4

commit v8 on v7

--- a/solution.py
+++ b/solution.py
@@ -52,14 +52,21 @@
     )
 
 
-def gather_quarters(w_qkv, w_proj, w_router, norm_gains, norm_shifts):
+def gather_quarter(which, ahead, w_qkv, w_proj, w_router, norm_gains, norm_shifts):
     peers, rank = lax.axis_size("expert"), lax.axis_index("expert")
     piece = w_qkv.shape[1] // peers
     packed = jnp.concatenate(
-        [w_qkv, w_proj, w_router, jnp.swapaxes(norm_gains, 1, 2), jnp.swapaxes(norm_shifts, 1, 2)],
-        axis=2,
-    )
-    block = lax.dynamic_slice_in_dim(packed, rank * piece, piece, axis=1)[None]
+        [
+            w_qkv[which],
+            w_proj[which],
+            w_router[which],
+            norm_gains[which].T,
+            norm_shifts[which].T,
+        ],
+        axis=1,
+    )
+    block = lax.dynamic_slice_in_dim(packed, rank * piece, piece, axis=0)[None]
+    block, ahead = lax.optimization_barrier((block, ahead))
     place, size, step = lax.axis_index("dp"), lax.axis_size("dp"), 2
     while step < size:
         moved = lax.ppermute(block, "dp", [(source, source ^ step) for source in range(size)])
@@ -67,7 +74,7 @@
         first, second = jnp.where(upper, moved, block), jnp.where(upper, block, moved)
         block = jnp.concatenate([first, second], axis=0)
         step = 2 * step
-    return block
+    return (block, ahead)
 
 
 def spread_quarter(quarter):
@@ -365,10 +372,11 @@
     return (kept.astype(jnp.float32) + moved.astype(jnp.float32)).astype(jnp.bfloat16)
 
 
-def sum_small(small):
+def sum_small(small, beside):
     place = lax.axis_index("dp")
     small = halve(small, place % 2, 1)
     small = exchange(small)
+    small, beside = lax.optimization_barrier((small, beside))
     small = jnp.sum(small.astype(jnp.float32), axis=0).astype(jnp.bfloat16)
     step = 2
     while small.shape[0] > 1:
@@ -376,7 +384,7 @@
         block = small.reshape(chips // 2, 2, rows, columns).swapaxes(0, 1)
         small = halve(block, (place // step) % 2, step)
         step = 2 * step
-    return small[0]
+    return (small[0], beside)
 
 
 def whole_step(
@@ -394,7 +402,13 @@
     resid = jnp.pad(embedded, fill).reshape(rows, width).astype(jnp.float32)
     grad = cot_low.astype(jnp.float32)
     dense, experts, tables = [], [], []
-    quarters = gather_quarters(w_qkv, w_proj, w_router, norm_gains, norm_shifts)
+    quarters = [()]
+    for which in range(LAYERS):
+        block, quarters[-1] = gather_quarter(
+            which, quarters[-1], w_qkv, w_proj, w_router, norm_gains, norm_shifts
+        )
+        quarters.append(block)
+    quarters = quarters[1:]
     for which in range(LAYERS):
         experts.append(gather_experts(which, w_first, w_second))
         route = jnp.pad(routes[which], fill, constant_values=experts_total).reshape(rows, 2)
@@ -404,7 +418,7 @@
     cot_rows = exchange(slots)
     parts = []
     for which in range(LAYERS):
-        parts.append(spread_quarter(quarters[:, which]))
+        parts.append(spread_quarter(quarters[which]))
     dense.append(join_cores(parts[0], experts_total))
     attn_saved, moe_saved, kept = [], [], []
     grad_result = None
@@ -452,11 +466,11 @@
             moe_saved[which],
         )
     for which in reversed(range(LAYERS)):
-        smalls[which] = sum_small(smalls[which])
+        beside = jnp.stack(seconds).astype(jnp.float32) if which == 0 else ()
+        smalls[which], beside = sum_small(smalls[which], beside)
     both = jnp.stack(smalls, axis=1)
     grad_first = jnp.stack(firsts).astype(jnp.float32)
-    grad_second = jnp.stack(seconds).astype(jnp.float32)
-    both, grad_first, grad_second = lax.optimization_barrier((both, grad_first, grad_second))
+    both, grad_first = lax.optimization_barrier((both, grad_first))
     total = lax.all_gather(both, "expert", axis=0, tiled=True)
     total = total.swapaxes(0, 1).astype(jnp.float32)
     grad_images = grad.reshape(images, SEQ_PAD, width)[:, :length]
@@ -470,7 +484,7 @@
         jnp.swapaxes(wide[:, :, experts_total : experts_total + 2], 1, 2),
         jnp.swapaxes(wide[:, :, experts_total + 2 :], 1, 2),
         grad_first,
-        grad_second,
+        beside,
     )
 
 

time: 524 us -> 528 us (level)
    all_to_all x12, waiting for transfers between devices: 86.1 us -> 75.5 us  [exchange(): lax.all_to_all(block, 'expert', split_axis=0, concat_axis=0, tiled=True)]
    ppermute x2 -> x4, waiting for transfers between devices: 32.3 us -> 39.2 us  [gather_quarter(): lax.ppermute(block, 'dp', [(source, source ^ step) for source in range(si...]
  transfers between devices with their start and end apart: 29 -> 31, of which waited for: 16 -> 17; matrix products, arithmetic and copies ran while one was open for 43% -> 43% of each run, Pallas kernels for 6% -> 6%
where the time goes in v8:
time: 528 us; the launch traced here: 519 us
  waiting for transfers between devices  166 us (31%)
  matrix products  140 us (27%)
  local copies, waits for them, and re-layouts  61 us (12%)
  starting transfers between devices  60.7 us (11%)
  other arithmetic  34.6 us (7%)
  Pallas kernels  31.1 us (6%)
  between operations  16.2 us (3%)
  blocking collectives  9.57 us (2%)
    all_to_all x12, waiting for transfers between devices, exchange(): lax.all_to_all(block, 'expert', split_axis=0, concat_axis=0, tiled=True)  75.5 us
    all_to_all x12, starting transfers between devices, exchange(): lax.all_to_all(block, 'expert', split_axis=0, concat_axis=0, tiled=True)  51.4 us
    ppermute x4, waiting for transfers between devices, gather_quarter(): lax.ppermute(block, 'dp', [(source, source ^ step) for source in range(si...  39.2 us
    reduce_scatter x2, waiting for transfers between devices, experts_backward(): lax.psum_scatter(grad_first, 'dp', scatter_dimension=2, tiled=True)  30.2 us
    ppermute x6, waiting for transfers between devices, halve(): lax.ppermute(sent, 'dp', [(source, source ^ step) for source in range(siz...  19.3 us
    pallas_call x2, Pallas kernels, attention_back(): pl.pallas_call(attention_back_kernel, grid=(rows // SEQ_PAD,), in_specs=[...  18.4 us
    dot_general x2, matrix products, experts_backward(): jnp.einsum('sjcd,jfd->sjcf', grad_result, second_full, preferred_element_...  18 us
    dot_general x2, matrix products, experts_hidden(): jnp.einsum('sjcd,jfd->sjcf', incoming, first_full, preferred_element_type...  17 us
  transfers between devices with their start and end apart: 31, of which 17 were waited for; matrix products, arithmetic and copies ran while one was open for 43% of the time, Pallas kernels for 6%

profile of v8, /device:TPU:0, one launch (start us, length us, event | category | flops | bytes accessed | tf_op | source)
XLA Modules:
  0.0 518.9 jit_solution(16621607248930475633)
XLA Ops:
  25.7 17.3 %collective-permute-done.1 = bf16[2,16,2060]{2,1,0:T(8,128)(2,1)S(1)} collective-permute-done((bf16[2,16,2060]{2,1,0:T(8,128)(2,1)S(1)}, bf16[2,16,2060]{2,1,0:T(8,128)(2,1)S(1)}, u32[]{:S(2)}, u32[]{:S(2)}) %collective-permute-start.1) | collective-permute-done | bytes 131872 | tf_op jit(solution)/shard_map/ppermute | solution.py:72
  45.8 3.8 all-to-all-start.1
  49.6 4.0 collective-permute-done.2
  53.9 17.9 %collective-permute-done.3 = bf16[2,16,2060]{2,1,0:T(8,128)(2,1)S(1)} collective-permute-done((bf16[2,16,2060]{2,1,0:T(8,128)(2,1)S(1)}, bf16[2,16,2060]{2,1,0:T(8,128)(2,1)S(1)}, u32[]{:S(2)}, u32[]{:S(2)}) %collective-permute-start.3) | collective-permute-done | bytes 131872 | tf_op jit(solution)/shard_map/ppermute | solution.py:72
  74.6 4.3 all-to-all-start
  93.2 6.3 %attention.2 = (bf16[416,512]{1,0:T(8,128)(2,1)}, f32[416,8]{1,0:T(8,128)}) custom-call(bf16[416,1536]{1,0:T(8,128)(2,1)} %convolution_convert_fusion.6.packed_ref), custom_call_target="tpu_custom_call" | custom-call | tf_op jit(solution)/shard_map/attention/pallas_call | solution.py:221
  107.3 4.9 all-to-all-start.2
  115.6 13.1 %all-to-all-done.2 = bf16[4,2,152,512]{3,2,1,0:T(8,128)(2,1)} async-done(((bf16[4,2,152,512]{3,2,1,0:T(8,128)(2,1)}), bf16[4,2,152,512]{3,2,1,0:T(8,128)(2,1)}, u32[]{:S(2)}, u32[]{:S(2)}) %all-to-all-start.2) | async-done | bytes 1245216 | tf_op jit(solution)/shard_map/all_to_all | solution.py:145
  128.7 8.1 %fusion.19 = (bf16[4,2,152,2048]{3,2,0,1:T(8,128)(2,1)S(1)}, f32[2,2048,4,152]{1,3,2,0:T(8,128)}) fusion(bf16[4,2,152,512]{3,2,1,0:T(8,128)(2,1)} %all-to-all-done.2, bf16[2,2,2048,512]{3,2,1,0:T(8,128)(2,1)} %all-gather.6.cloned.1.call-done), kind=kOutput, calls=%fused_computation.25 | convolution fusion | flops 2562588672 | bytes 20381696 | tf_op jit(solution)/shard_map/sjcd,jfd->sjcf/dot_general | solution.py:286
  140.7 4.4 all-to-all-start.3
  148.3 4.3 bitcast_select_fusion
  152.7 8.1 %all-to-all-done.3 = bf16[4,2,152,512]{3,2,1,0:T(8,128)(2,1)} async-done(((bf16[4,2,152,512]{3,2,1,0:T(8,128)(2,1)}), bf16[4,2,152,512]{3,2,1,0:T(8,128)(2,1)}, u32[]{:S(2)}, u32[]{:S(2)}) %all-to-all-start.3) | async-done | bytes 1245216 | tf_op jit(solution)/shard_map/all_to_all | solution.py:145
  163.1 3.7 fusion.159
  169.1 6.3 %attention.3 = (bf16[416,512]{1,0:T(8,128)(2,1)}, f32[416,8]{1,0:T(8,128)}) custom-call(bf16[416,1536]{1,0:T(8,128)(2,1)} %convolution_convert_fusion.5.packed_ref), custom_call_target="tpu_custom_call" | custom-call | tf_op jit(solution)/shard_map/attention/pallas_call | solution.py:221
  179.4 4.6 all-to-all-start.4
  186.2 13.0 %all-to-all-done.4 = bf16[4,2,152,512]{3,2,1,0:T(8,128)(2,1)} async-done(((bf16[4,2,152,512]{3,2,1,0:T(8,128)(2,1)}), bf16[4,2,152,512]{3,2,1,0:T(8,128)(2,1)}, u32[]{:S(2)}, u32[]{:S(2)}) %all-to-all-start.4) | async-done | bytes 1245216 | tf_op jit(solution)/shard_map/all_to_all | solution.py:145
  199.3 4.3 all-to-all-start.6
  205.4 9.0 %fusion.15 = (bf16[4,2,152,2048]{3,2,0,1:T(8,128)(2,1)}, f32[2,4,152,2048]{3,2,1,0:T(8,128)}) fusion(bf16[1,2,512,2048]{3,2,1,0:T(8,128)(2,1)} %all-gather.8.cloned.1.call-done, bf16[4,2,152,512]{3,2,1,0:T(8,128)(2,1)} %all-to-all-done.4), kind=kOutput, calls=%fused_computation.19 | convolution fusion | flops 2562588672 | bytes 20381696 | tf_op jit(solution)/shard_map/sjcd,jfd->sjcf/dot_general | solution.py:286
  214.4 4.5 all-to-all-done.6
  218.9 8.3 %bitcast_convert_fusion = bf16[2,2048,512]{2,1,0:T(8,128)(2,1)} fusion(bf16[4,2,152,2048]{3,2,0,1:T(8,128)(2,1)} %get-tuple-element.182, bf16[4,2,152,512]{3,2,1,0:T(8,128)(2,1)} %all-to-all-done.6, f32[4,2,152]{2,1,0:T(2,128)S(1)} %fusion.174), kind=kOutput, calls=%fused_computation.28 | convolution fusion | flops 2554101760 | bytes 10425088 | tf_op jit(solution)/shard_map/sjcf,sjcd->jfd/dot_general | solution.py:304
  227.3 8.4 %fusion.7 = bf16[4,2,152,2048]{3,2,0,1:T(8,128)(2,1)S(1)} fusion(f32[2,4,152,2048]{3,2,1,0:T(8,128)} %get-tuple-element.183, bf16[1,2,2048,512]{3,2,1,0:T(8,128)(2,1)} %all-gather.10.cloned.1.call-done, bf16[4,2,152,512]{3,2,1,0:T(8,128)(2,1)} %all-to-all-done.6, f32[4,2,152]{2,1,0:T(2,128)S(1)} %fusion.174), kind=kOutput, calls=%fused_computation.9 | convolution fusion | flops 2576908288 | bytes 20386560 | tf_op jit(solution)/shard_map/sjcd,jfd->sjcf/dot_general | solution.py:308
  239.8 4.5 all-to-all-start.7
  244.3 6.5 %fusion.63 = bf16[4,2,152,512]{3,2,0,1:T(8,128)(2,1)S(1)} fusion(bf16[4,2,152,2048]{3,2,0,1:T(8,128)(2,1)} %get-tuple-element.182, bf16[1,2,2048,512]{3,2,1,0:T(8,128)(2,1)} %all-gather.10.cloned.1.call-done), kind=kOutput, calls=%fused_computation.84 | convolution fusion | flops 2550759424 | bytes 10420224 | tf_op jit(solution)/shard_map/sjcf,jfd->sjcd/dot_general | solution.py:293
  252.0 7.4 %all-to-all-done.7 = bf16[4,2,152,512]{3,2,1,0:T(8,128)(2,1)} async-done(((bf16[4,2,152,512]{3,2,1,0:T(8,128)(2,1)}), bf16[4,2,152,512]{3,2,1,0:T(8,128)(2,1)}, u32[]{:S(2)}, u32[]{:S(2)}) %all-to-all-start.7) | async-done | bytes 1245216 | tf_op jit(solution)/shard_map/all_to_all | solution.py:145
  259.4 4.3 all-to-all-start.5
  263.7 8.3 %bitcast_convert_fusion.3 = bf16[2,512,2048]{2,1,0:T(8,128)(2,1)} fusion(bf16[4,2,152,512]{3,2,1,0:T(8,128)(2,1)} %all-to-all-done.4, bf16[4,2,152,2048]{3,2,0,1:T(8,128)(2,1)} %copy-done.86), kind=kOutput, calls=%fused_computation.31 | convolution fusion | flops 2552233984 | bytes 10420224 | tf_op jit(solution)/shard_map/sjcd,sjcf->jdf/dot_general | solution.py:316
  272.0 7.0 %all-to-all-done.5 = bf16[4,2,152,512]{3,2,1,0:T(8,128)(2,1)} async-done(((bf16[4,2,152,512]{3,2,1,0:T(8,128)(2,1)}), bf16[4,2,152,512]{3,2,1,0:T(8,128)(2,1)}, u32[]{:S(2)}, u32[]{:S(2)}) %all-to-all-start.5) | async-done | bytes 1245216 | tf_op jit(solution)/shard_map/all_to_all | solution.py:145
  289.4 9.3 %attention_back.2 = bf16[416,1536]{1,0:T(8,128)(2,1)} custom-call(bf16[416,1536]{1,0:T(8,128)(2,1)} %convolution_convert_fusion.5.packed_ref, bf16[416,512]{1,0:T(8,128)(2,1)} %convolution_convert_fusion.10.grad_ref, f32[416,8]{1,0:T(8,128)} %get-tuple-element.45.total_ref), custom_call_target="tpu_custom_call" | custom-call | tf_op jit(solution)/shard_map/attention_back/pallas_call | solution.py:236
  298.8 3.7 multiply_reduce_fusion.7
  306.5 4.4 all-to-all-start.8
  322.7 3.6 concatenate.32
  327.9 8.3 %bitcast_convert_fusion.1 = bf16[2,2048,512]{2,1,0:T(8,128)(2,1)} fusion(bf16[4,2,152,2048]{3,2,0,1:T(8,128)(2,1)} %copy-done.85, bf16[4,2,152,512]{3,2,1,0:T(8,128)(2,1)} %all-to-all-done.8), kind=kOutput, calls=%fused_computation.29 | convolution fusion | flops 2552233984 | bytes 10420224 | tf_op jit(solution)/shard_map/sjcf,sjcd->jfd/dot_general | solution.py:304
  339.8 9.5 %fusion.13 = bf16[4,2,152,2048]{3,2,0,1:T(8,128)(2,1)S(1)} fusion(f32[2,2048,4,152]{1,3,2,0:T(8,128)} %get-tuple-element.176, bf16[2,2,2048,512]{3,2,1,0:T(8,128)(2,1)} %all-gather.6.cloned.1.call-done, bf16[4,2,152,512]{3,2,1,0:T(8,128)(2,1)} %all-to-all-done.8), kind=kOutput, calls=%fused_computation.15 | convolution fusion | flops 2575040512 | bytes 20381696 | tf_op jit(solution)/shard_map/sjcd,jfd->sjcf/dot_general | solution.py:308
  349.3 6.8 %fusion.67 = bf16[4,2,152,512]{3,2,0,1:T(8,128)(2,1)S(1)} fusion(bf16[4,2,152,2048]{3,2,0,1:T(8,128)(2,1)S(1)} %fusion.13, bf16[2,2,2048,512]{3,2,1,0:T(8,128)(2,1)} %all-gather.6.cloned.1.call-done), kind=kOutput, calls=%fused_computation.86 | convolution fusion | flops 2550759424 | bytes 10420224 | tf_op jit(solution)/shard_map/sjcf,jfd->sjcd/dot_general | solution.py:312
  357.3 4.3 all-to-all-start.9
  362.7 8.4 %bitcast_convert_fusion.2 = bf16[2,512,2048]{2,1,0:T(8,128)(2,1)} fusion(bf16[4,2,152,512]{3,2,1,0:T(8,128)(2,1)} %all-to-all-done.2, bf16[4,2,152,2048]{3,2,0,1:T(8,128)(2,1)} %copy-done.87), kind=kOutput, calls=%fused_computation.30 | convolution fusion | flops 2552233984 | bytes 10420224 | tf_op jit(solution)/shard_map/sjcd,sjcf->jdf/dot_general | solution.py:316
  371.1 5.5 %all-to-all-done.9 = bf16[4,2,152,512]{3,2,1,0:T(8,128)(2,1)} async-done(((bf16[4,2,152,512]{3,2,1,0:T(8,128)(2,1)}), bf16[4,2,152,512]{3,2,1,0:T(8,128)(2,1)}, u32[]{:S(2)}, u32[]{:S(2)}) %all-to-all-start.9) | async-done | bytes 1245216 | tf_op jit(solution)/shard_map/all_to_all | solution.py:145
  383.3 9.1 %attention_back.3 = bf16[416,1536]{1,0:T(8,128)(2,1)} custom-call(bf16[416,1536]{1,0:T(8,128)(2,1)} %convolution_convert_fusion.6.packed_ref, bf16[416,512]{1,0:T(8,128)(2,1)} %convolution_convert_fusion.9.grad_ref, f32[416,8]{1,0:T(8,128)} %get-tuple-element.49.total_ref), custom_call_target="tpu_custom_call" | custom-call | tf_op jit(solution)/shard_map/attention_back/pallas_call | solution.py:236
  392.5 3.3 multiply_reduce_fusion.1
  399.4 4.4 concatenate.33
  406.6 4.2 all-to-all-start.11
  416.1 8.7 %all-to-all-done.11 = bf16[4,4,16,2060]{3,2,1,0:T(8,128)(2,1)} async-done(((bf16[4,4,16,2060]{3,2,1,0:T(8,128)(2,1)}), bf16[4,4,16,2060]{3,2,1,0:T(8,128)(2,1)}, u32[]{:S(2)}, u32[]{:S(2)}) %all-to-all-start.11) | async-done | bytes 1054752 | tf_op jit(solution)/shard_map/all_to_all | solution.py:145
  428.9 3.5 all-to-all-start.10
  438.2 8.1 %all-to-all-done.10 = bf16[4,4,16,2060]{3,2,1,0:T(8,128)(2,1)S(1)} async-done(((bf16[4,4,16,2060]{3,2,1,0:T(8,128)(2,1)}), bf16[4,4,16,2060]{3,2,1,0:T(8,128)(2,1)S(1)}, u32[]{:S(2)}, u32[]{:S(2)}) %all-to-all-start.10) | async-done | bytes 1054752 | tf_op jit(solution)/shard_map/all_to_all | solution.py:145
  448.6 8.4 %collective-permute-done.7 = bf16[2,16,2060]{2,1,0:T(8,128)(2,1)S(1)} collective-permute-done((bf16[2,16,2060]{2,1,0:T(8,128)(2,1)S(1)}, bf16[2,16,2060]{2,1,0:T(8,128)(2,1)S(1)}, u32[]{:S(2)}, u32[]{:S(2)}) %collective-permute-start.7) | collective-permute-done | bytes 131872 | tf_op jit(solution)/shard_map/ppermute | solution.py:371
  458.3 7.1 %collective-permute-done.8 = bf16[1,16,2060]{2,1,0:T(8,128)(2,1)S(1)} collective-permute-done((bf16[1,16,2060]{2,1,0:T(8,128)(2,1)S(1)}, bf16[1,16,2060]{2,1,0:T(8,128)(2,1)S(1)}, u32[]{:S(2)}, u32[]{:S(2)}) %collective-permute-start.8) | collective-permute-done | bytes 65952 | tf_op jit(solution)/shard_map/ppermute | solution.py:371
  465.5 30.2 %reduce-scatter.9.cloned.1.call-done = bf16[2,512,256]{2,1,0:T(8,128)(2,1)} async-done(((bf16[2,512,2048]{2,1,0:T(8,128)(2,1)}), bf16[2,512,256]{2,1,0:T(8,128)(2,1)}) %reduce-scatter.9.cloned.1.call-update) | async-done | bytes 524304 | tf_op jit(solution)/shard_map/reduce_scatter | solution.py:320
  498.4 9.6 %all_gather.15 = bf16[64,2,2060]{2,0,1:T(8,128)(2,1)S(1)} all-gather(bf16[16,2,2060]{2,0,1:T(8,128)(2,1)S(1)} %pad_maximum_fusion.5), channel_id=1, replica_groups=mesh['dp'=8,'expert'=4] {'expert'}, dimensions={0}, use_global_device_ids=true | all-gather | bytes 659200 | tf_op jit(solution)/shard_map/all_gather | solution.py:474
  (427 shorter events, 145.5 us)
Async XLA Ops:
  7.2 121.5 %all-gather.6.cloned.1.call-start = ((), (), s32[]{:S(2)}) async-start(), calls=%async_computation.16 | async-start | bytes 9437184 | tf_op jit(solution)/shard_map/all_gather | solution.py:118
  11.7 9.6 %copy-start.30 = (bf16[2,197,512]{2,0,1:T(2,128)(2,1)S(1)}, bf16[2,197,512]{2,0,1:T(2,128)(2,1)}, u32[]{:S(2)}) copy-start(bf16[2,197,512]{2,0,1:T(2,128)(2,1)} %param.10) | copy-start | bytes 1210372
  11.7 193.7 %all-gather.8.cloned.1.call-start = ((), (), s32[]{:S(2)}) async-start(), calls=%async_computation.21 | async-start | bytes 4718592 | tf_op jit(solution)/shard_map/all_gather | solution.py:120
  12.4 214.8 %all-gather.10.cloned.1.call-start = ((), (), s32[]{:S(2)}) async-start(), calls=%async_computation.22 | async-start | bytes 4718592 | tf_op jit(solution)/shard_map/all_gather | solution.py:121
  13.0 9.3 %collective-permute-start = (bf16[1,16,2060]{2,1,0:T(8,128)(2,1)S(1)}, bf16[1,16,2060]{2,1,0:T(8,128)(2,1)S(1)}, u32[]{:S(2)}, u32[]{:S(2)}) collective-permute-start(bf16[1,16,2060]{2,1,0:T(8,128)(2,1)S(1)} %dynamic-slice_bitcast_fusion.3), channel_id=1, source_target_pairs={{0,8},{4,12},{8,0},{12,4},{16,24},{20,28},{24,16},{28,20},{1,9},{5... | collective-permute-start | bytes 197768 | tf_op jit(solution)/shard_map/ppermute | solution.py:72
  18.0 25.9 %copy-start.31 = (bf16[2,197,512]{2,0,1:T(2,128)(2,1)S(1)}, bf16[2,197,512]{2,0,1:T(2,128)(2,1)}, u32[]{:S(2)}) copy-start(bf16[2,197,512]{2,0,1:T(2,128)(2,1)} %param.11) | copy-start | bytes 1210372
  22.5 20.5 %collective-permute-start.1 = (bf16[2,16,2060]{2,1,0:T(8,128)(2,1)S(1)}, bf16[2,16,2060]{2,1,0:T(8,128)(2,1)S(1)}, u32[]{:S(2)}, u32[]{:S(2)}) collective-permute-start(bf16[2,16,2060]{2,1,0:T(8,128)(2,1)S(1)} %pad_maximum_fusion.3), channel_id=1, source_target_pairs={{0,16},{4,20},{8,24},{12,28},{16,0},{20,4},{24,8},{28,12},{1,17},{... | collective-permute-start | bytes 395528 | tf_op jit(solution)/shard_map/ppermute | solution.py:72
  43.1 10.5 %collective-permute-start.2 = (bf16[1,16,2060]{2,1,0:T(8,128)(2,1)S(1)}, bf16[1,16,2060]{2,1,0:T(8,128)(2,1)S(1)}, u32[]{:S(2)}, u32[]{:S(2)}) collective-permute-start(bf16[1,16,2060]{2,1,0:T(8,128)(2,1)S(1)} %dynamic-slice_bitcast_fusion.4), channel_id=1, source_target_pairs={{0,8},{4,12},{8,0},{12,4},{16,24},{20,28},{24,16},{28,20},{1,9},{5... | collective-permute-start | bytes 197768 | tf_op jit(solution)/shard_map/ppermute | solution.py:72
  45.8 26.7 %all-to-all-start.1 = ((bf16[4,4,16,2060]{3,2,1,0:T(8,128)(2,1)}), bf16[4,4,16,2060]{3,2,1,0:T(8,128)(2,1)S(1)}, u32[]{:S(2)}, u32[]{:S(2)}) async-start(bf16[4,4,16,2060]{3,2,1,0:T(8,128)(2,1)} %broadcast_in_dim.227), calls=%async_computation.1 | async-start | bytes 2228224 | tf_op jit(solution)/shard_map/all_to_all | solution.py:145
  53.7 18.1 %collective-permute-start.3 = (bf16[2,16,2060]{2,1,0:T(8,128)(2,1)S(1)}, bf16[2,16,2060]{2,1,0:T(8,128)(2,1)S(1)}, u32[]{:S(2)}, u32[]{:S(2)}) collective-permute-start(bf16[2,16,2060]{2,1,0:T(8,128)(2,1)S(1)} %pad_maximum_fusion.4), channel_id=1, source_target_pairs={{0,16},{4,20},{8,24},{12,28},{16,0},{20,4},{24,8},{28,12},{1,17},{... | collective-permute-start | bytes 395528 | tf_op jit(solution)/shard_map/ppermute | solution.py:72
  53.8 46.9 %copy-start.1 = (f32[2,208,512]{2,1,0:T(8,128)}, f32[2,208,512]{2,1,0:T(8,128)S(1)}, u32[]{:S(2)}) copy-start(f32[2,208,512]{2,1,0:T(8,128)S(1)} %pad_convert_fusion) | copy-start | bytes 2555908
  72.5 11.3 %collective-permute-start.4 = (bf16[4,4,16,2060]{3,2,1,0:T(8,128)(2,1)S(1)}, bf16[4,4,16,2060]{3,2,1,0:T(8,128)(2,1)S(1)}, u32[]{:S(2)}, u32[]{:S(2)}) collective-permute-start(bf16[4,4,16,2060]{3,2,1,0:T(8,128)(2,1)S(1)} %all-to-all-done.1), channel_id=1, source_target_pairs={{0,4},{4,0},{8,12},{12,8},{16,20},{20,16},{24,28},{28,24},{1,5},{5... | collective-permute-start | bytes 3164168 | tf_op jit(solution)/shard_map/ppermute | solution.py:88
  74.6 28.5 %all-to-all-start = ((bf16[4,4,16,2060]{3,2,1,0:T(8,128)(2,1)}), bf16[4,4,16,2060]{3,2,1,0:T(8,128)(2,1)}, u32[]{:S(2)}, u32[]{:S(2)}) async-start(bf16[4,4,16,2060]{3,2,1,0:T(8,128)(2,1)} %broadcast_in_dim.223), calls=%async_computation | async-start | bytes 2228224 | tf_op jit(solution)/shard_map/all_to_all | solution.py:145
  88.0 24.1 %copy-start.45 = (bf16[512,12]{0,1:T(8,128)(2,1)}, bf16[512,12]{0,1:T(8,128)(2,1)S(1)}, u32[]{:S(2)}) copy-start(bf16[512,12]{0,1:T(8,128)(2,1)S(1)} %broadcast_select_fusion.10) | copy-start | bytes 36868
  88.1 17.0 %copy-start.51 = (f32[1,512]{1,0:T(1,128)}, f32[1,512]{1,0:T(1,128)S(1)}, u32[]{:S(2)}) copy-start(f32[1,512]{1,0:T(1,128)S(1)} %get-tuple-element.161) | copy-start | bytes 6148
  103.9 8.6 %collective-permute-start.5 = (bf16[4,4,16,2060]{3,2,1,0:T(8,128)(2,1)}, bf16[4,4,16,2060]{3,2,1,0:T(8,128)(2,1)}, u32[]{:S(2)}, u32[]{:S(2)}) collective-permute-start(bf16[4,4,16,2060]{3,2,1,0:T(8,128)(2,1)} %all-to-all-done), channel_id=1, source_target_pairs={{0,4},{4,0},{8,12},{12,8},{16,20},{20,16},{24,28},{28,24},{1,5},{5... | collective-permute-start | bytes 3164168 | tf_op jit(solution)/shard_map/ppermute | solution.py:88
  107.3 21.4 %all-to-all-start.2 = ((bf16[4,2,152,512]{3,2,1,0:T(8,128)(2,1)}), bf16[4,2,152,512]{3,2,1,0:T(8,128)(2,1)}, u32[]{:S(2)}, u32[]{:S(2)}) async-start(bf16[4,2,152,512]{3,2,1,0:T(8,128)(2,1)} %bitcast.368), calls=%async_computation.2 | async-start | bytes 2490368 | tf_op jit(solution)/shard_map/all_to_all | solution.py:145
  140.7 20.1 %all-to-all-start.3 = ((bf16[4,2,152,512]{3,2,1,0:T(8,128)(2,1)}), bf16[4,2,152,512]{3,2,1,0:T(8,128)(2,1)}, u32[]{:S(2)}, u32[]{:S(2)}) async-start(bf16[4,2,152,512]{3,2,1,0:T(8,128)(2,1)} %copy.182), calls=%async_computation.3 | async-start | bytes 2490368 | tf_op jit(solution)/shard_map/all_to_all | solution.py:145
  152.7 149.7 %copy-start.67 = (f32[1,512]{1,0:T(1,128)}, f32[1,512]{1,0:T(1,128)S(1)}, u32[]{:S(2)}) copy-start(f32[1,512]{1,0:T(1,128)S(1)} %get-tuple-element.156) | copy-start | bytes 6148
  152.7 14.4 %copy-start.78 = (f32[1,512]{1,0:T(1,128)}, f32[1,512]{1,0:T(1,128)S(1)}, u32[]{:S(2)}) copy-start(f32[1,512]{1,0:T(1,128)S(1)} %get-tuple-element.158) | copy-start | bytes 6148
  166.8 135.6 %copy-start.56 = (f32[416]{0:T(512)}, f32[416]{0:T(512)S(1)}, u32[]{:S(2)}) copy-start(f32[416]{0:T(512)S(1)} %broadcast_multiply_fusion.9) | copy-start | bytes 4996
  167.1 135.4 %copy-start.64 = (f32[416]{0:T(512)}, f32[416]{0:T(512)S(1)}, u32[]{:S(2)}) copy-start(f32[416]{0:T(512)S(1)} %add_rsqrt_fusion.1) | copy-start | bytes 4996
  179.4 19.9 %all-to-all-start.4 = ((bf16[4,2,152,512]{3,2,1,0:T(8,128)(2,1)}), bf16[4,2,152,512]{3,2,1,0:T(8,128)(2,1)}, u32[]{:S(2)}, u32[]{:S(2)}) async-start(bf16[4,2,152,512]{3,2,1,0:T(8,128)(2,1)} %bitcast.369), calls=%async_computation.4 | async-start | bytes 2490368 | tf_op jit(solution)/shard_map/all_to_all | solution.py:145
  199.3 19.6 %all-to-all-start.6 = ((bf16[4,2,152,512]{3,2,1,0:T(8,128)(2,1)}), bf16[4,2,152,512]{3,2,1,0:T(8,128)(2,1)}, u32[]{:S(2)}, u32[]{:S(2)}) async-start(bf16[4,2,152,512]{3,2,1,0:T(8,128)(2,1)} %bitcast.367), calls=%async_computation.6 | async-start | bytes 2490368 | tf_op jit(solution)/shard_map/all_to_all | solution.py:145
  203.5 232.0 %reduce-scatter.7.cloned.1.call-start = ((), (), s32[]{:S(2)}) async-start(), calls=%async_computation.18 | async-start | bytes 4718592 | tf_op jit(solution)/shard_map/reduce_scatter | solution.py:307
  239.8 19.7 %all-to-all-start.7 = ((bf16[4,2,152,512]{3,2,1,0:T(8,128)(2,1)}), bf16[4,2,152,512]{3,2,1,0:T(8,128)(2,1)}, u32[]{:S(2)}, u32[]{:S(2)}) async-start(bf16[4,2,152,512]{3,2,1,0:T(8,128)(2,1)} %copy.195), calls=%async_computation.7 | async-start | bytes 2490368 | tf_op jit(solution)/shard_map/all_to_all | solution.py:145
  259.4 19.6 %all-to-all-start.5 = ((bf16[4,2,152,512]{3,2,1,0:T(8,128)(2,1)}), bf16[4,2,152,512]{3,2,1,0:T(8,128)(2,1)}, u32[]{:S(2)}, u32[]{:S(2)}) async-start(bf16[4,2,152,512]{3,2,1,0:T(8,128)(2,1)} %copy.191), calls=%async_computation.5 | async-start | bytes 2490368 | tf_op jit(solution)/shard_map/all_to_all | solution.py:145
  306.5 11.9 %copy-start.20 = (bf16[416,512]{1,0:T(8,128)(2,1)S(1)}, bf16[416,512]{1,0:T(8,128)(2,1)}, u32[]{:S(2)}) copy-start(bf16[416,512]{1,0:T(8,128)(2,1)} %get-tuple-element.40) | copy-start | bytes 1277956
  306.5 21.4 %all-to-all-start.8 = ((bf16[4,2,152,512]{3,2,1,0:T(8,128)(2,1)}), bf16[4,2,152,512]{3,2,1,0:T(8,128)(2,1)}, u32[]{:S(2)}, u32[]{:S(2)}) async-start(bf16[4,2,152,512]{3,2,1,0:T(8,128)(2,1)} %bitcast.366), calls=%async_computation.8 | async-start | bytes 2490368 | tf_op jit(solution)/shard_map/all_to_all | solution.py:145
  310.9 124.6 %reduce-scatter.5.cloned.1.call-start = ((), (), s32[]{:S(2)}) async-start(), calls=%async_computation.17 | async-start | bytes 4718592 | tf_op jit(solution)/shard_map/reduce_scatter | solution.py:307
  336.4 129.1 %reduce-scatter.11.cloned.1.call-start = ((), (), s32[]{:S(2)}) async-start(), calls=%async_computation.20 | async-start | bytes 4718592 | tf_op jit(solution)/shard_map/reduce_scatter | solution.py:320
  357.3 19.3 %all-to-all-start.9 = ((bf16[4,2,152,512]{3,2,1,0:T(8,128)(2,1)}), bf16[4,2,152,512]{3,2,1,0:T(8,128)(2,1)}, u32[]{:S(2)}, u32[]{:S(2)}) async-start(bf16[4,2,152,512]{3,2,1,0:T(8,128)(2,1)} %copy.205), calls=%async_computation.9 | async-start | bytes 2490368 | tf_op jit(solution)/shard_map/all_to_all | solution.py:145
  361.6 134.1 %reduce-scatter.9.cloned.1.call-start = ((), (), s32[]{:S(2)}) async-start(), calls=%async_computation.19 | async-start | bytes 4718592 | tf_op jit(solution)/shard_map/reduce_scatter | solution.py:320
  362.7 13.9 %copy-start.63 = (s32[416]{0:T(512)S(1)}, s32[416]{0:T(512)}, u32[]{:S(2)}) copy-start(s32[416]{0:T(512)} %multiply_add_fusion.5) | copy-start | bytes 4996
  362.7 13.9 %copy-start.75 = (s32[416]{0:T(512)S(1)}, s32[416]{0:T(512)}, u32[]{:S(2)}) copy-start(s32[416]{0:T(512)} %multiply_add_fusion.6) | copy-start | bytes 4996
  362.7 41.1 %collective-permute-start.9 = (bf16[4,4,16,2060]{3,2,1,0:T(8,128)(2,1)}, bf16[4,4,16,2060]{3,2,1,0:T(8,128)(2,1)}, u32[]{:S(2)}, u32[]{:S(2)}) collective-permute-start(bf16[4,4,16,2060]{3,2,1,0:T(8,128)(2,1)} %dynamic-slice_bitcast_fusion), channel_id=1, source_target_pairs={{0,4},{4,0},{8,12},{12,8},{16,20},{20,16},{24,28},{28,24},{1,5},{5... | collective-permute-start | bytes 3164168 | tf_op jit(solution)/shard_map/ppermute | solution.py:371
  382.0 10.4 %copy-start.2 = (f32[2,208,512]{2,1,0:T(8,128)S(1)}, f32[2,208,512]{2,1,0:T(8,128)}, u32[]{:S(2)}) copy-start(f32[2,208,512]{2,1,0:T(8,128)} %copy-done.1) | copy-start | bytes 2555908
  382.0 10.4 %copy-start.21 = (bf16[512,1536]{1,0:T(8,128)(2,1)S(1)}, bf16[512,1536]{1,0:T(8,128)(2,1)}, u32[]{:S(2)}) copy-start(bf16[512,1536]{1,0:T(8,128)(2,1)} %get-tuple-element.171) | copy-start | bytes 4718596
  382.1 10.4 %copy-start.58 = (f32[1,512]{1,0:T(1,128)S(1)}, f32[1,512]{1,0:T(1,128)}, u32[]{:S(2)}) copy-start(f32[1,512]{1,0:T(1,128)} %copy-done.57) | copy-start | bytes 6148
  382.1 10.4 %copy-start.65 = (f32[416]{0:T(512)S(1)}, f32[416]{0:T(512)}, u32[]{:S(2)}) copy-start(f32[416]{0:T(512)} %div.122) | copy-start | bytes 4996
  382.1 10.3 %copy-start.66 = (f32[416]{0:T(512)S(1)}, f32[416]{0:T(512)}, u32[]{:S(2)}) copy-start(f32[416]{0:T(512)} %rsqrt.40) | copy-start | bytes 4996
  406.6 18.2 %all-to-all-start.11 = ((bf16[4,4,16,2060]{3,2,1,0:T(8,128)(2,1)}), bf16[4,4,16,2060]{3,2,1,0:T(8,128)(2,1)}, u32[]{:S(2)}, u32[]{:S(2)}) async-start(bf16[4,4,16,2060]{3,2,1,0:T(8,128)(2,1)} %fusion.50), calls=%async_computation.13 | async-start | bytes 2228224 | tf_op jit(solution)/shard_map/all_to_all | solution.py:145
  413.8 12.6 %collective-permute-start.6 = (bf16[4,4,16,2060]{3,2,1,0:T(8,128)(2,1)}, bf16[4,4,16,2060]{3,2,1,0:T(8,128)(2,1)}, u32[]{:S(2)}, u32[]{:S(2)}) collective-permute-start(bf16[4,4,16,2060]{3,2,1,0:T(8,128)(2,1)} %bitcast.353), channel_id=1, source_target_pairs={{0,4},{4,0},{8,12},{12,8},{16,20},{20,16},{24,28},{28,24},{1,5},{5... | collective-permute-start | bytes 3164168 | tf_op jit(solution)/shard_map/ppermute | solution.py:371
  426.3 9.1 %collective-permute-start.10 = (bf16[2,16,2060]{2,1,0:T(8,128)(2,1)S(1)}, bf16[2,16,2060]{2,1,0:T(8,128)(2,1)S(1)}, u32[]{:S(2)}, u32[]{:S(2)}) collective-permute-start(bf16[2,16,2060]{2,1,0:T(8,128)(2,1)S(1)} %dynamic-slice_bitcast_fusion.1), channel_id=1, source_target_pairs={{0,8},{4,12},{8,0},{12,4},{16,24},{20,28},{24,16},{28,20},{1,9},{5... | collective-permute-start | bytes 395528 | tf_op jit(solution)/shard_map/ppermute | solution.py:371
  428.9 17.4 %all-to-all-start.10 = ((bf16[4,4,16,2060]{3,2,1,0:T(8,128)(2,1)}), bf16[4,4,16,2060]{3,2,1,0:T(8,128)(2,1)S(1)}, u32[]{:S(2)}, u32[]{:S(2)}) async-start(bf16[4,4,16,2060]{3,2,1,0:T(8,128)(2,1)} %fusion.51), calls=%async_computation.10 | async-start | bytes 2228224 | tf_op jit(solution)/shard_map/all_to_all | solution.py:145
  446.5 10.4 %collective-permute-start.7 = (bf16[2,16,2060]{2,1,0:T(8,128)(2,1)S(1)}, bf16[2,16,2060]{2,1,0:T(8,128)(2,1)S(1)}, u32[]{:S(2)}, u32[]{:S(2)}) collective-permute-start(bf16[2,16,2060]{2,1,0:T(8,128)(2,1)S(1)} %dynamic-slice_bitcast_fusion.2), channel_id=1, source_target_pairs={{0,8},{4,12},{8,0},{12,4},{16,24},{20,28},{24,16},{28,20},{1,9},{5... | collective-permute-start | bytes 395528 | tf_op jit(solution)/shard_map/ppermute | solution.py:371
  448.3 10.0 %collective-permute-start.11 = (bf16[1,16,2060]{2,1,0:T(8,128)(2,1)S(1)}, bf16[1,16,2060]{2,1,0:T(8,128)(2,1)S(1)}, u32[]{:S(2)}, u32[]{:S(2)}) collective-permute-start(bf16[1,16,2060]{2,1,0:T(8,128)(2,1)S(1)} %constant_dynamic-slice_fusion), channel_id=1, source_target_pairs={{0,16},{4,20},{8,24},{12,28},{16,0},{20,4},{24,8},{28,12},{1,17},{... | collective-permute-start | bytes 197768 | tf_op jit(solution)/shard_map/ppermute | solution.py:371
  457.0 8.4 %collective-permute-start.8 = (bf16[1,16,2060]{2,1,0:T(8,128)(2,1)S(1)}, bf16[1,16,2060]{2,1,0:T(8,128)(2,1)S(1)}, u32[]{:S(2)}, u32[]{:S(2)}) collective-permute-start(bf16[1,16,2060]{2,1,0:T(8,128)(2,1)S(1)} %constant_dynamic-slice_fusion.1), channel_id=1, source_target_pairs={{0,16},{4,20},{8,24},{12,28},{16,0},{20,4},{24,8},{28,12},{1,17},{... | collective-permute-start | bytes 197768 | tf_op jit(solution)/shard_map/ppermute | solution.py:371
  (71 other events, 250.0 us)
Sparse Core Ops, SparseCore 0:
  11.8 95.1 all-gather.5
  108.5 47.8 all-gather.7
  158.0 45.0 all-gather.9
  227.4 48.1 reduce-scatter.6
  336.4 49.4 reduce-scatter.4
  388.1 51.3 reduce-scatter.10
  441.8 53.8 reduce-scatter.8
